TPU v7x, 128 devices: a whole 4x4x4 slice. The times are simulated.
128 devices in a mesh: seq: 16 (over y, x), tensor: 8 (over z, core).
Axes of the slice: x: 4, y: 4, z: 4, core: 2. Of those that a mesh axis runs over, the one named last changes fastest.
Arguments:
- tokens: bfloat16 [2048, 4096], P('seq'), may hold values from -8 to 8
- segment_ids: int32 [2048], replicated, may hold values from -1 to 14, as said below
- routes: int32 [2048, 2], P('seq'), may hold values from 0 to 7, all different within a row; in each aligned block of 128 rows (0 to 127, 128 to 255, ...) at most 64 rows name the same one
- owners: int32 [15], replicated, may hold values from 0 to 15
- gain_attn: float32 [4096], replicated, may hold values from 0.5 to 1.5
- w_query: bfloat16 [4096, 4096], P(None, 'tensor'), may hold values from -1 to 1
- w_kv: bfloat16 [4096, 2048], P(None, 'tensor'), may hold values from -1 to 1
- w_out: bfloat16 [4096, 4096], P('tensor'), may hold values from -0.09375 to 0.09375
- gain_moe: float32 [4096], replicated, may hold values from 0.5 to 1.5
- w_router: float32 [4096, 8], replicated, may hold values from -0.09375 to 0.09375
- w_gate: bfloat16 [4096, 65536], P(None, ('seq', 'tensor')), may hold values from -0.09375 to 0.09375
- w_up: bfloat16 [4096, 65536], P(None, ('seq', 'tensor')), may hold values from -0.09375 to 0.09375
- w_down: bfloat16 [65536, 4096], P(('seq', 'tensor')), may hold values from -0.0625 to 0.0625
Outputs:
- layer_out: bfloat16 [2048, 4096], P('seq', 'tensor')
- kv_cache: bfloat16 [32768, 2048], P('seq', 'tensor')
Inputs may be any that keep to these rules, and one draw needn't show every extreme that they name: `segment_ids`: tokens 0 to 1599 form segment 0; segments 1 to 14 follow in order, each of 8 to 31 tokens; all later tokens are -1. `routes`: in each aligned block of 128 rows no expert is named by more than 64 rows; the two experts of a row differ.
All inputs are finite; a program needn't handle non-finite values.
Results may differ from a plain program's by a relative error of at most 0.014.
Values may be sent and summed in bfloat16 or wider, within the bound.
No kernel may reach another device: no remote copies, remote signals or barrier semaphores. Data moves between devices by JAX's collectives and lax.ppermute only.
A program may use at most 128 MiB of HBM per device.

v0:
```python
import jax
import jax.numpy as jnp
from jax import lax
from jax.experimental import pallas as pl
from jax.experimental.pallas import tpu as pltpu
from jax.sharding import PartitionSpec as P


HEADS = 32
KV_HEADS = 8
HEAD_DIM = 128
EXPERTS = 8
EPS = 1e-05
THETA = 1000000.0
FLOOR = -1e30
NZ = 4
MIB = 1024 * 1024
F32 = jnp.float32
BF16 = jnp.bfloat16


VMEM_SPEC = pl.BlockSpec(memory_space=pltpu.VMEM)
ANY_SPEC = pl.BlockSpec(memory_space=pl.ANY)
SMEM_SPEC = pl.BlockSpec(memory_space=pltpu.SMEM)


def z_perm(step):
    return [(2 * z + c, 2 * ((z + step) % NZ) + c) for z in range(NZ) for c in range(2)]


def core_perm():
    return [(t, t ^ 1) for t in range(2 * NZ)]


def send_z(value, step):
    return lax.ppermute(value, "tensor", z_perm(step))


def send_core(value):
    return lax.ppermute(value, "tensor", core_perm())


def rotate(values, cosine, sine):
    half = values.shape[-1] // 2
    first = values[..., :half]
    second = values[..., half:]
    return jnp.concatenate(
        [first * cosine - second * sine, second * cosine + first * sine], axis=-1
    )


def attention_kernel(ids, first_ref, q_ref, start_ref, kv_ref, w_hbm, mine_ref, sib_ref, w_ref, sem):
    copy = pltpu.make_async_copy(w_hbm, w_ref, sem)
    copy.start()
    rows, dim = start_ref.shape[0], HEAD_DIM
    group = q_ref.shape[0] // rows
    count = kv_ref.shape[0]
    query = first_ref[0] + lax.broadcasted_iota(jnp.int32, (rows, count), 0)
    key = lax.broadcasted_iota(jnp.int32, (rows, count), 1)
    mask = (key <= query) & (key >= start_ref[...])
    scale = HEAD_DIM ** (-0.5)
    heads = []
    for g in range(group):
        q = q_ref[g * rows : (g + 1) * rows, :]
        s = lax.dot_general(
            q, kv_ref[:, :dim], (((1,), (1,)), ((), ())), preferred_element_type=F32
        )
        s = jnp.where(mask, s * scale, FLOOR)
        w = jnp.where(mask, jnp.exp(s - jnp.max(s, axis=1, keepdims=True)), 0.0)
        mass = jnp.sum(w, axis=1, keepdims=True)
        acc = jnp.dot(w.astype(BF16), kv_ref[:, dim:], preferred_element_type=F32)
        heads.append((acc / mass).astype(BF16))
    attended = jnp.concatenate(heads, axis=1)
    copy.wait()
    share = mine_ref.shape[2]

    def project(at):
        w = w_ref[:, pl.ds(pl.multiple_of(at * share, share), share)]
        return jnp.dot(attended, w, preferred_element_type=F32)

    def body(d, carry):
        sib_ref[d] = project(ids[4 + d]).astype(BF16)
        mine_ref[d] = project(ids[d])
        return carry

    lax.fori_loop(0, NZ, body, 0)


def attend(ids, first, q, start, kv, w_out, share):
    rows = start.shape[0]
    return pl.pallas_call(
        attention_kernel,
        out_shape=(
            jax.ShapeDtypeStruct((NZ, rows, share), F32),
            jax.ShapeDtypeStruct((NZ, rows, share), BF16),
        ),
        in_specs=[SMEM_SPEC, SMEM_SPEC, VMEM_SPEC, VMEM_SPEC, VMEM_SPEC, ANY_SPEC],
        out_specs=(VMEM_SPEC, VMEM_SPEC),
        scratch_shapes=[pltpu.VMEM(w_out.shape, BF16), pltpu.SemaphoreType.DMA],
        compiler_params=pltpu.CompilerParams(vmem_limit_bytes=24 * MIB),
    )(ids, first, q, start, kv, w_out)


def ffn_kernel(ids, gain_ref, wg_hbm, wu_hbm, wd_hbm, *refs):
    pieces = refs[:8]
    mine_ref, sib_ref = refs[-9:-7]
    xs_ref, act_ref, wg_ref, wu_ref, wd_ref, sems, _ = refs[-7:]
    copies = [
        pltpu.make_async_copy(hbm, ref, sems.at[i])
        for i, (hbm, ref) in enumerate(((wg_hbm, wg_ref), (wu_hbm, wu_ref), (wd_hbm, wd_ref)))
    ]
    for copy in copies:
        copy.start()
    rows, share = pieces[0].shape
    width = wg_ref.shape[0]
    tile = 32

    def norm(i, carry):
        at_row = pl.ds(pl.multiple_of(i * tile, tile), tile)
        total = jnp.zeros((tile, share), F32)
        for ref in pieces:
            v = ref[at_row, :].astype(F32)
            total = total + v * v
        mean = jnp.sum(total, axis=1, keepdims=True) * (1.0 / width)
        scale = lax.rsqrt(mean + EPS)
        for k, ref in enumerate(pieces):
            at = ids[k]
            v = ref[at_row, :].astype(F32) * scale * gain_ref[pl.ds(at, 1), :]
            xs_ref[at_row, pl.ds(pl.multiple_of(at * share, share), share)] = v.astype(BF16)
        return carry

    lax.fori_loop(0, rows // tile, norm, 0)
    copies[0].wait()
    copies[1].wait()
    block = 256

    def hidden(i, carry):
        at_row = pl.ds(pl.multiple_of(i * block, block), block)
        v = xs_ref[at_row, :]
        gate = jnp.dot(v, wg_ref[...], preferred_element_type=F32)
        up = jnp.dot(v, wu_ref[...], preferred_element_type=F32)
        act_ref[at_row, :] = (gate / (1.0 + jnp.exp(-gate)) * up).astype(BF16)
        return carry

    lax.fori_loop(0, rows // block, hidden, 0)
    copies[2].wait()

    def down(at):
        w = wd_ref[:, pl.ds(pl.multiple_of(at * share, share), share)]
        return jnp.dot(act_ref[...], w, preferred_element_type=F32).astype(BF16)

    def body(d, carry):
        sib_ref[d] = down(ids[12 + d])
        mine_ref[d] = down(ids[8 + d])
        return carry

    lax.fori_loop(0, NZ, body, 0)


def ffn(ids, gain, w_gate, w_up, w_down, pieces, after):
    rows, share = pieces[0].shape
    return pl.pallas_call(
        ffn_kernel,
        out_shape=(
            jax.ShapeDtypeStruct((NZ, rows, share), BF16),
            jax.ShapeDtypeStruct((NZ, rows, share), BF16),
        ),
        in_specs=[SMEM_SPEC, VMEM_SPEC]
        + [ANY_SPEC] * 3
        + [VMEM_SPEC] * len(pieces)
        + [ANY_SPEC] * len(after),
        out_specs=(VMEM_SPEC,) * 2,
        scratch_shapes=[
            pltpu.VMEM((rows, w_gate.shape[0]), BF16),
            pltpu.VMEM((rows, w_gate.shape[1]), BF16),
            pltpu.VMEM(w_gate.shape, BF16),
            pltpu.VMEM(w_up.shape, BF16),
            pltpu.VMEM(w_down.shape, BF16),
            pltpu.SemaphoreType.DMA((3,)),
            pltpu.VMEM((8, 128), F32),
        ],
        compiler_params=pltpu.CompilerParams(vmem_limit_bytes=36 * MIB),
    )(ids, gain, w_gate, w_up, w_down, *pieces, *after)


def gather_ring(own):
    ring = [own] + [send_z(own, d) for d in (1, 3, 2)]
    return ring + [send_core(v) for v in ring]


def add(*parts):
    total = parts[0].astype(F32)
    for part in parts[1:]:
        total = total + part.astype(F32)
    return total.astype(BF16)


def scatter_start(mine, sib):
    got = send_core(sib)
    return [add(mine[d], got[d]) for d in range(1, NZ)], (mine[0], got[0])


def scatter_end(sums, own):
    moved = [send_z(sums[d - 1], d) for d in (1, 3, 2)]
    return add(*own, *moved)


def local(
    tokens,
    segment_ids,
    routes,
    owners,
    gain_attn,
    w_query,
    w_kv,
    w_out,
    gain_moe,
    w_router,
    w_gate,
    w_up,
    w_down,
):
    seq_count = lax.axis_size("seq")
    ten_count = lax.axis_size("tensor")
    seq_rank = lax.axis_index("seq").astype(jnp.int32)
    ten_rank = lax.axis_index("tensor").astype(jnp.int32)
    rows, width = tokens.shape
    total = segment_ids.shape[0]
    share = width // ten_count
    group = HEADS // KV_HEADS
    z = ten_rank // 2
    c = ten_rank - z * 2
    first = seq_rank * rows

    short_count = owners.shape[0] - 1
    labels = jnp.where(segment_ids < 0, short_count + 1, segment_ids)
    my_labels = lax.dynamic_slice_in_dim(labels, first, rows)
    seg_start = jnp.sum((labels[None, :] < my_labels[:, None]).astype(jnp.int32), axis=1)
    position = first + jnp.arange(rows, dtype=jnp.int32) - seg_start

    values = tokens.astype(F32)
    scale = lax.rsqrt(jnp.mean(values * values, axis=-1, keepdims=True) + EPS)
    normed = (values * scale * gain_attn).astype(BF16)
    half_dim = HEAD_DIM // 2
    freqs = THETA ** (-(jnp.arange(half_dim, dtype=F32) * 2.0) / HEAD_DIM)
    angles = position.astype(F32)[:, None] * freqs[None, :]
    cosine = jnp.cos(angles)
    sine = jnp.sin(angles)
    pairs = jnp.dot(normed, w_kv, preferred_element_type=F32)
    keys = rotate(pairs[:, :HEAD_DIM], cosine, sine).astype(BF16)
    kv_own = jnp.concatenate([keys, pairs[:, HEAD_DIM:].astype(BF16)], axis=1)
    queries = jnp.dot(normed, w_query, preferred_element_type=F32)
    q = jnp.concatenate(
        [
            rotate(queries[:, g * HEAD_DIM : (g + 1) * HEAD_DIM], cosine, sine).astype(BF16)
            for g in range(group)
        ],
        axis=0,
    )

    kv_all = lax.all_to_all(
        jnp.broadcast_to(kv_own[None], (seq_count,) + kv_own.shape), "seq", 0, 0, tiled=True
    ).reshape(total, kv_own.shape[1])

    ring = lax.rem(z + jnp.arange(NZ, dtype=jnp.int32), NZ) * 2
    other_c = 1 - c
    out_ids = jnp.concatenate([ring + c, ring + other_c])
    out_mine, out_sib = attend(
        out_ids, first.reshape(1), q, seg_start[:, None], kv_all, w_out, share
    )
    out_sib_r = send_core(out_sib)
    sums = [out_mine[d] + out_sib_r[d].astype(F32) for d in range(NZ)]
    attn_sum = sums[0]
    for d in (1, 3, 2):
        attn_sum = attn_sum + send_z(sums[d].astype(BF16), d).astype(F32)
    own_tokens = lax.dynamic_slice_in_dim(tokens, ten_rank * share, share, 1)
    residual = (own_tokens.astype(F32) + attn_sum).astype(BF16)

    capacity = rows // 2
    slots = capacity // 2
    holders = seq_count // EXPERTS
    expert_ids = jnp.arange(EXPERTS, dtype=jnp.int32)
    hit = (routes[:, 0:1] == expert_ids[None, :]) | (routes[:, 1:2] == expert_ids[None, :])
    index = jnp.arange(rows, dtype=jnp.int32)
    before = (index[:, None] > index[None, :]).astype(BF16)
    rank = jnp.dot(before, hit.astype(BF16), preferred_element_type=F32).astype(jnp.int32)
    slot_of = jnp.where(hit, rank, -1)
    slot_dup = jnp.repeat(slot_of.T, holders, axis=0)

    def pack(low):
        want = low + jnp.arange(slots, dtype=jnp.int32)
        return slot_dup[:, None, :] == want[None, :, None]

    picks = [pack(0), pack(slots)]

    def dispatch(pick):
        flat = pick.reshape(seq_count * slots, rows).astype(BF16)
        out = jnp.dot(flat, residual, preferred_element_type=F32).astype(BF16)
        got = lax.all_to_all(out.reshape(seq_count, slots, share), "seq", 0, 0, tiled=True)
        return got.reshape(seq_count * slots, share)

    gain_share = lax.dynamic_slice_in_dim(gain_moe, ten_rank * share, share)
    router = lax.dynamic_slice_in_dim(w_router, ten_rank * share, share)
    res32 = residual.astype(F32)
    part = jnp.dot(
        res32 * gain_share, router, preferred_element_type=F32, precision=lax.Precision.HIGHEST
    )
    square = jnp.sum(res32 * res32, axis=1, keepdims=True)
    stats = jnp.concatenate([part, square, jnp.zeros((rows, 7), F32)], axis=1)
    stats = stats + send_core(stats)
    stats = stats + lax.ppermute(stats, "tensor", [(t, t ^ 2) for t in range(ten_count)])
    stats = stats + lax.ppermute(stats, "tensor", [(t, t ^ 4) for t in range(ten_count)])
    logits = stats[:, :EXPERTS] * lax.rsqrt(stats[:, EXPERTS : EXPERTS + 1] / width + EPS)
    picked = routes[:, :, None] == expert_ids[None, None, :]
    chosen = jnp.sum(jnp.where(picked, logits[:, None, :], 0.0), axis=2)
    gates = jax.nn.softmax(chosen, axis=1)
    gate_of = jnp.sum(jnp.where(picked, gates[:, :, None], 0.0), axis=1)
    gate_dup = jnp.repeat(gate_of, holders, axis=1)

    gain_rows = gain_moe.reshape(ten_count, share)
    order = jnp.array([0, 3, 1, 2], jnp.int32)
    source = lax.rem(z + order, NZ) * 2
    ids = jnp.concatenate([source + c, source + other_c, out_ids])
    a_own = dispatch(picks[0])
    a_pieces = gather_ring(a_own)
    b_own = dispatch(picks[1])
    b_pieces = gather_ring(b_own)
    a_out = ffn(ids, gain_rows, w_gate, w_up, w_down, a_pieces, [b_own])
    a_sums, a_rest = scatter_start(*a_out)
    b_out = ffn(ids, gain_rows, w_gate, w_up, w_down, b_pieces, a_sums)
    b_sums, b_rest = scatter_start(*b_out)

    def give_back(parts):
        got = lax.all_to_all(parts.reshape(seq_count, slots, share), "seq", 0, 0, tiled=True)
        return got.reshape(seq_count * slots, share)

    a_final = scatter_end(a_sums, a_rest)
    b_final = scatter_end(b_sums, b_rest)
    a_back = give_back(a_final)
    b_back = give_back(b_final)

    def combine(pick, back):
        weight = jnp.where(pick.transpose(2, 0, 1), gate_dup[:, :, None], 0.0)
        weight = weight.reshape(rows, seq_count * slots)
        high = weight.astype(BF16)
        low = (weight - high.astype(F32)).astype(BF16)
        return jnp.dot(high, back, preferred_element_type=F32) + jnp.dot(
            low, back, preferred_element_type=F32
        )

    mixture = combine(picks[0], a_back) + combine(picks[1], b_back)
    layer_out = (res32 + mixture).astype(BF16)

    owner_ext = jnp.concatenate([owners, jnp.full((1,), -1, jnp.int32)])
    label_ids = jnp.arange(short_count + 2, dtype=jnp.int32)
    owner_tok = jnp.sum(
        jnp.where(labels[:, None] == label_ids[None, :], owner_ext[None, :], 0), axis=1
    )
    held = (owner_tok == seq_rank).reshape(seq_count, rows)
    held_b = held.astype(BF16)
    inside = jnp.dot(held_b, before.T, preferred_element_type=F32)
    seq_index = jnp.arange(seq_count, dtype=jnp.int32)
    earlier = (seq_index[:, None] > seq_index[None, :]).astype(BF16)
    sizes = jnp.sum(held.astype(F32), axis=1).astype(BF16)
    ahead = jnp.dot(earlier, sizes[:, None], preferred_element_type=F32)
    slot = jnp.where(held, (inside + ahead).astype(jnp.int32), -1).reshape(1, total)
    places = jnp.arange(total, dtype=jnp.int32)
    take = (places[:, None] == slot).astype(BF16)
    cache = jnp.dot(take, kv_all, preferred_element_type=F32)
    return layer_out, cache.astype(BF16)


def solution(mesh):
    return jax.shard_map(
        local,
        mesh=mesh,
        in_specs=(
            P("seq", None),
            P(),
            P("seq", None),
            P(),
            P(),
            P(None, "tensor"),
            P(None, "tensor"),
            P("tensor", None),
            P(),
            P(),
            P(None, ("seq", "tensor")),
            P(None, ("seq", "tensor")),
            P(("seq", "tensor"), None),
        ),
        out_specs=(P("seq", "tensor"), P("seq", "tensor")),
        check_vma=False,
    )
```

profile of v0, /device:TPU:33, one launch (start us, length us, event | category | flops | bytes accessed | tf_op | source)
XLA Modules:
  0.0 232.2 jit_solution(8792703619877002393)
XLA Ops:
  1.8 1.5 fusion.3
  3.4 1.7 fusion.27
  6.6 6.8 %all-to-all-start = ((bf16[16,128,256]{2,1,0:T(8,128)(2,1)}), bf16[16,128,256]{2,1,0:T(8,128)(2,1)S(1)}, u32[]{:S(2)}, u32[]{:S(2)}) async-start(bf16[16,128,256]{2,1,0:T(8,128)(2,1)} %broadcast_in_dim.110), calls=%async_computation | async-start | bytes 2097152 | tf_op jit(solution)/shard_map/all_to_all | solution.py:261
  13.6 3.3 %fusion.29 = f32[128,512]{1,0:T(8,128)S(1)} fusion(bf16[4096,512]{1,0:T(8,128)(2,1)} %param.19, bf16[128,4096]{1,0:T(8,128)(2,1)} %param.14, f32[4096]{0:T(1024)S(1)} %copy-done.13, f32[128]{0:T(128)S(1)} %add_rsqrt_fusion), kind=kOutput, calls=%fused_computation.57 | convolution fusion | flops 538968064 | bytes 5521920 | tf_op jit(solution)/shard_map/dot_general | solution.py:252
  17.4 12.0 %all-to-all-done = bf16[16,128,256]{2,1,0:T(8,128)(2,1)S(1)} async-done(((bf16[16,128,256]{2,1,0:T(8,128)(2,1)}), bf16[16,128,256]{2,1,0:T(8,128)(2,1)S(1)}, u32[]{:S(2)}, u32[]{:S(2)}) %all-to-all-start) | async-done | bytes 1048608 | tf_op jit(solution)/shard_map/all_to_all | solution.py:261
  29.4 2.6 %copy-done.3 = bf16[512,4096]{1,0:T(8,128)(2,1)S(1)} copy-done((bf16[512,4096]{1,0:T(8,128)(2,1)S(1)}, bf16[512,4096]{1,0:T(8,128)(2,1)}, u32[]{:S(2)}) %copy-start.3) | copy-done | bytes 4194328
  32.0 5.6 %shard_map.149 = (f32[4,128,512]{2,1,0:T(8,128)S(1)}, bf16[4,128,512]{2,1,0:T(8,128)(2,1)}) custom-call(s32[8]{0:T(128)S(1)} %pad_add_fusion.ids, s32[1]{0:T(128)} %bitcast.first_ref, bf16[512,128]{1,0:T(8,128)(2,1)S(1)} %maximum_maximum_fusion.q_ref, s32[128,1]{1,0:T(8,128)S(1)} %copy.19.start_ref, bf16[2048,256]{1,0:T(8,128)(2,1)S(1)} %bitcast.114, ...), custom_call_target="tpu_custom_call" | custom-call | tf_op jit(solution)/shard_map/pallas_call | solution.py:91
  38.6 2.6 %collective-permute-start = (bf16[4,128,512]{2,1,0:T(8,128)(2,1)}, bf16[4,128,512]{2,1,0:T(8,128)(2,1)S(1)}, u32[]{:S(2)}, u32[]{:S(2)}) collective-permute-start(bf16[4,128,512]{2,1,0:T(8,128)(2,1)} %get-tuple-element.9), channel_id=1, source_target_pairs={{0,1},{1,0},{2,3},{3,2},{4,5},{5,4},{6,7},{7,6},{8,9},{9,8},{10,11... | collective-permute-start | bytes 1572872 | tf_op jit(solution)/shard_map/ppermute | solution.py:40
  41.4 1.6 collective-permute-done
  42.9 1.2 fusion.41
  44.2 1.7 collective-permute-start.1
  45.9 2.5 %collective-permute-start.3 = (bf16[128,512]{1,0:T(8,128)(2,1)S(1)}, bf16[128,512]{1,0:T(8,128)(2,1)S(1)}, u32[]{:S(2)}, u32[]{:S(2)}) collective-permute-start(bf16[128,512]{1,0:T(8,128)(2,1)S(1)} %get-tuple-element.27), channel_id=1, source_target_pairs={{0,4},{1,5},{2,6},{3,7},{4,0},{5,1},{6,2},{7,3},{8,12},{9,13},{10,... | collective-permute-start | bytes 393224 | tf_op jit(solution)/shard_map/ppermute | solution.py:36
  48.9 1.4 collective-permute-done.2
  50.3 3.9 %collective-permute-done.3 = bf16[128,512]{1,0:T(8,128)(2,1)S(1)} collective-permute-done((bf16[128,512]{1,0:T(8,128)(2,1)S(1)}, bf16[128,512]{1,0:T(8,128)(2,1)S(1)}, u32[]{:S(2)}, u32[]{:S(2)}) %collective-permute-start.3) | collective-permute-done | bytes 131104 | tf_op jit(solution)/shard_map/ppermute | solution.py:36
  55.6 12.8 %all_to_all.25 = bf16[16,32,512]{2,1,0:T(8,128)(2,1)S(1)} all-to-all(bf16[16,32,512]{2,1,0:T(8,128)(2,1)S(1)} %bitcast.122), channel_id=1, replica_groups=mesh['seq'=16,'tensor'=8] {'seq'}, dimensions={0} | all-to-all | bytes 1048576 | tf_op jit(solution)/shard_map/all_to_all | solution.py:299
  68.4 1.5 collective-permute-start.8
  69.9 1.5 collective-permute-start.9
  72.5 3.6 %all-to-all-start.2 = ((bf16[16,32,512]{2,1,0:T(8,128)(2,1)}), bf16[16,32,512]{2,1,0:T(8,128)(2,1)S(1)}, u32[]{:S(2)}, u32[]{:S(2)}) async-start(bf16[16,32,512]{2,1,0:T(8,128)(2,1)} %bitcast.121), calls=%async_computation.2 | async-start | bytes 1048576 | tf_op jit(solution)/shard_map/all_to_all | solution.py:299
  76.0 2.7 %collective-permute-start.10 = (bf16[512,512]{1,0:T(8,128)(2,1)S(1)}, bf16[512,512]{1,0:T(8,128)(2,1)}, u32[]{:S(2)}, u32[]{:S(2)}) collective-permute-start(bf16[512,512]{1,0:T(8,128)(2,1)S(1)} %bitcast.119), channel_id=1, source_target_pairs={{0,1},{1,0},{2,3},{3,2},{4,5},{5,4},{6,7},{7,6},{8,9},{9,8},{10,11... | collective-permute-start | bytes 1572872 | tf_op jit(solution)/shard_map/ppermute | solution.py:40
  79.7 6.0 %collective-permute-start.11 = (bf16[512,512]{1,0:T(8,128)(2,1)}, bf16[512,512]{1,0:T(8,128)(2,1)}, u32[]{:S(2)}, u32[]{:S(2)}) collective-permute-start(bf16[512,512]{1,0:T(8,128)(2,1)} %collective-permute-done.7.refs_1_), channel_id=1, source_target_pairs={{0,1},{1,0},{2,3},{3,2},{4,5},{5,4},{6,7},{7,6},{8,9},{9,8},{10,11... | collective-permute-start | bytes 1572872 | tf_op jit(solution)/shard_map/ppermute | solution.py:40
  85.6 7.0 %collective-permute-done.9.refs_3_ = bf16[512,512]{1,0:T(8,128)(2,1)} collective-permute-done((bf16[512,512]{1,0:T(8,128)(2,1)S(1)}, bf16[512,512]{1,0:T(8,128)(2,1)}, u32[]{:S(2)}, u32[]{:S(2)}) %collective-permute-start.9) | collective-permute-done | bytes 524320 | tf_op jit(solution)/shard_map/ppermute | solution.py:36
  92.7 2.9 %collective-permute-start.13 = (bf16[512,512]{1,0:T(8,128)(2,1)}, bf16[512,512]{1,0:T(8,128)(2,1)}, u32[]{:S(2)}, u32[]{:S(2)}) collective-permute-start(bf16[512,512]{1,0:T(8,128)(2,1)} %collective-permute-done.9.refs_3_), channel_id=1, source_target_pairs={{0,1},{1,0},{2,3},{3,2},{4,5},{5,4},{6,7},{7,6},{8,9},{9,8},{10,11... | collective-permute-start | bytes 1572872 | tf_op jit(solution)/shard_map/ppermute | solution.py:40
  95.7 1.7 collective-permute-done.13.refs_7_
  97.5 2.2 copy-done.1
  99.7 2.2 copy-done.2
  101.8 12.9 %shard_map.150 = (bf16[4,512,512]{2,1,0:T(8,128)(2,1)S(1)}, bf16[4,512,512]{2,1,0:T(8,128)(2,1)S(1)}) custom-call(s32[16]{0:T(128)S(1)} %pad_add_fusion.1.ids, f32[8,512]{1,0:T(8,128)S(1)} %reshape.197.gain_ref, bf16[4096,512]{1,0:T(8,128)(2,1)S(1)} %copy-done.1, bf16[4096,512]{1,0:T(8,128)(2,1)S(1)} %copy-done.2, bf16[512,4096]{1,0:T(8,128)(2,1)} %wd_hbm.3, ...), custom_call_target="tpu_custom_call" | custom-call | tf_op jit(solution)/shard_map/pallas_call | solution.py:162
  115.2 2.4 %collective-permute-start.19 = (bf16[512,512]{1,0:T(8,128)(2,1)S(1)}, bf16[512,512]{1,0:T(8,128)(2,1)S(1)}, u32[]{:S(2)}, u32[]{:S(2)}) collective-permute-start(bf16[512,512]{1,0:T(8,128)(2,1)S(1)} %bitcast.110), channel_id=1, source_target_pairs={{0,6},{1,7},{2,0},{3,1},{4,2},{5,3},{6,4},{7,5},{8,14},{9,15},{10,... | collective-permute-start | bytes 1572872 | tf_op jit(solution)/shard_map/ppermute | solution.py:36
  117.6 2.5 %collective-permute-start.20 = (bf16[512,512]{1,0:T(8,128)(2,1)S(1)}, bf16[512,512]{1,0:T(8,128)(2,1)S(1)}, u32[]{:S(2)}, u32[]{:S(2)}) collective-permute-start(bf16[512,512]{1,0:T(8,128)(2,1)S(1)} %bitcast.111), channel_id=1, source_target_pairs={{0,4},{1,5},{2,6},{3,7},{4,0},{5,1},{6,2},{7,3},{8,12},{9,13},{10,... | collective-permute-start | bytes 1572872 | tf_op jit(solution)/shard_map/ppermute | solution.py:36
  121.1 8.7 %collective-permute-done.18.refs_1_ = bf16[512,512]{1,0:T(8,128)(2,1)S(1)} collective-permute-done((bf16[512,512]{1,0:T(8,128)(2,1)S(1)}, bf16[512,512]{1,0:T(8,128)(2,1)S(1)}, u32[]{:S(2)}, u32[]{:S(2)}) %collective-permute-start.18) | collective-permute-done | bytes 524320 | tf_op jit(solution)/shard_map/ppermute | solution.py:36
  131.8 11.1 %collective-permute-done.20.refs_3_ = bf16[512,512]{1,0:T(8,128)(2,1)S(1)} collective-permute-done((bf16[512,512]{1,0:T(8,128)(2,1)S(1)}, bf16[512,512]{1,0:T(8,128)(2,1)S(1)}, u32[]{:S(2)}, u32[]{:S(2)}) %collective-permute-start.20) | collective-permute-done | bytes 524320 | tf_op jit(solution)/shard_map/ppermute | solution.py:36
  143.0 1.3 collective-permute-start.24
  145.8 11.5 %shard_map.151 = (bf16[4,512,512]{2,1,0:T(8,128)(2,1)S(1)}, bf16[4,512,512]{2,1,0:T(8,128)(2,1)S(1)}) custom-call(s32[16]{0:T(128)S(1)} %pad_add_fusion.1.ids, f32[8,512]{1,0:T(8,128)S(1)} %reshape.197.gain_ref, bf16[4096,512]{1,0:T(8,128)(2,1)S(1)} %copy-done.1, bf16[4096,512]{1,0:T(8,128)(2,1)S(1)} %copy-done.2, bf16[512,4096]{1,0:T(8,128)(2,1)} %wd_hbm.3, ...), custom_call_target="tpu_custom_call" | custom-call | tf_op jit(solution)/shard_map/pallas_call | solution.py:162
  159.6 1.9 collective-permute-done.4
  162.4 1.8 collective-permute-done.5
  164.2 2.7 %collective-permute-start.6 = (f32[128,16]{0,1:T(8,128)S(1)}, f32[128,16]{0,1:T(8,128)S(1)}, u32[]{:S(2)}, u32[]{:S(2)}) collective-permute-start(f32[128,16]{0,1:T(8,128)S(1)} %add.226), channel_id=1, source_target_pairs={{0,4},{1,5},{2,6},{3,7},{4,0},{5,1},{6,2},{7,3},{8,12},{9,13},{10,... | collective-permute-start | bytes 24584 | tf_op jit(solution)/shard_map/ppermute | solution.py:312
  166.9 1.5 collective-permute-start.16
  169.3 4.2 %fusion.2 = bf16[2048,256]{1,0:T(8,128)(2,1)} fusion(bf16[2048,256]{1,0:T(8,128)(2,1)S(1)} %bitcast.115, s32[2048]{0:T(1024)S(1)} %fusion.13), kind=kOutput, calls=%fused_computation.5 | convolution fusion | flops 2152202240 | bytes 2105344 | tf_op jit(solution)/shard_map/dot_general | solution.py:369
  173.5 1.7 fusion.24
  175.1 2.1 collective-permute-start.26
  177.2 1.5 collective-permute-done.15
  179.6 11.5 %collective-permute-done.17 = bf16[512,512]{1,0:T(8,128)(2,1)S(1)} collective-permute-done((bf16[512,512]{1,0:T(8,128)(2,1)S(1)}, bf16[512,512]{1,0:T(8,128)(2,1)S(1)}, u32[]{:S(2)}, u32[]{:S(2)}) %collective-permute-start.17) | collective-permute-done | bytes 524320 | tf_op jit(solution)/shard_map/ppermute | solution.py:36
  192.2 3.6 %all-to-all-start.3 = ((bf16[16,32,512]{2,1,0:T(8,128)(2,1)}), bf16[16,32,512]{2,1,0:T(8,128)(2,1)S(1)}, u32[]{:S(2)}, u32[]{:S(2)}) async-start(bf16[16,32,512]{2,1,0:T(8,128)(2,1)} %bitcast.23), calls=%async_computation.3 | async-start | bytes 1048576 | tf_op jit(solution)/shard_map/all_to_all | solution.py:334
  195.8 5.5 %collective-permute-done.26 = bf16[512,512]{1,0:T(8,128)(2,1)} collective-permute-done((bf16[512,512]{1,0:T(8,128)(2,1)}, bf16[512,512]{1,0:T(8,128)(2,1)}, u32[]{:S(2)}, u32[]{:S(2)}) %collective-permute-start.26) | collective-permute-done | bytes 524320 | tf_op jit(solution)/shard_map/ppermute | solution.py:36
  201.3 1.3 collective-permute-done.27
  202.6 11.0 %collective-permute-done.28 = bf16[512,512]{1,0:T(8,128)(2,1)} collective-permute-done((bf16[512,512]{1,0:T(8,128)(2,1)S(1)}, bf16[512,512]{1,0:T(8,128)(2,1)}, u32[]{:S(2)}, u32[]{:S(2)}) %collective-permute-start.28) | collective-permute-done | bytes 524320 | tf_op jit(solution)/shard_map/ppermute | solution.py:36
  213.6 2.8 %fusion.17 = bf16[512,512]{1,0:T(8,128)(2,1)} fusion(bf16[512,512]{1,0:T(8,128)(2,1)} %collective-permute-done.28, bf16[512,512]{1,0:T(8,128)(2,1)} %collective-permute-done.27, bf16[512,512]{1,0:T(8,128)(2,1)} %collective-permute-done.26, bf16[4,512,512]{2,1,0:T(8,128)(2,1)} %copy-done.8, bf16[4,512,512]{2,1,0:T(8,128)(2,1)} %copy-done.6), kind=kLoop, calls=%fused_computation.30 | loop fusion | flops 2621440 | bytes 3145728 | tf_op jit(solution)/shard_map/convert_element_type | solution.py:195
  216.4 3.6 %all-to-all-start.4 = ((bf16[16,32,512]{2,1,0:T(8,128)(2,1)}), bf16[16,32,512]{2,1,0:T(8,128)(2,1)S(1)}, u32[]{:S(2)}, u32[]{:S(2)}) async-start(bf16[16,32,512]{2,1,0:T(8,128)(2,1)} %bitcast.123), calls=%async_computation.4 | async-start | bytes 1048576 | tf_op jit(solution)/shard_map/all_to_all | solution.py:334
  220.3 9.0 %all-to-all-done.4 = bf16[16,32,512]{2,1,0:T(8,128)(2,1)S(1)} async-done(((bf16[16,32,512]{2,1,0:T(8,128)(2,1)}), bf16[16,32,512]{2,1,0:T(8,128)(2,1)S(1)}, u32[]{:S(2)}, u32[]{:S(2)}) %all-to-all-start.4) | async-done | bytes 524320 | tf_op jit(solution)/shard_map/all_to_all | solution.py:334
  (117 shorter events, 23.0 us)
Async XLA Ops:
  0.6 2.8 %copy-start = (bf16[4096,256]{1,0:T(8,128)(2,1)S(1)}, bf16[4096,256]{1,0:T(8,128)(2,1)}, u32[]{:S(2)}) copy-start(bf16[4096,256]{1,0:T(8,128)(2,1)} %param.20) | copy-start | bytes 6291460
  5.1 8.5 %copy-start.13 = (f32[4096]{0:T(1024)S(1)}, f32[4096]{0:T(1024)}, u32[]{:S(2)}) copy-start(f32[4096]{0:T(1024)} %param.18) | copy-start | bytes 49156
  6.6 22.8 %all-to-all-start = ((bf16[16,128,256]{2,1,0:T(8,128)(2,1)}), bf16[16,128,256]{2,1,0:T(8,128)(2,1)S(1)}, u32[]{:S(2)}, u32[]{:S(2)}) async-start(bf16[16,128,256]{2,1,0:T(8,128)(2,1)} %broadcast_in_dim.110), calls=%async_computation | async-start | bytes 2097152 | tf_op jit(solution)/shard_map/all_to_all | solution.py:261
  29.4 8.2 %copy-start.4 = (bf16[16,128,256]{2,1,0:T(8,128)(2,1)}, bf16[16,128,256]{2,1,0:T(8,128)(2,1)S(1)}, u32[]{:S(2)}) copy-start(bf16[16,128,256]{2,1,0:T(8,128)(2,1)S(1)} %all-to-all-done) | copy-start | bytes 3145732
  29.4 2.6 %copy-start.3 = (bf16[512,4096]{1,0:T(8,128)(2,1)S(1)}, bf16[512,4096]{1,0:T(8,128)(2,1)}, u32[]{:S(2)}) copy-start(bf16[512,4096]{1,0:T(8,128)(2,1)} %w_hbm.1) | copy-start | bytes 12582916
  32.0 9.3 %copy-start.10 = (s32[128,2]{0,1:T(2,128)S(1)}, s32[128,2]{0,1:T(2,128)}, u32[]{:S(2)}) copy-start(s32[128,2]{0,1:T(2,128)} %param.16) | copy-start | bytes 3076
  37.6 1.0 copy-start.7
  38.6 4.3 %collective-permute-start = (bf16[4,128,512]{2,1,0:T(8,128)(2,1)}, bf16[4,128,512]{2,1,0:T(8,128)(2,1)S(1)}, u32[]{:S(2)}, u32[]{:S(2)}) collective-permute-start(bf16[4,128,512]{2,1,0:T(8,128)(2,1)} %get-tuple-element.9), channel_id=1, source_target_pairs={{0,1},{1,0},{2,3},{3,2},{4,5},{5,4},{6,7},{7,6},{8,9},{9,8},{10,11... | collective-permute-start | bytes 1572872 | tf_op jit(solution)/shard_map/ppermute | solution.py:40
  41.2 1.7 copy-start.11
  42.9 28.4 %copy-start.9 = (f32[4096]{0:T(1024)S(1)}, f32[4096]{0:T(1024)}, u32[]{:S(2)}) copy-start(f32[4096]{0:T(1024)} %param.22) | copy-start | bytes 49156
  44.2 4.8 %collective-permute-start.1 = (bf16[128,512]{1,0:T(8,128)(2,1)S(1)}, bf16[128,512]{1,0:T(8,128)(2,1)S(1)}, u32[]{:S(2)}, u32[]{:S(2)}) collective-permute-start(bf16[128,512]{1,0:T(8,128)(2,1)S(1)} %get-tuple-element.26), channel_id=1, source_target_pairs={{0,2},{1,3},{2,4},{3,5},{4,6},{5,7},{6,0},{7,1},{8,10},{9,11},{10,... | collective-permute-start | bytes 393224 | tf_op jit(solution)/shard_map/ppermute | solution.py:36
  45.9 4.4 %collective-permute-start.2 = (bf16[128,512]{1,0:T(8,128)(2,1)S(1)}, bf16[128,512]{1,0:T(8,128)(2,1)S(1)}, u32[]{:S(2)}, u32[]{:S(2)}) collective-permute-start(bf16[128,512]{1,0:T(8,128)(2,1)S(1)} %get-tuple-element.28), channel_id=1, source_target_pairs={{0,6},{1,7},{2,0},{3,1},{4,2},{5,3},{6,4},{7,5},{8,14},{9,15},{10,... | collective-permute-start | bytes 393224 | tf_op jit(solution)/shard_map/ppermute | solution.py:36
  45.9 8.3 %collective-permute-start.3 = (bf16[128,512]{1,0:T(8,128)(2,1)S(1)}, bf16[128,512]{1,0:T(8,128)(2,1)S(1)}, u32[]{:S(2)}, u32[]{:S(2)}) collective-permute-start(bf16[128,512]{1,0:T(8,128)(2,1)S(1)} %get-tuple-element.27), channel_id=1, source_target_pairs={{0,4},{1,5},{2,6},{3,7},{4,0},{5,1},{6,2},{7,3},{8,12},{9,13},{10,... | collective-permute-start | bytes 393224 | tf_op jit(solution)/shard_map/ppermute | solution.py:36
  48.9 46.7 %copy-start.12 = (s32[4]{0:T(128)S(1)}, s32[4]{0:T(128)}, u32[]{:S(2)}) copy-start(s32[4]{0:T(128)} %constant.70.clone) | copy-start | bytes 52
  68.4 11.3 %collective-permute-start.7 = (bf16[512,512]{1,0:T(8,128)(2,1)S(1)}, bf16[512,512]{1,0:T(8,128)(2,1)}, u32[]{:S(2)}, u32[]{:S(2)}) collective-permute-start(bf16[512,512]{1,0:T(8,128)(2,1)S(1)} %bitcast.116), channel_id=1, source_target_pairs={{0,2},{1,3},{2,4},{3,5},{4,6},{5,7},{6,0},{7,1},{8,10},{9,11},{10,... | collective-permute-start | bytes 1572872 | tf_op jit(solution)/shard_map/ppermute | solution.py:36
  68.4 17.2 %collective-permute-start.8 = (bf16[512,512]{1,0:T(8,128)(2,1)S(1)}, bf16[512,512]{1,0:T(8,128)(2,1)}, u32[]{:S(2)}, u32[]{:S(2)}) collective-permute-start(bf16[512,512]{1,0:T(8,128)(2,1)S(1)} %bitcast.117), channel_id=1, source_target_pairs={{0,6},{1,7},{2,0},{3,1},{4,2},{5,3},{6,4},{7,5},{8,14},{9,15},{10,... | collective-permute-start | bytes 1572872 | tf_op jit(solution)/shard_map/ppermute | solution.py:36
  69.9 22.8 %collective-permute-start.9 = (bf16[512,512]{1,0:T(8,128)(2,1)S(1)}, bf16[512,512]{1,0:T(8,128)(2,1)}, u32[]{:S(2)}, u32[]{:S(2)}) collective-permute-start(bf16[512,512]{1,0:T(8,128)(2,1)S(1)} %bitcast.118), channel_id=1, source_target_pairs={{0,4},{1,5},{2,6},{3,7},{4,0},{5,1},{6,2},{7,3},{8,12},{9,13},{10,... | collective-permute-start | bytes 1572872 | tf_op jit(solution)/shard_map/ppermute | solution.py:36
  72.5 23.2 %all-to-all-start.2 = ((bf16[16,32,512]{2,1,0:T(8,128)(2,1)}), bf16[16,32,512]{2,1,0:T(8,128)(2,1)S(1)}, u32[]{:S(2)}, u32[]{:S(2)}) async-start(bf16[16,32,512]{2,1,0:T(8,128)(2,1)} %bitcast.121), calls=%async_computation.2 | async-start | bytes 1048576 | tf_op jit(solution)/shard_map/all_to_all | solution.py:299
  76.0 19.7 %collective-permute-start.10 = (bf16[512,512]{1,0:T(8,128)(2,1)S(1)}, bf16[512,512]{1,0:T(8,128)(2,1)}, u32[]{:S(2)}, u32[]{:S(2)}) collective-permute-start(bf16[512,512]{1,0:T(8,128)(2,1)S(1)} %bitcast.119), channel_id=1, source_target_pairs={{0,1},{1,0},{2,3},{3,2},{4,5},{5,4},{6,7},{7,6},{8,9},{9,8},{10,11... | collective-permute-start | bytes 1572872 | tf_op jit(solution)/shard_map/ppermute | solution.py:40
  79.7 16.0 %collective-permute-start.11 = (bf16[512,512]{1,0:T(8,128)(2,1)}, bf16[512,512]{1,0:T(8,128)(2,1)}, u32[]{:S(2)}, u32[]{:S(2)}) collective-permute-start(bf16[512,512]{1,0:T(8,128)(2,1)} %collective-permute-done.7.refs_1_), channel_id=1, source_target_pairs={{0,1},{1,0},{2,3},{3,2},{4,5},{5,4},{6,7},{7,6},{8,9},{9,8},{10,11... | collective-permute-start | bytes 1572872 | tf_op jit(solution)/shard_map/ppermute | solution.py:40
  85.6 10.1 %collective-permute-start.12 = (bf16[512,512]{1,0:T(8,128)(2,1)}, bf16[512,512]{1,0:T(8,128)(2,1)}, u32[]{:S(2)}, u32[]{:S(2)}) collective-permute-start(bf16[512,512]{1,0:T(8,128)(2,1)} %collective-permute-done.8.refs_2_), channel_id=1, source_target_pairs={{0,1},{1,0},{2,3},{3,2},{4,5},{5,4},{6,7},{7,6},{8,9},{9,8},{10,11... | collective-permute-start | bytes 1572872 | tf_op jit(solution)/shard_map/ppermute | solution.py:40
  92.7 4.8 %collective-permute-start.13 = (bf16[512,512]{1,0:T(8,128)(2,1)}, bf16[512,512]{1,0:T(8,128)(2,1)}, u32[]{:S(2)}, u32[]{:S(2)}) collective-permute-start(bf16[512,512]{1,0:T(8,128)(2,1)} %collective-permute-done.9.refs_3_), channel_id=1, source_target_pairs={{0,1},{1,0},{2,3},{3,2},{4,5},{5,4},{6,7},{7,6},{8,9},{9,8},{10,11... | collective-permute-start | bytes 1572872 | tf_op jit(solution)/shard_map/ppermute | solution.py:40
  97.5 2.2 copy-start.1
  99.7 2.2 copy-start.2
  114.8 29.5 %collective-permute-start.14 = (bf16[4,512,512]{2,1,0:T(8,128)(2,1)S(1)}, bf16[4,512,512]{2,1,0:T(8,128)(2,1)S(1)}, u32[]{:S(2)}, u32[]{:S(2)}) collective-permute-start(bf16[4,512,512]{2,1,0:T(8,128)(2,1)S(1)} %get-tuple-element.11), channel_id=1, source_target_pairs={{0,1},{1,0},{2,3},{3,2},{4,5},{5,4},{6,7},{7,6},{8,9},{9,8},{10,11... | collective-permute-start | bytes 6291464 | tf_op jit(solution)/shard_map/ppermute | solution.py:40
  115.2 14.5 %collective-permute-start.18 = (bf16[512,512]{1,0:T(8,128)(2,1)S(1)}, bf16[512,512]{1,0:T(8,128)(2,1)S(1)}, u32[]{:S(2)}, u32[]{:S(2)}) collective-permute-start(bf16[512,512]{1,0:T(8,128)(2,1)S(1)} %bitcast.109), channel_id=1, source_target_pairs={{0,2},{1,3},{2,4},{3,5},{4,6},{5,7},{6,0},{7,1},{8,10},{9,11},{10,... | collective-permute-start | bytes 1572872 | tf_op jit(solution)/shard_map/ppermute | solution.py:36
  115.2 15.6 %collective-permute-start.19 = (bf16[512,512]{1,0:T(8,128)(2,1)S(1)}, bf16[512,512]{1,0:T(8,128)(2,1)S(1)}, u32[]{:S(2)}, u32[]{:S(2)}) collective-permute-start(bf16[512,512]{1,0:T(8,128)(2,1)S(1)} %bitcast.110), channel_id=1, source_target_pairs={{0,6},{1,7},{2,0},{3,1},{4,2},{5,3},{6,4},{7,5},{8,14},{9,15},{10,... | collective-permute-start | bytes 1572872 | tf_op jit(solution)/shard_map/ppermute | solution.py:36
  117.6 25.3 %collective-permute-start.20 = (bf16[512,512]{1,0:T(8,128)(2,1)S(1)}, bf16[512,512]{1,0:T(8,128)(2,1)S(1)}, u32[]{:S(2)}, u32[]{:S(2)}) collective-permute-start(bf16[512,512]{1,0:T(8,128)(2,1)S(1)} %bitcast.111), channel_id=1, source_target_pairs={{0,4},{1,5},{2,6},{3,7},{4,0},{5,1},{6,2},{7,3},{8,12},{9,13},{10,... | collective-permute-start | bytes 1572872 | tf_op jit(solution)/shard_map/ppermute | solution.py:36
  120.1 24.6 %collective-permute-start.21 = (bf16[512,512]{1,0:T(8,128)(2,1)S(1)}, bf16[512,512]{1,0:T(8,128)(2,1)S(1)}, u32[]{:S(2)}, u32[]{:S(2)}) collective-permute-start(bf16[512,512]{1,0:T(8,128)(2,1)S(1)} %bitcast.112), channel_id=1, source_target_pairs={{0,1},{1,0},{2,3},{3,2},{4,5},{5,4},{6,7},{7,6},{8,9},{9,8},{10,11... | collective-permute-start | bytes 1572872 | tf_op jit(solution)/shard_map/ppermute | solution.py:40
  129.8 14.9 %collective-permute-start.22 = (bf16[512,512]{1,0:T(8,128)(2,1)S(1)}, bf16[512,512]{1,0:T(8,128)(2,1)S(1)}, u32[]{:S(2)}, u32[]{:S(2)}) collective-permute-start(bf16[512,512]{1,0:T(8,128)(2,1)S(1)} %collective-permute-done.18.refs_1_), channel_id=1, source_target_pairs={{0,1},{1,0},{2,3},{3,2},{4,5},{5,4},{6,7},{7,6},{8,9},{9,8},{10,11... | collective-permute-start | bytes 1572872 | tf_op jit(solution)/shard_map/ppermute | solution.py:40
  130.8 13.9 %collective-permute-start.23 = (bf16[512,512]{1,0:T(8,128)(2,1)S(1)}, bf16[512,512]{1,0:T(8,128)(2,1)S(1)}, u32[]{:S(2)}, u32[]{:S(2)}) collective-permute-start(bf16[512,512]{1,0:T(8,128)(2,1)S(1)} %collective-permute-done.19.refs_2_), channel_id=1, source_target_pairs={{0,1},{1,0},{2,3},{3,2},{4,5},{5,4},{6,7},{7,6},{8,9},{9,8},{10,11... | collective-permute-start | bytes 1572872 | tf_op jit(solution)/shard_map/ppermute | solution.py:40
  143.0 2.8 %collective-permute-start.24 = (bf16[512,512]{1,0:T(8,128)(2,1)S(1)}, bf16[512,512]{1,0:T(8,128)(2,1)S(1)}, u32[]{:S(2)}, u32[]{:S(2)}) collective-permute-start(bf16[512,512]{1,0:T(8,128)(2,1)S(1)} %collective-permute-done.20.refs_3_), channel_id=1, source_target_pairs={{0,1},{1,0},{2,3},{3,2},{4,5},{5,4},{6,7},{7,6},{8,9},{9,8},{10,11... | collective-permute-start | bytes 1572872 | tf_op jit(solution)/shard_map/ppermute | solution.py:40
  145.8 12.1 %copy-start.14 = (s32[15]{0:T(128)S(1)}, s32[15]{0:T(128)}, u32[]{:S(2)}) copy-start(s32[15]{0:T(128)} %param.17) | copy-start | bytes 184
  145.8 23.5 %copy-start.5 = (bf16[16,128,256]{2,1,0:T(8,128)(2,1)S(1)}, bf16[16,128,256]{2,1,0:T(8,128)(2,1)}, u32[]{:S(2)}) copy-start(bf16[16,128,256]{2,1,0:T(8,128)(2,1)} %copy-done.4) | copy-start | bytes 3145732
  157.3 16.2 %copy-start.6 = (bf16[4,512,512]{2,1,0:T(8,128)(2,1)}, bf16[4,512,512]{2,1,0:T(8,128)(2,1)S(1)}, u32[]{:S(2)}) copy-start(bf16[4,512,512]{2,1,0:T(8,128)(2,1)S(1)} %get-tuple-element.12) | copy-start | bytes 6291460
  157.3 16.1 %collective-permute-start.25 = (bf16[4,512,512]{2,1,0:T(8,128)(2,1)S(1)}, bf16[4,512,512]{2,1,0:T(8,128)(2,1)S(1)}, u32[]{:S(2)}, u32[]{:S(2)}) collective-permute-start(bf16[4,512,512]{2,1,0:T(8,128)(2,1)S(1)} %get-tuple-element.13), channel_id=1, source_target_pairs={{0,1},{1,0},{2,3},{3,2},{4,5},{5,4},{6,7},{7,6},{8,9},{9,8},{10,11... | collective-permute-start | bytes 6291464 | tf_op jit(solution)/shard_map/ppermute | solution.py:40
  159.3 2.3 collective-permute-start.4
  161.6 2.5 %collective-permute-start.5 = (f32[128,16]{0,1:T(8,128)S(1)}, f32[128,16]{0,1:T(8,128)S(1)}, u32[]{:S(2)}, u32[]{:S(2)}) collective-permute-start(f32[128,16]{0,1:T(8,128)S(1)} %fusion.121), channel_id=1, source_target_pairs={{0,2},{1,3},{2,0},{3,1},{4,6},{5,7},{6,4},{7,5},{8,10},{9,11},{10,... | collective-permute-start | bytes 24584 | tf_op jit(solution)/shard_map/ppermute | solution.py:311
  164.2 9.3 %collective-permute-start.6 = (f32[128,16]{0,1:T(8,128)S(1)}, f32[128,16]{0,1:T(8,128)S(1)}, u32[]{:S(2)}, u32[]{:S(2)}) collective-permute-start(f32[128,16]{0,1:T(8,128)S(1)} %add.226), channel_id=1, source_target_pairs={{0,4},{1,5},{2,6},{3,7},{4,0},{5,1},{6,2},{7,3},{8,12},{9,13},{10,... | collective-permute-start | bytes 24584 | tf_op jit(solution)/shard_map/ppermute | solution.py:312
  166.9 11.8 %collective-permute-start.15 = (bf16[512,512]{1,0:T(8,128)(2,1)S(1)}, bf16[512,512]{1,0:T(8,128)(2,1)S(1)}, u32[]{:S(2)}, u32[]{:S(2)}) collective-permute-start(bf16[512,512]{1,0:T(8,128)(2,1)S(1)} %get-tuple-element.25.refs_8_), channel_id=1, source_target_pairs={{0,2},{1,3},{2,4},{3,5},{4,6},{5,7},{6,0},{7,1},{8,10},{9,11},{10,... | collective-permute-start | bytes 1572872 | tf_op jit(solution)/shard_map/ppermute | solution.py:36
  166.9 12.7 %collective-permute-start.16 = (bf16[512,512]{1,0:T(8,128)(2,1)S(1)}, bf16[512,512]{1,0:T(8,128)(2,1)S(1)}, u32[]{:S(2)}, u32[]{:S(2)}) collective-permute-start(bf16[512,512]{1,0:T(8,128)(2,1)S(1)} %get-tuple-element.23.refs_10_), channel_id=1, source_target_pairs={{0,6},{1,7},{2,0},{3,1},{4,2},{5,3},{6,4},{7,5},{8,14},{9,15},{10,... | collective-permute-start | bytes 1572872 | tf_op jit(solution)/shard_map/ppermute | solution.py:36
  168.3 22.7 %collective-permute-start.17 = (bf16[512,512]{1,0:T(8,128)(2,1)S(1)}, bf16[512,512]{1,0:T(8,128)(2,1)S(1)}, u32[]{:S(2)}, u32[]{:S(2)}) collective-permute-start(bf16[512,512]{1,0:T(8,128)(2,1)S(1)} %get-tuple-element.24.refs_9_), channel_id=1, source_target_pairs={{0,4},{1,5},{2,6},{3,7},{4,0},{5,1},{6,2},{7,3},{8,12},{9,13},{10,... | collective-permute-start | bytes 1572872 | tf_op jit(solution)/shard_map/ppermute | solution.py:36
  173.4 1.7 copy-start.8
  175.1 26.2 %collective-permute-start.26 = (bf16[512,512]{1,0:T(8,128)(2,1)}, bf16[512,512]{1,0:T(8,128)(2,1)}, u32[]{:S(2)}, u32[]{:S(2)}) collective-permute-start(bf16[512,512]{1,0:T(8,128)(2,1)} %get-tuple-element.20), channel_id=1, source_target_pairs={{0,2},{1,3},{2,4},{3,5},{4,6},{5,7},{6,0},{7,1},{8,10},{9,11},{10,... | collective-permute-start | bytes 1572872 | tf_op jit(solution)/shard_map/ppermute | solution.py:36
  177.2 25.4 %collective-permute-start.27 = (bf16[512,512]{1,0:T(8,128)(2,1)}, bf16[512,512]{1,0:T(8,128)(2,1)}, u32[]{:S(2)}, u32[]{:S(2)}) collective-permute-start(bf16[512,512]{1,0:T(8,128)(2,1)} %get-tuple-element.22), channel_id=1, source_target_pairs={{0,6},{1,7},{2,0},{3,1},{4,2},{5,3},{6,4},{7,5},{8,14},{9,15},{10,... | collective-permute-start | bytes 1572872 | tf_op jit(solution)/shard_map/ppermute | solution.py:36
  178.7 34.9 %collective-permute-start.28 = (bf16[512,512]{1,0:T(8,128)(2,1)S(1)}, bf16[512,512]{1,0:T(8,128)(2,1)}, u32[]{:S(2)}, u32[]{:S(2)}) collective-permute-start(bf16[512,512]{1,0:T(8,128)(2,1)S(1)} %get-tuple-element.21), channel_id=1, source_target_pairs={{0,4},{1,5},{2,6},{3,7},{4,0},{5,1},{6,2},{7,3},{8,12},{9,13},{10,... | collective-permute-start | bytes 1572872 | tf_op jit(solution)/shard_map/ppermute | solution.py:36
  192.2 24.2 %all-to-all-start.3 = ((bf16[16,32,512]{2,1,0:T(8,128)(2,1)}), bf16[16,32,512]{2,1,0:T(8,128)(2,1)S(1)}, u32[]{:S(2)}, u32[]{:S(2)}) async-start(bf16[16,32,512]{2,1,0:T(8,128)(2,1)} %bitcast.23), calls=%async_computation.3 | async-start | bytes 1048576 | tf_op jit(solution)/shard_map/all_to_all | solution.py:334
  216.4 12.9 %all-to-all-start.4 = ((bf16[16,32,512]{2,1,0:T(8,128)(2,1)}), bf16[16,32,512]{2,1,0:T(8,128)(2,1)S(1)}, u32[]{:S(2)}, u32[]{:S(2)}) async-start(bf16[16,32,512]{2,1,0:T(8,128)(2,1)} %bitcast.123), calls=%async_computation.4 | async-start | bytes 1048576 | tf_op jit(solution)/shard_map/all_to_all | solution.py:334
where the time goes:
time: 237 us; the launch traced here: 232 us
  waiting for transfers between devices  92.9 us (39%)
  starting transfers between devices  57.8 us (24%)
  Pallas kernels  30 us (13%)
  matrix products  15.1 us (6%)
  other arithmetic  13 us (5%)
  blocking collectives  12.8 us (5%)
  local copies, waits for them, and re-layouts  9.56 us (4%)
    ppermute x15, waiting for transfers between devices, send_z(): return lax.ppermute(value, 'tensor', z_perm(step))  63.8 us
    pallas_call x2, Pallas kernels, ffn(): pl.pallas_call(ffn_kernel, out_shape=(jax.ShapeDtypeStruct((NZ, rows, sha...  24.4 us
    ppermute x12, starting transfers between devices, send_core(): return lax.ppermute(value, 'tensor', core_perm())  19.5 us
    ppermute x15, starting transfers between devices, send_z(): return lax.ppermute(value, 'tensor', z_perm(step))  17.4 us
    all_to_all x1, blocking collectives, dispatch(): lax.all_to_all(out.reshape(seq_count, slots, share), 'seq', 0, 0, tiled=T...  12.8 us
    all_to_all x1, waiting for transfers between devices, local(): lax.all_to_all(jnp.broadcast_to(kv_own[None], (seq_count,) + kv_own.shape...  12 us
    all_to_all x2, waiting for transfers between devices, give_back(): lax.all_to_all(parts.reshape(seq_count, slots, share), 'seq', 0, 0, tiled...  8.96 us
    unnamed x30, local copies, waits for them, and re-layouts  7.96 us
  transfers between devices with their start and end apart: 33, of which 18 were waited for; matrix products, arithmetic and copies ran while one was open for 8% of the time, Pallas kernels for 0%

commit v1 on v0

--- a/solution.py
+++ b/solution.py
@@ -21,6 +21,7 @@
 
 VMEM_SPEC = pl.BlockSpec(memory_space=pltpu.VMEM)
 ANY_SPEC = pl.BlockSpec(memory_space=pl.ANY)
+HBM_SPEC = pl.BlockSpec(memory_space=pltpu.HBM)
 SMEM_SPEC = pl.BlockSpec(memory_space=pltpu.SMEM)
 
 
@@ -94,7 +95,7 @@
             jax.ShapeDtypeStruct((NZ, rows, share), F32),
             jax.ShapeDtypeStruct((NZ, rows, share), BF16),
         ),
-        in_specs=[SMEM_SPEC, SMEM_SPEC, VMEM_SPEC, VMEM_SPEC, VMEM_SPEC, ANY_SPEC],
+        in_specs=[SMEM_SPEC, SMEM_SPEC, VMEM_SPEC, VMEM_SPEC, VMEM_SPEC, HBM_SPEC],
         out_specs=(VMEM_SPEC, VMEM_SPEC),
         scratch_shapes=[pltpu.VMEM(w_out.shape, BF16), pltpu.SemaphoreType.DMA],
         compiler_params=pltpu.CompilerParams(vmem_limit_bytes=24 * MIB),
@@ -166,7 +167,7 @@
             jax.ShapeDtypeStruct((NZ, rows, share), BF16),
         ),
         in_specs=[SMEM_SPEC, VMEM_SPEC]
-        + [ANY_SPEC] * 3
+        + [HBM_SPEC] * 3
         + [VMEM_SPEC] * len(pieces)
         + [ANY_SPEC] * len(after),
         out_specs=(VMEM_SPEC,) * 2,
@@ -185,7 +186,8 @@
 
 def gather_ring(own):
     ring = [own] + [send_z(own, d) for d in (1, 3, 2)]
-    return ring + [send_core(v) for v in ring]
+    near = [send_core(own)]
+    return ring + near + [send_core(v) for v in ring[1:]]
 
 
 def add(*parts):
@@ -226,6 +228,9 @@
     ten_rank = lax.axis_index("tensor").astype(jnp.int32)
     rows, width = tokens.shape
     total = segment_ids.shape[0]
+    w_out, w_gate, w_up, w_down = (
+        pltpu.with_memory_space_constraint(w, pltpu.HBM) for w in (w_out, w_gate, w_up, w_down)
+    )
     share = width // ten_count
     group = HEADS // KV_HEADS
     z = ten_rank // 2

time: 237 us -> 232 us (0.979)
  local copies, waits for them, and re-layouts: 9.56 us -> 2.62 us
    unnamed x30 -> x24, local copies, waits for them, and re-layouts: 7.96 us -> 1.02 us
where the time goes in v1:
time: 232 us; the launch traced here: 227 us
  waiting for transfers between devices  92.9 us (40%)
  starting transfers between devices  57.8 us (25%)
  Pallas kernels  31.9 us (14%)
  matrix products  15.1 us (7%)
  other arithmetic  13 us (6%)
  blocking collectives  12.8 us (6%)
  local copies, waits for them, and re-layouts  2.62 us (1%)
    ppermute x15, waiting for transfers between devices, send_z(): return lax.ppermute(value, 'tensor', z_perm(step))  63.9 us
    pallas_call x2, Pallas kernels, ffn(): pl.pallas_call(ffn_kernel, out_shape=(jax.ShapeDtypeStruct((NZ, rows, sha...  24.6 us
    ppermute x12, starting transfers between devices, send_core(): return lax.ppermute(value, 'tensor', core_perm())  19.6 us
    ppermute x15, starting transfers between devices, send_z(): return lax.ppermute(value, 'tensor', z_perm(step))  17.4 us
    all_to_all x1, blocking collectives, dispatch(): lax.all_to_all(out.reshape(seq_count, slots, share), 'seq', 0, 0, tiled=T...  12.8 us
    all_to_all x1, waiting for transfers between devices, local(): lax.all_to_all(jnp.broadcast_to(kv_own[None], (seq_count,) + kv_own.shape...  12 us
    all_to_all x2, waiting for transfers between devices, give_back(): lax.all_to_all(parts.reshape(seq_count, slots, share), 'seq', 0, 0, tiled...  8.96 us
    pallas_call x1, Pallas kernels, attend(): pl.pallas_call(attention_kernel, out_shape=(jax.ShapeDtypeStruct((NZ, row...  7.33 us
  transfers between devices with their start and end apart: 33, of which 18 were waited for; matrix products, arithmetic and copies ran while one was open for 8% of the time, Pallas kernels for 0%

profile of v1, /device:TPU:33, one launch (start us, length us, event | category | flops | bytes accessed | tf_op | source)
XLA Modules:
  0.0 227.1 jit_solution(3739035860572546971)
XLA Ops:
  1.8 1.5 fusion.3
  3.4 1.7 fusion.27
  6.6 6.8 %all-to-all-start = ((bf16[16,128,256]{2,1,0:T(8,128)(2,1)}), bf16[16,128,256]{2,1,0:T(8,128)(2,1)S(1)}, u32[]{:S(2)}, u32[]{:S(2)}) async-start(bf16[16,128,256]{2,1,0:T(8,128)(2,1)} %broadcast_in_dim.110), calls=%async_computation | async-start | bytes 2097152 | tf_op jit(solution)/shard_map/all_to_all | solution.py:266
  13.6 3.3 %fusion.29 = f32[128,512]{1,0:T(8,128)S(1)} fusion(bf16[4096,512]{1,0:T(8,128)(2,1)} %param.19, bf16[128,4096]{1,0:T(8,128)(2,1)} %param.14, f32[4096]{0:T(1024)S(1)} %copy-done.10, f32[128]{0:T(128)S(1)} %add_rsqrt_fusion), kind=kOutput, calls=%fused_computation.57 | convolution fusion | flops 538968064 | bytes 5521920 | tf_op jit(solution)/shard_map/dot_general | solution.py:257
  17.4 12.0 %all-to-all-done = bf16[16,128,256]{2,1,0:T(8,128)(2,1)S(1)} async-done(((bf16[16,128,256]{2,1,0:T(8,128)(2,1)}), bf16[16,128,256]{2,1,0:T(8,128)(2,1)S(1)}, u32[]{:S(2)}, u32[]{:S(2)}) %all-to-all-start) | async-done | bytes 1048608 | tf_op jit(solution)/shard_map/all_to_all | solution.py:266
  29.4 7.3 %shard_map.149 = (f32[4,128,512]{2,1,0:T(8,128)S(1)}, bf16[4,128,512]{2,1,0:T(8,128)(2,1)}) custom-call(s32[8]{0:T(128)S(1)} %pad_add_fusion.ids, s32[1]{0:T(128)} %bitcast.first_ref, bf16[512,128]{1,0:T(8,128)(2,1)S(1)} %maximum_maximum_fusion.q_ref, s32[128,1]{1,0:T(8,128)S(1)} %copy.19.start_ref, bf16[2048,256]{1,0:T(8,128)(2,1)S(1)} %bitcast.114, ...), custom_call_target="tpu_custom_call" | custom-call | tf_op jit(solution)/shard_map/pallas_call | solution.py:92
  37.8 2.6 %collective-permute-start = (bf16[4,128,512]{2,1,0:T(8,128)(2,1)}, bf16[4,128,512]{2,1,0:T(8,128)(2,1)S(1)}, u32[]{:S(2)}, u32[]{:S(2)}) collective-permute-start(bf16[4,128,512]{2,1,0:T(8,128)(2,1)} %get-tuple-element.9), channel_id=1, source_target_pairs={{0,1},{1,0},{2,3},{3,2},{4,5},{5,4},{6,7},{7,6},{8,9},{9,8},{10,11... | collective-permute-start | bytes 1572872 | tf_op jit(solution)/shard_map/ppermute | solution.py:41
  40.5 1.6 collective-permute-done
  42.1 1.2 fusion.41
  43.4 1.7 collective-permute-start.1
  45.1 2.5 %collective-permute-start.3 = (bf16[128,512]{1,0:T(8,128)(2,1)S(1)}, bf16[128,512]{1,0:T(8,128)(2,1)S(1)}, u32[]{:S(2)}, u32[]{:S(2)}) collective-permute-start(bf16[128,512]{1,0:T(8,128)(2,1)S(1)} %get-tuple-element.27), channel_id=1, source_target_pairs={{0,4},{1,5},{2,6},{3,7},{4,0},{5,1},{6,2},{7,3},{8,12},{9,13},{10,... | collective-permute-start | bytes 393224 | tf_op jit(solution)/shard_map/ppermute | solution.py:37
  48.1 1.4 collective-permute-done.2
  49.5 3.9 %collective-permute-done.3 = bf16[128,512]{1,0:T(8,128)(2,1)S(1)} collective-permute-done((bf16[128,512]{1,0:T(8,128)(2,1)S(1)}, bf16[128,512]{1,0:T(8,128)(2,1)S(1)}, u32[]{:S(2)}, u32[]{:S(2)}) %collective-permute-start.3) | collective-permute-done | bytes 131104 | tf_op jit(solution)/shard_map/ppermute | solution.py:37
  53.3 1.2 fusion.34
  54.8 12.8 %all_to_all.25 = bf16[16,32,512]{2,1,0:T(8,128)(2,1)S(1)} all-to-all(bf16[16,32,512]{2,1,0:T(8,128)(2,1)S(1)} %bitcast.122), channel_id=1, replica_groups=mesh['seq'=16,'tensor'=8] {'seq'}, dimensions={0} | all-to-all | bytes 1048576 | tf_op jit(solution)/shard_map/all_to_all | solution.py:304
  67.6 1.5 collective-permute-start.8
  69.0 1.5 collective-permute-start.9
  70.6 1.1 convolution_convert_fusion
  71.6 3.6 %all-to-all-start.2 = ((bf16[16,32,512]{2,1,0:T(8,128)(2,1)}), bf16[16,32,512]{2,1,0:T(8,128)(2,1)S(1)}, u32[]{:S(2)}, u32[]{:S(2)}) async-start(bf16[16,32,512]{2,1,0:T(8,128)(2,1)} %bitcast.121), calls=%async_computation.2 | async-start | bytes 1048576 | tf_op jit(solution)/shard_map/all_to_all | solution.py:304
  75.2 2.7 %collective-permute-start.10 = (bf16[512,512]{1,0:T(8,128)(2,1)S(1)}, bf16[512,512]{1,0:T(8,128)(2,1)}, u32[]{:S(2)}, u32[]{:S(2)}) collective-permute-start(bf16[512,512]{1,0:T(8,128)(2,1)S(1)} %bitcast.119), channel_id=1, source_target_pairs={{0,1},{1,0},{2,3},{3,2},{4,5},{5,4},{6,7},{7,6},{8,9},{9,8},{10,11... | collective-permute-start | bytes 1572872 | tf_op jit(solution)/shard_map/ppermute | solution.py:41
  78.8 6.0 %collective-permute-start.11 = (bf16[512,512]{1,0:T(8,128)(2,1)}, bf16[512,512]{1,0:T(8,128)(2,1)}, u32[]{:S(2)}, u32[]{:S(2)}) collective-permute-start(bf16[512,512]{1,0:T(8,128)(2,1)} %collective-permute-done.7.refs_1_), channel_id=1, source_target_pairs={{0,1},{1,0},{2,3},{3,2},{4,5},{5,4},{6,7},{7,6},{8,9},{9,8},{10,11... | collective-permute-start | bytes 1572872 | tf_op jit(solution)/shard_map/ppermute | solution.py:41
  84.8 7.0 %collective-permute-done.9.refs_3_ = bf16[512,512]{1,0:T(8,128)(2,1)} collective-permute-done((bf16[512,512]{1,0:T(8,128)(2,1)S(1)}, bf16[512,512]{1,0:T(8,128)(2,1)}, u32[]{:S(2)}, u32[]{:S(2)}) %collective-permute-start.9) | collective-permute-done | bytes 524320 | tf_op jit(solution)/shard_map/ppermute | solution.py:37
  91.9 2.9 %collective-permute-start.13 = (bf16[512,512]{1,0:T(8,128)(2,1)}, bf16[512,512]{1,0:T(8,128)(2,1)}, u32[]{:S(2)}, u32[]{:S(2)}) collective-permute-start(bf16[512,512]{1,0:T(8,128)(2,1)} %collective-permute-done.9.refs_3_), channel_id=1, source_target_pairs={{0,1},{1,0},{2,3},{3,2},{4,5},{5,4},{6,7},{7,6},{8,9},{9,8},{10,11... | collective-permute-start | bytes 1572872 | tf_op jit(solution)/shard_map/ppermute | solution.py:41
  94.9 1.7 collective-permute-done.13.refs_7_
  96.6 13.0 %shard_map.150 = (bf16[4,512,512]{2,1,0:T(8,128)(2,1)S(1)}, bf16[4,512,512]{2,1,0:T(8,128)(2,1)S(1)}) custom-call(s32[16]{0:T(128)S(1)} %pad_add_fusion.1.ids, f32[8,512]{1,0:T(8,128)S(1)} %reshape.197.gain_ref, bf16[4096,512]{1,0:T(8,128)(2,1)} %wg_hbm.3, bf16[4096,512]{1,0:T(8,128)(2,1)} %wu_hbm.3, bf16[512,4096]{1,0:T(8,128)(2,1)} %wd_hbm.3, ...), custom_call_target="tpu_custom_call" | custom-call | tf_op jit(solution)/shard_map/pallas_call | solution.py:163
  110.1 2.4 %collective-permute-start.19 = (bf16[512,512]{1,0:T(8,128)(2,1)S(1)}, bf16[512,512]{1,0:T(8,128)(2,1)S(1)}, u32[]{:S(2)}, u32[]{:S(2)}) collective-permute-start(bf16[512,512]{1,0:T(8,128)(2,1)S(1)} %bitcast.110), channel_id=1, source_target_pairs={{0,6},{1,7},{2,0},{3,1},{4,2},{5,3},{6,4},{7,5},{8,14},{9,15},{10,... | collective-permute-start | bytes 1572872 | tf_op jit(solution)/shard_map/ppermute | solution.py:37
  112.5 2.5 %collective-permute-start.20 = (bf16[512,512]{1,0:T(8,128)(2,1)S(1)}, bf16[512,512]{1,0:T(8,128)(2,1)S(1)}, u32[]{:S(2)}, u32[]{:S(2)}) collective-permute-start(bf16[512,512]{1,0:T(8,128)(2,1)S(1)} %bitcast.111), channel_id=1, source_target_pairs={{0,4},{1,5},{2,6},{3,7},{4,0},{5,1},{6,2},{7,3},{8,12},{9,13},{10,... | collective-permute-start | bytes 1572872 | tf_op jit(solution)/shard_map/ppermute | solution.py:37
  116.0 8.7 %collective-permute-done.18.refs_1_ = bf16[512,512]{1,0:T(8,128)(2,1)S(1)} collective-permute-done((bf16[512,512]{1,0:T(8,128)(2,1)S(1)}, bf16[512,512]{1,0:T(8,128)(2,1)S(1)}, u32[]{:S(2)}, u32[]{:S(2)}) %collective-permute-start.18) | collective-permute-done | bytes 524320 | tf_op jit(solution)/shard_map/ppermute | solution.py:37
  126.7 11.1 %collective-permute-done.20.refs_3_ = bf16[512,512]{1,0:T(8,128)(2,1)S(1)} collective-permute-done((bf16[512,512]{1,0:T(8,128)(2,1)S(1)}, bf16[512,512]{1,0:T(8,128)(2,1)S(1)}, u32[]{:S(2)}, u32[]{:S(2)}) %collective-permute-start.20) | collective-permute-done | bytes 524320 | tf_op jit(solution)/shard_map/ppermute | solution.py:37
  137.8 1.3 collective-permute-start.24
  140.6 11.5 %shard_map.151 = (bf16[4,512,512]{2,1,0:T(8,128)(2,1)S(1)}, bf16[4,512,512]{2,1,0:T(8,128)(2,1)S(1)}) custom-call(s32[16]{0:T(128)S(1)} %pad_add_fusion.1.ids, f32[8,512]{1,0:T(8,128)S(1)} %reshape.197.gain_ref, bf16[4096,512]{1,0:T(8,128)(2,1)} %wg_hbm.3, bf16[4096,512]{1,0:T(8,128)(2,1)} %wu_hbm.3, bf16[512,4096]{1,0:T(8,128)(2,1)} %wd_hbm.3, ...), custom_call_target="tpu_custom_call" | custom-call | tf_op jit(solution)/shard_map/pallas_call | solution.py:163
  154.5 1.9 collective-permute-done.4
  157.3 1.8 collective-permute-done.5
  159.1 2.7 %collective-permute-start.6 = (f32[128,16]{0,1:T(8,128)S(1)}, f32[128,16]{0,1:T(8,128)S(1)}, u32[]{:S(2)}, u32[]{:S(2)}) collective-permute-start(f32[128,16]{0,1:T(8,128)S(1)} %add.226), channel_id=1, source_target_pairs={{0,4},{1,5},{2,6},{3,7},{4,0},{5,1},{6,2},{7,3},{8,12},{9,13},{10,... | collective-permute-start | bytes 24584 | tf_op jit(solution)/shard_map/ppermute | solution.py:317
  161.8 1.5 collective-permute-start.16
  164.2 4.2 %fusion.2 = bf16[2048,256]{1,0:T(8,128)(2,1)} fusion(bf16[2048,256]{1,0:T(8,128)(2,1)S(1)} %bitcast.115, s32[2048]{0:T(1024)S(1)} %fusion.13), kind=kOutput, calls=%fused_computation.5 | convolution fusion | flops 2152202240 | bytes 2105344 | tf_op jit(solution)/shard_map/dot_general | solution.py:374
  168.4 1.6 fusion.24
  170.0 2.1 collective-permute-start.26
  172.1 1.5 collective-permute-done.15
  174.5 11.5 %collective-permute-done.17 = bf16[512,512]{1,0:T(8,128)(2,1)S(1)} collective-permute-done((bf16[512,512]{1,0:T(8,128)(2,1)S(1)}, bf16[512,512]{1,0:T(8,128)(2,1)S(1)}, u32[]{:S(2)}, u32[]{:S(2)}) %collective-permute-start.17) | collective-permute-done | bytes 524320 | tf_op jit(solution)/shard_map/ppermute | solution.py:37
  186.0 1.2 fusion.20
  187.1 3.6 %all-to-all-start.3 = ((bf16[16,32,512]{2,1,0:T(8,128)(2,1)}), bf16[16,32,512]{2,1,0:T(8,128)(2,1)S(1)}, u32[]{:S(2)}, u32[]{:S(2)}) async-start(bf16[16,32,512]{2,1,0:T(8,128)(2,1)} %bitcast.23), calls=%async_computation.3 | async-start | bytes 1048576 | tf_op jit(solution)/shard_map/all_to_all | solution.py:339
  190.7 5.5 %collective-permute-done.26 = bf16[512,512]{1,0:T(8,128)(2,1)} collective-permute-done((bf16[512,512]{1,0:T(8,128)(2,1)}, bf16[512,512]{1,0:T(8,128)(2,1)}, u32[]{:S(2)}, u32[]{:S(2)}) %collective-permute-start.26) | collective-permute-done | bytes 524320 | tf_op jit(solution)/shard_map/ppermute | solution.py:37
  196.3 1.3 collective-permute-done.27
  197.5 11.0 %collective-permute-done.28 = bf16[512,512]{1,0:T(8,128)(2,1)} collective-permute-done((bf16[512,512]{1,0:T(8,128)(2,1)S(1)}, bf16[512,512]{1,0:T(8,128)(2,1)}, u32[]{:S(2)}, u32[]{:S(2)}) %collective-permute-start.28) | collective-permute-done | bytes 524320 | tf_op jit(solution)/shard_map/ppermute | solution.py:37
  208.5 2.8 %fusion.17 = bf16[512,512]{1,0:T(8,128)(2,1)} fusion(bf16[512,512]{1,0:T(8,128)(2,1)} %collective-permute-done.28, bf16[512,512]{1,0:T(8,128)(2,1)} %collective-permute-done.27, bf16[512,512]{1,0:T(8,128)(2,1)} %collective-permute-done.26, bf16[4,512,512]{2,1,0:T(8,128)(2,1)} %copy-done.5, bf16[4,512,512]{2,1,0:T(8,128)(2,1)} %copy-done.3), kind=kLoop, calls=%fused_computation.30 | loop fusion | flops 2621440 | bytes 3145728 | tf_op jit(solution)/shard_map/convert_element_type | solution.py:197
  211.4 3.6 %all-to-all-start.4 = ((bf16[16,32,512]{2,1,0:T(8,128)(2,1)}), bf16[16,32,512]{2,1,0:T(8,128)(2,1)S(1)}, u32[]{:S(2)}, u32[]{:S(2)}) async-start(bf16[16,32,512]{2,1,0:T(8,128)(2,1)} %bitcast.123), calls=%async_computation.4 | async-start | bytes 1048576 | tf_op jit(solution)/shard_map/all_to_all | solution.py:339
  215.2 9.0 %all-to-all-done.4 = bf16[16,32,512]{2,1,0:T(8,128)(2,1)S(1)} async-done(((bf16[16,32,512]{2,1,0:T(8,128)(2,1)}), bf16[16,32,512]{2,1,0:T(8,128)(2,1)S(1)}, u32[]{:S(2)}, u32[]{:S(2)}) %all-to-all-start.4) | async-done | bytes 524320 | tf_op jit(solution)/shard_map/all_to_all | solution.py:339
  (111 shorter events, 19.6 us)
Async XLA Ops:
  0.6 2.8 %copy-start = (bf16[4096,256]{1,0:T(8,128)(2,1)S(1)}, bf16[4096,256]{1,0:T(8,128)(2,1)}, u32[]{:S(2)}) copy-start(bf16[4096,256]{1,0:T(8,128)(2,1)} %param.20) | copy-start | bytes 6291460
  5.1 8.5 %copy-start.10 = (f32[4096]{0:T(1024)S(1)}, f32[4096]{0:T(1024)}, u32[]{:S(2)}) copy-start(f32[4096]{0:T(1024)} %param.18) | copy-start | bytes 49156
  6.6 22.8 %all-to-all-start = ((bf16[16,128,256]{2,1,0:T(8,128)(2,1)}), bf16[16,128,256]{2,1,0:T(8,128)(2,1)S(1)}, u32[]{:S(2)}, u32[]{:S(2)}) async-start(bf16[16,128,256]{2,1,0:T(8,128)(2,1)} %broadcast_in_dim.110), calls=%async_computation | async-start | bytes 2097152 | tf_op jit(solution)/shard_map/all_to_all | solution.py:266
  29.4 7.3 %copy-start.1 = (bf16[16,128,256]{2,1,0:T(8,128)(2,1)}, bf16[16,128,256]{2,1,0:T(8,128)(2,1)S(1)}, u32[]{:S(2)}) copy-start(bf16[16,128,256]{2,1,0:T(8,128)(2,1)S(1)} %all-to-all-done) | copy-start | bytes 3145732
  29.4 11.1 %copy-start.7 = (s32[128,2]{0,1:T(2,128)S(1)}, s32[128,2]{0,1:T(2,128)}, u32[]{:S(2)}) copy-start(s32[128,2]{0,1:T(2,128)} %param.16) | copy-start | bytes 3076
  36.8 1.0 copy-start.4
  37.8 4.3 %collective-permute-start = (bf16[4,128,512]{2,1,0:T(8,128)(2,1)}, bf16[4,128,512]{2,1,0:T(8,128)(2,1)S(1)}, u32[]{:S(2)}, u32[]{:S(2)}) collective-permute-start(bf16[4,128,512]{2,1,0:T(8,128)(2,1)} %get-tuple-element.9), channel_id=1, source_target_pairs={{0,1},{1,0},{2,3},{3,2},{4,5},{5,4},{6,7},{7,6},{8,9},{9,8},{10,11... | collective-permute-start | bytes 1572872 | tf_op jit(solution)/shard_map/ppermute | solution.py:41
  40.4 1.7 copy-start.8
  42.1 28.4 %copy-start.6 = (f32[4096]{0:T(1024)S(1)}, f32[4096]{0:T(1024)}, u32[]{:S(2)}) copy-start(f32[4096]{0:T(1024)} %param.22) | copy-start | bytes 49156
  43.4 4.8 %collective-permute-start.1 = (bf16[128,512]{1,0:T(8,128)(2,1)S(1)}, bf16[128,512]{1,0:T(8,128)(2,1)S(1)}, u32[]{:S(2)}, u32[]{:S(2)}) collective-permute-start(bf16[128,512]{1,0:T(8,128)(2,1)S(1)} %get-tuple-element.26), channel_id=1, source_target_pairs={{0,2},{1,3},{2,4},{3,5},{4,6},{5,7},{6,0},{7,1},{8,10},{9,11},{10,... | collective-permute-start | bytes 393224 | tf_op jit(solution)/shard_map/ppermute | solution.py:37
  45.1 4.4 %collective-permute-start.2 = (bf16[128,512]{1,0:T(8,128)(2,1)S(1)}, bf16[128,512]{1,0:T(8,128)(2,1)S(1)}, u32[]{:S(2)}, u32[]{:S(2)}) collective-permute-start(bf16[128,512]{1,0:T(8,128)(2,1)S(1)} %get-tuple-element.28), channel_id=1, source_target_pairs={{0,6},{1,7},{2,0},{3,1},{4,2},{5,3},{6,4},{7,5},{8,14},{9,15},{10,... | collective-permute-start | bytes 393224 | tf_op jit(solution)/shard_map/ppermute | solution.py:37
  45.1 8.3 %collective-permute-start.3 = (bf16[128,512]{1,0:T(8,128)(2,1)S(1)}, bf16[128,512]{1,0:T(8,128)(2,1)S(1)}, u32[]{:S(2)}, u32[]{:S(2)}) collective-permute-start(bf16[128,512]{1,0:T(8,128)(2,1)S(1)} %get-tuple-element.27), channel_id=1, source_target_pairs={{0,4},{1,5},{2,6},{3,7},{4,0},{5,1},{6,2},{7,3},{8,12},{9,13},{10,... | collective-permute-start | bytes 393224 | tf_op jit(solution)/shard_map/ppermute | solution.py:37
  48.1 46.7 %copy-start.9 = (s32[4]{0:T(128)S(1)}, s32[4]{0:T(128)}, u32[]{:S(2)}) copy-start(s32[4]{0:T(128)} %constant.70.clone) | copy-start | bytes 52
  67.6 11.3 %collective-permute-start.7 = (bf16[512,512]{1,0:T(8,128)(2,1)S(1)}, bf16[512,512]{1,0:T(8,128)(2,1)}, u32[]{:S(2)}, u32[]{:S(2)}) collective-permute-start(bf16[512,512]{1,0:T(8,128)(2,1)S(1)} %bitcast.116), channel_id=1, source_target_pairs={{0,2},{1,3},{2,4},{3,5},{4,6},{5,7},{6,0},{7,1},{8,10},{9,11},{10,... | collective-permute-start | bytes 1572872 | tf_op jit(solution)/shard_map/ppermute | solution.py:37
  67.6 17.2 %collective-permute-start.8 = (bf16[512,512]{1,0:T(8,128)(2,1)S(1)}, bf16[512,512]{1,0:T(8,128)(2,1)}, u32[]{:S(2)}, u32[]{:S(2)}) collective-permute-start(bf16[512,512]{1,0:T(8,128)(2,1)S(1)} %bitcast.117), channel_id=1, source_target_pairs={{0,6},{1,7},{2,0},{3,1},{4,2},{5,3},{6,4},{7,5},{8,14},{9,15},{10,... | collective-permute-start | bytes 1572872 | tf_op jit(solution)/shard_map/ppermute | solution.py:37
  69.0 22.8 %collective-permute-start.9 = (bf16[512,512]{1,0:T(8,128)(2,1)S(1)}, bf16[512,512]{1,0:T(8,128)(2,1)}, u32[]{:S(2)}, u32[]{:S(2)}) collective-permute-start(bf16[512,512]{1,0:T(8,128)(2,1)S(1)} %bitcast.118), channel_id=1, source_target_pairs={{0,4},{1,5},{2,6},{3,7},{4,0},{5,1},{6,2},{7,3},{8,12},{9,13},{10,... | collective-permute-start | bytes 1572872 | tf_op jit(solution)/shard_map/ppermute | solution.py:37
  71.6 23.2 %all-to-all-start.2 = ((bf16[16,32,512]{2,1,0:T(8,128)(2,1)}), bf16[16,32,512]{2,1,0:T(8,128)(2,1)S(1)}, u32[]{:S(2)}, u32[]{:S(2)}) async-start(bf16[16,32,512]{2,1,0:T(8,128)(2,1)} %bitcast.121), calls=%async_computation.2 | async-start | bytes 1048576 | tf_op jit(solution)/shard_map/all_to_all | solution.py:304
  75.2 19.7 %collective-permute-start.10 = (bf16[512,512]{1,0:T(8,128)(2,1)S(1)}, bf16[512,512]{1,0:T(8,128)(2,1)}, u32[]{:S(2)}, u32[]{:S(2)}) collective-permute-start(bf16[512,512]{1,0:T(8,128)(2,1)S(1)} %bitcast.119), channel_id=1, source_target_pairs={{0,1},{1,0},{2,3},{3,2},{4,5},{5,4},{6,7},{7,6},{8,9},{9,8},{10,11... | collective-permute-start | bytes 1572872 | tf_op jit(solution)/shard_map/ppermute | solution.py:41
  78.8 16.0 %collective-permute-start.11 = (bf16[512,512]{1,0:T(8,128)(2,1)}, bf16[512,512]{1,0:T(8,128)(2,1)}, u32[]{:S(2)}, u32[]{:S(2)}) collective-permute-start(bf16[512,512]{1,0:T(8,128)(2,1)} %collective-permute-done.7.refs_1_), channel_id=1, source_target_pairs={{0,1},{1,0},{2,3},{3,2},{4,5},{5,4},{6,7},{7,6},{8,9},{9,8},{10,11... | collective-permute-start | bytes 1572872 | tf_op jit(solution)/shard_map/ppermute | solution.py:41
  84.8 10.1 %collective-permute-start.12 = (bf16[512,512]{1,0:T(8,128)(2,1)}, bf16[512,512]{1,0:T(8,128)(2,1)}, u32[]{:S(2)}, u32[]{:S(2)}) collective-permute-start(bf16[512,512]{1,0:T(8,128)(2,1)} %collective-permute-done.8.refs_2_), channel_id=1, source_target_pairs={{0,1},{1,0},{2,3},{3,2},{4,5},{5,4},{6,7},{7,6},{8,9},{9,8},{10,11... | collective-permute-start | bytes 1572872 | tf_op jit(solution)/shard_map/ppermute | solution.py:41
  91.9 4.8 %collective-permute-start.13 = (bf16[512,512]{1,0:T(8,128)(2,1)}, bf16[512,512]{1,0:T(8,128)(2,1)}, u32[]{:S(2)}, u32[]{:S(2)}) collective-permute-start(bf16[512,512]{1,0:T(8,128)(2,1)} %collective-permute-done.9.refs_3_), channel_id=1, source_target_pairs={{0,1},{1,0},{2,3},{3,2},{4,5},{5,4},{6,7},{7,6},{8,9},{9,8},{10,11... | collective-permute-start | bytes 1572872 | tf_op jit(solution)/shard_map/ppermute | solution.py:41
  109.7 29.5 %collective-permute-start.14 = (bf16[4,512,512]{2,1,0:T(8,128)(2,1)S(1)}, bf16[4,512,512]{2,1,0:T(8,128)(2,1)S(1)}, u32[]{:S(2)}, u32[]{:S(2)}) collective-permute-start(bf16[4,512,512]{2,1,0:T(8,128)(2,1)S(1)} %get-tuple-element.11), channel_id=1, source_target_pairs={{0,1},{1,0},{2,3},{3,2},{4,5},{5,4},{6,7},{7,6},{8,9},{9,8},{10,11... | collective-permute-start | bytes 6291464 | tf_op jit(solution)/shard_map/ppermute | solution.py:41
  110.1 14.6 %collective-permute-start.18 = (bf16[512,512]{1,0:T(8,128)(2,1)S(1)}, bf16[512,512]{1,0:T(8,128)(2,1)S(1)}, u32[]{:S(2)}, u32[]{:S(2)}) collective-permute-start(bf16[512,512]{1,0:T(8,128)(2,1)S(1)} %bitcast.109), channel_id=1, source_target_pairs={{0,2},{1,3},{2,4},{3,5},{4,6},{5,7},{6,0},{7,1},{8,10},{9,11},{10,... | collective-permute-start | bytes 1572872 | tf_op jit(solution)/shard_map/ppermute | solution.py:37
  110.1 15.6 %collective-permute-start.19 = (bf16[512,512]{1,0:T(8,128)(2,1)S(1)}, bf16[512,512]{1,0:T(8,128)(2,1)S(1)}, u32[]{:S(2)}, u32[]{:S(2)}) collective-permute-start(bf16[512,512]{1,0:T(8,128)(2,1)S(1)} %bitcast.110), channel_id=1, source_target_pairs={{0,6},{1,7},{2,0},{3,1},{4,2},{5,3},{6,4},{7,5},{8,14},{9,15},{10,... | collective-permute-start | bytes 1572872 | tf_op jit(solution)/shard_map/ppermute | solution.py:37
  112.5 25.3 %collective-permute-start.20 = (bf16[512,512]{1,0:T(8,128)(2,1)S(1)}, bf16[512,512]{1,0:T(8,128)(2,1)S(1)}, u32[]{:S(2)}, u32[]{:S(2)}) collective-permute-start(bf16[512,512]{1,0:T(8,128)(2,1)S(1)} %bitcast.111), channel_id=1, source_target_pairs={{0,4},{1,5},{2,6},{3,7},{4,0},{5,1},{6,2},{7,3},{8,12},{9,13},{10,... | collective-permute-start | bytes 1572872 | tf_op jit(solution)/shard_map/ppermute | solution.py:37
  115.0 24.6 %collective-permute-start.21 = (bf16[512,512]{1,0:T(8,128)(2,1)S(1)}, bf16[512,512]{1,0:T(8,128)(2,1)S(1)}, u32[]{:S(2)}, u32[]{:S(2)}) collective-permute-start(bf16[512,512]{1,0:T(8,128)(2,1)S(1)} %bitcast.112), channel_id=1, source_target_pairs={{0,1},{1,0},{2,3},{3,2},{4,5},{5,4},{6,7},{7,6},{8,9},{9,8},{10,11... | collective-permute-start | bytes 1572872 | tf_op jit(solution)/shard_map/ppermute | solution.py:41
  124.7 14.9 %collective-permute-start.22 = (bf16[512,512]{1,0:T(8,128)(2,1)S(1)}, bf16[512,512]{1,0:T(8,128)(2,1)S(1)}, u32[]{:S(2)}, u32[]{:S(2)}) collective-permute-start(bf16[512,512]{1,0:T(8,128)(2,1)S(1)} %collective-permute-done.18.refs_1_), channel_id=1, source_target_pairs={{0,1},{1,0},{2,3},{3,2},{4,5},{5,4},{6,7},{7,6},{8,9},{9,8},{10,11... | collective-permute-start | bytes 1572872 | tf_op jit(solution)/shard_map/ppermute | solution.py:41
  125.7 13.9 %collective-permute-start.23 = (bf16[512,512]{1,0:T(8,128)(2,1)S(1)}, bf16[512,512]{1,0:T(8,128)(2,1)S(1)}, u32[]{:S(2)}, u32[]{:S(2)}) collective-permute-start(bf16[512,512]{1,0:T(8,128)(2,1)S(1)} %collective-permute-done.19.refs_2_), channel_id=1, source_target_pairs={{0,1},{1,0},{2,3},{3,2},{4,5},{5,4},{6,7},{7,6},{8,9},{9,8},{10,11... | collective-permute-start | bytes 1572872 | tf_op jit(solution)/shard_map/ppermute | solution.py:41
  137.8 2.8 %collective-permute-start.24 = (bf16[512,512]{1,0:T(8,128)(2,1)S(1)}, bf16[512,512]{1,0:T(8,128)(2,1)S(1)}, u32[]{:S(2)}, u32[]{:S(2)}) collective-permute-start(bf16[512,512]{1,0:T(8,128)(2,1)S(1)} %collective-permute-done.20.refs_3_), channel_id=1, source_target_pairs={{0,1},{1,0},{2,3},{3,2},{4,5},{5,4},{6,7},{7,6},{8,9},{9,8},{10,11... | collective-permute-start | bytes 1572872 | tf_op jit(solution)/shard_map/ppermute | solution.py:41
  140.6 12.2 %copy-start.11 = (s32[15]{0:T(128)S(1)}, s32[15]{0:T(128)}, u32[]{:S(2)}) copy-start(s32[15]{0:T(128)} %param.17) | copy-start | bytes 184
  140.6 23.5 %copy-start.2 = (bf16[16,128,256]{2,1,0:T(8,128)(2,1)S(1)}, bf16[16,128,256]{2,1,0:T(8,128)(2,1)}, u32[]{:S(2)}) copy-start(bf16[16,128,256]{2,1,0:T(8,128)(2,1)} %copy-done.1) | copy-start | bytes 3145732
  152.2 16.2 %copy-start.3 = (bf16[4,512,512]{2,1,0:T(8,128)(2,1)}, bf16[4,512,512]{2,1,0:T(8,128)(2,1)S(1)}, u32[]{:S(2)}) copy-start(bf16[4,512,512]{2,1,0:T(8,128)(2,1)S(1)} %get-tuple-element.12) | copy-start | bytes 6291460
  152.2 16.1 %collective-permute-start.25 = (bf16[4,512,512]{2,1,0:T(8,128)(2,1)S(1)}, bf16[4,512,512]{2,1,0:T(8,128)(2,1)S(1)}, u32[]{:S(2)}, u32[]{:S(2)}) collective-permute-start(bf16[4,512,512]{2,1,0:T(8,128)(2,1)S(1)} %get-tuple-element.13), channel_id=1, source_target_pairs={{0,1},{1,0},{2,3},{3,2},{4,5},{5,4},{6,7},{7,6},{8,9},{9,8},{10,11... | collective-permute-start | bytes 6291464 | tf_op jit(solution)/shard_map/ppermute | solution.py:41
  154.2 2.3 %collective-permute-start.4 = (f32[128,16]{0,1:T(8,128)S(1)}, f32[128,16]{0,1:T(8,128)S(1)}, u32[]{:S(2)}, u32[]{:S(2)}) collective-permute-start(f32[128,16]{0,1:T(8,128)S(1)} %maximum_maximum_fusion.1), channel_id=1, source_target_pairs={{0,1},{1,0},{2,3},{3,2},{4,5},{5,4},{6,7},{7,6},{8,9},{9,8},{10,11... | collective-permute-start | bytes 24584 | tf_op jit(solution)/shard_map/ppermute | solution.py:41
  156.5 2.5 %collective-permute-start.5 = (f32[128,16]{0,1:T(8,128)S(1)}, f32[128,16]{0,1:T(8,128)S(1)}, u32[]{:S(2)}, u32[]{:S(2)}) collective-permute-start(f32[128,16]{0,1:T(8,128)S(1)} %fusion.121), channel_id=1, source_target_pairs={{0,2},{1,3},{2,0},{3,1},{4,6},{5,7},{6,4},{7,5},{8,10},{9,11},{10,... | collective-permute-start | bytes 24584 | tf_op jit(solution)/shard_map/ppermute | solution.py:316
  159.1 9.3 %collective-permute-start.6 = (f32[128,16]{0,1:T(8,128)S(1)}, f32[128,16]{0,1:T(8,128)S(1)}, u32[]{:S(2)}, u32[]{:S(2)}) collective-permute-start(f32[128,16]{0,1:T(8,128)S(1)} %add.226), channel_id=1, source_target_pairs={{0,4},{1,5},{2,6},{3,7},{4,0},{5,1},{6,2},{7,3},{8,12},{9,13},{10,... | collective-permute-start | bytes 24584 | tf_op jit(solution)/shard_map/ppermute | solution.py:317
  161.8 11.9 %collective-permute-start.15 = (bf16[512,512]{1,0:T(8,128)(2,1)S(1)}, bf16[512,512]{1,0:T(8,128)(2,1)S(1)}, u32[]{:S(2)}, u32[]{:S(2)}) collective-permute-start(bf16[512,512]{1,0:T(8,128)(2,1)S(1)} %get-tuple-element.25.refs_8_), channel_id=1, source_target_pairs={{0,2},{1,3},{2,4},{3,5},{4,6},{5,7},{6,0},{7,1},{8,10},{9,11},{10,... | collective-permute-start | bytes 1572872 | tf_op jit(solution)/shard_map/ppermute | solution.py:37
  161.8 12.7 %collective-permute-start.16 = (bf16[512,512]{1,0:T(8,128)(2,1)S(1)}, bf16[512,512]{1,0:T(8,128)(2,1)S(1)}, u32[]{:S(2)}, u32[]{:S(2)}) collective-permute-start(bf16[512,512]{1,0:T(8,128)(2,1)S(1)} %get-tuple-element.23.refs_10_), channel_id=1, source_target_pairs={{0,6},{1,7},{2,0},{3,1},{4,2},{5,3},{6,4},{7,5},{8,14},{9,15},{10,... | collective-permute-start | bytes 1572872 | tf_op jit(solution)/shard_map/ppermute | solution.py:37
  163.2 22.7 %collective-permute-start.17 = (bf16[512,512]{1,0:T(8,128)(2,1)S(1)}, bf16[512,512]{1,0:T(8,128)(2,1)S(1)}, u32[]{:S(2)}, u32[]{:S(2)}) collective-permute-start(bf16[512,512]{1,0:T(8,128)(2,1)S(1)} %get-tuple-element.24.refs_9_), channel_id=1, source_target_pairs={{0,4},{1,5},{2,6},{3,7},{4,0},{5,1},{6,2},{7,3},{8,12},{9,13},{10,... | collective-permute-start | bytes 1572872 | tf_op jit(solution)/shard_map/ppermute | solution.py:37
  168.4 1.7 copy-start.5
  170.0 26.2 %collective-permute-start.26 = (bf16[512,512]{1,0:T(8,128)(2,1)}, bf16[512,512]{1,0:T(8,128)(2,1)}, u32[]{:S(2)}, u32[]{:S(2)}) collective-permute-start(bf16[512,512]{1,0:T(8,128)(2,1)} %get-tuple-element.20), channel_id=1, source_target_pairs={{0,2},{1,3},{2,4},{3,5},{4,6},{5,7},{6,0},{7,1},{8,10},{9,11},{10,... | collective-permute-start | bytes 1572872 | tf_op jit(solution)/shard_map/ppermute | solution.py:37
  172.1 25.4 %collective-permute-start.27 = (bf16[512,512]{1,0:T(8,128)(2,1)}, bf16[512,512]{1,0:T(8,128)(2,1)}, u32[]{:S(2)}, u32[]{:S(2)}) collective-permute-start(bf16[512,512]{1,0:T(8,128)(2,1)} %get-tuple-element.22), channel_id=1, source_target_pairs={{0,6},{1,7},{2,0},{3,1},{4,2},{5,3},{6,4},{7,5},{8,14},{9,15},{10,... | collective-permute-start | bytes 1572872 | tf_op jit(solution)/shard_map/ppermute | solution.py:37
  173.6 34.9 %collective-permute-start.28 = (bf16[512,512]{1,0:T(8,128)(2,1)S(1)}, bf16[512,512]{1,0:T(8,128)(2,1)}, u32[]{:S(2)}, u32[]{:S(2)}) collective-permute-start(bf16[512,512]{1,0:T(8,128)(2,1)S(1)} %get-tuple-element.21), channel_id=1, source_target_pairs={{0,4},{1,5},{2,6},{3,7},{4,0},{5,1},{6,2},{7,3},{8,12},{9,13},{10,... | collective-permute-start | bytes 1572872 | tf_op jit(solution)/shard_map/ppermute | solution.py:37
  187.1 24.2 %all-to-all-start.3 = ((bf16[16,32,512]{2,1,0:T(8,128)(2,1)}), bf16[16,32,512]{2,1,0:T(8,128)(2,1)S(1)}, u32[]{:S(2)}, u32[]{:S(2)}) async-start(bf16[16,32,512]{2,1,0:T(8,128)(2,1)} %bitcast.23), calls=%async_computation.3 | async-start | bytes 1048576 | tf_op jit(solution)/shard_map/all_to_all | solution.py:339
  211.4 12.8 %all-to-all-start.4 = ((bf16[16,32,512]{2,1,0:T(8,128)(2,1)}), bf16[16,32,512]{2,1,0:T(8,128)(2,1)S(1)}, u32[]{:S(2)}, u32[]{:S(2)}) async-start(bf16[16,32,512]{2,1,0:T(8,128)(2,1)} %bitcast.123), calls=%async_computation.4 | async-start | bytes 1048576 | tf_op jit(solution)/shard_map/all_to_all | solution.py:339

commit v2 on v1

--- a/solution.py
+++ b/solution.py
@@ -67,7 +67,7 @@
             q, kv_ref[:, :dim], (((1,), (1,)), ((), ())), preferred_element_type=F32
         )
         s = jnp.where(mask, s * scale, FLOOR)
-        w = jnp.where(mask, jnp.exp(s - jnp.max(s, axis=1, keepdims=True)), 0.0)
+        w = jnp.exp(s - jnp.max(s, axis=1, keepdims=True))
         mass = jnp.sum(w, axis=1, keepdims=True)
         acc = jnp.dot(w.astype(BF16), kv_ref[:, dim:], preferred_element_type=F32)
         heads.append((acc / mass).astype(BF16))
@@ -103,9 +103,9 @@
 
 
 def ffn_kernel(ids, gain_ref, wg_hbm, wu_hbm, wd_hbm, *refs):
-    pieces = refs[:8]
-    mine_ref, sib_ref = refs[-9:-7]
-    xs_ref, act_ref, wg_ref, wu_ref, wd_ref, sems, _ = refs[-7:]
+    pieces = refs[:10]
+    mine_ref, sib_ref = refs[-8:-6]
+    xs_ref, act_ref, wg_ref, wu_ref, wd_ref, sems = refs[-6:]
     copies = [
         pltpu.make_async_copy(hbm, ref, sems.at[i])
         for i, (hbm, ref) in enumerate(((wg_hbm, wg_ref), (wu_hbm, wu_ref), (wd_hbm, wd_ref)))
@@ -113,49 +113,55 @@
     for copy in copies:
         copy.start()
     rows, share = pieces[0].shape
+    half = rows // 2
     width = wg_ref.shape[0]
     tile = 32
 
-    def norm(i, carry):
-        at_row = pl.ds(pl.multiple_of(i * tile, tile), tile)
-        total = jnp.zeros((tile, share), F32)
-        for ref in pieces:
-            v = ref[at_row, :].astype(F32)
-            total = total + v * v
-        mean = jnp.sum(total, axis=1, keepdims=True) * (1.0 / width)
-        scale = lax.rsqrt(mean + EPS)
-        for k, ref in enumerate(pieces):
-            at = ids[k]
-            v = ref[at_row, :].astype(F32) * scale * gain_ref[pl.ds(at, 1), :]
-            xs_ref[at_row, pl.ds(pl.multiple_of(at * share, share), share)] = v.astype(BF16)
-        return carry
-
-    lax.fori_loop(0, rows // tile, norm, 0)
+    for side in range(2):
+        chosen = [(pieces[5 * s + k], 0, 4 * s + k) for s in range(2) for k in range(3)]
+        chosen += [(pieces[5 * s + 3 + side], side * half, 4 * s + 3) for s in range(2)]
+
+        def norm(i, carry):
+            at_row = pl.multiple_of(side * half + i * tile, tile)
+            total = jnp.zeros((tile, share), F32)
+            for ref, low, _ in chosen:
+                v = ref[pl.ds(pl.multiple_of(at_row - low, tile), tile), :].astype(F32)
+                total = total + v * v
+            mean = jnp.sum(total, axis=1, keepdims=True) * (1.0 / width)
+            scale = lax.rsqrt(mean + EPS)
+            for ref, low, k in chosen:
+                at = ids[k]
+                v = ref[pl.ds(pl.multiple_of(at_row - low, tile), tile), :].astype(F32)
+                v = v * scale * gain_ref[pl.ds(at, 1), :]
+                column = pl.ds(pl.multiple_of(at * share, share), share)
+                xs_ref[pl.ds(at_row, tile), column] = v.astype(BF16)
+            return carry
+
+        lax.fori_loop(0, half // tile, norm, 0)
     copies[0].wait()
     copies[1].wait()
-    block = 256
 
     def hidden(i, carry):
-        at_row = pl.ds(pl.multiple_of(i * block, block), block)
+        at_row = pl.ds(pl.multiple_of(i * half, half), half)
         v = xs_ref[at_row, :]
         gate = jnp.dot(v, wg_ref[...], preferred_element_type=F32)
         up = jnp.dot(v, wu_ref[...], preferred_element_type=F32)
         act_ref[at_row, :] = (gate / (1.0 + jnp.exp(-gate)) * up).astype(BF16)
         return carry
 
-    lax.fori_loop(0, rows // block, hidden, 0)
+    lax.fori_loop(0, 2, hidden, 0)
     copies[2].wait()
 
-    def down(at):
-        w = wd_ref[:, pl.ds(pl.multiple_of(at * share, share), share)]
-        return jnp.dot(act_ref[...], w, preferred_element_type=F32).astype(BF16)
-
-    def body(d, carry):
-        sib_ref[d] = down(ids[12 + d])
-        mine_ref[d] = down(ids[8 + d])
+    def body(i, carry):
+        block = i // 2
+        at_row = pl.ds(pl.multiple_of((i - block * 2) * half, half), half)
+        for ref, base in ((sib_ref, 16), (mine_ref, 8)):
+            w = wd_ref[:, pl.ds(pl.multiple_of(ids[base + i] * share, share), share)]
+            out = jnp.dot(act_ref[at_row, :], w, preferred_element_type=F32)
+            ref[block, at_row, :] = out.astype(BF16)
         return carry
 
-    lax.fori_loop(0, NZ, body, 0)
+    lax.fori_loop(0, 8, body, 0)
 
 
 def ffn(ids, gain, w_gate, w_up, w_down, pieces, after):
@@ -178,33 +184,76 @@
             pltpu.VMEM(w_up.shape, BF16),
             pltpu.VMEM(w_down.shape, BF16),
             pltpu.SemaphoreType.DMA((3,)),
-            pltpu.VMEM((8, 128), F32),
         ],
         compiler_params=pltpu.CompilerParams(vmem_limit_bytes=36 * MIB),
     )(ids, gain, w_gate, w_up, w_down, *pieces, *after)
 
 
 def gather_ring(own):
-    ring = [own] + [send_z(own, d) for d in (1, 3, 2)]
-    near = [send_core(own)]
-    return ring + near + [send_core(v) for v in ring[1:]]
-
-
-def add(*parts):
-    total = parts[0].astype(F32)
-    for part in parts[1:]:
-        total = total + part.astype(F32)
-    return total.astype(BF16)
+    half = own.shape[0] // 2
+    below = send_z(own, 1)
+    above = send_z(own, -1)
+    far_a = send_z(below[:half], 1)
+    far_b = send_z(above[half:], -1)
+    own_s = send_core(own)
+    near_s = [send_core(below), send_core(above)]
+    far_s = [send_core(far_a), send_core(far_b)]
+    return [own, below, above, far_a, far_b, own_s] + near_s + far_s
+
+
+def mix_kernel(mine_ref, got_ref, up_ref, down_ref):
+    for k, ref in enumerate((up_ref, down_ref)):
+        ref[...] = (mine_ref[k].astype(F32) + got_ref[k].astype(F32)).astype(BF16)
+
+
+def relay_kernel(mine_ref, got_ref, below_ref, above_ref, low_ref, high_ref):
+    total = mine_ref[0].astype(F32) + got_ref[0].astype(F32)
+    half = low_ref.shape[0]
+    low_ref[...] = (total[:half] + below_ref[:half, :].astype(F32)).astype(BF16)
+    high_ref[...] = (total[half:] + above_ref[half:, :].astype(F32)).astype(BF16)
+
+
+def end_kernel(mine_ref, got_ref, below_ref, above_ref, low_ref, high_ref, out_ref):
+    total = mine_ref[0].astype(F32) + got_ref[0].astype(F32)
+    half = low_ref.shape[0]
+    first = total[:half] + above_ref[:half, :].astype(F32) + low_ref[...].astype(F32)
+    second = total[half:] + below_ref[half:, :].astype(F32) + high_ref[...].astype(F32)
+    out_ref[:half, :] = first.astype(BF16)
+    out_ref[half:, :] = second.astype(BF16)
+
+
+def combine_blocks(kernel, pair, count, index, more, outs):
+    _, rows, share = pair[0].shape
+    block = pl.BlockSpec((count, rows, share), lambda i: (index, 0, 0))
+
+    def whole(height):
+        return pl.BlockSpec((height, share), lambda i: (0, 0))
+
+    return pl.pallas_call(
+        kernel,
+        grid=(1,),
+        out_shape=tuple(jax.ShapeDtypeStruct((height, share), BF16) for height in outs),
+        in_specs=[block, block] + [whole(v.shape[0]) for v in more],
+        out_specs=tuple(whole(height) for height in outs),
+        compiler_params=pltpu.CompilerParams(vmem_limit_bytes=16 * MIB),
+    )(*pair, *more)
 
 
 def scatter_start(mine, sib):
+    rows = mine.shape[1]
     got = send_core(sib)
-    return [add(mine[d], got[d]) for d in range(1, NZ)], (mine[0], got[0])
-
-
-def scatter_end(sums, own):
-    moved = [send_z(sums[d - 1], d) for d in (1, 3, 2)]
-    return add(*own, *moved)
+    return *combine_blocks(mix_kernel, (mine, got), 2, 0, (), (rows, rows)), mine, got
+
+
+def scatter_end(up, down, mine, got):
+    rows = up.shape[0]
+    half = rows // 2
+    from_below = send_z(up, 1)
+    from_above = send_z(down, -1)
+    moved = (from_below, from_above)
+    low, high = combine_blocks(relay_kernel, (mine, got), 1, 2, moved, (half, half))
+    last = (send_z(low, 1), send_z(high, -1))
+    return combine_blocks(end_kernel, (mine, got), 1, 3, moved + last, (rows,))[0]
 
 
 def local(
@@ -323,24 +372,24 @@
     gate_dup = jnp.repeat(gate_of, holders, axis=1)
 
     gain_rows = gain_moe.reshape(ten_count, share)
-    order = jnp.array([0, 3, 1, 2], jnp.int32)
-    source = lax.rem(z + order, NZ) * 2
-    ids = jnp.concatenate([source + c, source + other_c, out_ids])
+    source = lax.rem(z + jnp.array([0, 3, 1, 2], jnp.int32), NZ) * 2
+    target = lax.rem(z + jnp.array([2, 1, 3, 2, 1, 3, 0, 0], jnp.int32), NZ) * 2
+    ids = jnp.concatenate([source + c, source + other_c, target + c, target + other_c])
     a_own = dispatch(picks[0])
     a_pieces = gather_ring(a_own)
     b_own = dispatch(picks[1])
     b_pieces = gather_ring(b_own)
-    a_out = ffn(ids, gain_rows, w_gate, w_up, w_down, a_pieces, [b_own])
-    a_sums, a_rest = scatter_start(*a_out)
-    b_out = ffn(ids, gain_rows, w_gate, w_up, w_down, b_pieces, a_sums)
-    b_sums, b_rest = scatter_start(*b_out)
+    a_out = ffn(ids, gain_rows, w_gate, w_up, w_down, a_pieces, [])
+    a_start = scatter_start(*a_out)
+    b_out = ffn(ids, gain_rows, w_gate, w_up, w_down, b_pieces, a_start[:2])
+    b_start = scatter_start(*b_out)
 
     def give_back(parts):
         got = lax.all_to_all(parts.reshape(seq_count, slots, share), "seq", 0, 0, tiled=True)
         return got.reshape(seq_count * slots, share)
 
-    a_final = scatter_end(a_sums, a_rest)
-    b_final = scatter_end(b_sums, b_rest)
+    a_final = scatter_end(*a_start)
+    b_final = scatter_end(*b_start)
     a_back = give_back(a_final)
     b_back = give_back(b_final)
 

time: 232 us -> 245 us (1.056)
  the two profiles are of different devices: /device:TPU:33 before, /device:TPU:0 now
where the time goes in v2:
time: 245 us; the launch traced here: 244 us
  waiting for transfers between devices  73.4 us (30%)
  starting transfers between devices  54.1 us (22%)
  Pallas kernels  38.3 us (16%)
  blocking collectives  29.1 us (12%)
  local copies, waits for them, and re-layouts  18.8 us (8%)
  matrix products  16.2 us (7%)
  other arithmetic  13.1 us (5%)
    ppermute x19, waiting for transfers between devices, send_z(): return lax.ppermute(value, 'tensor', z_perm(step))  37.7 us
    ppermute x19, starting transfers between devices, send_z(): return lax.ppermute(value, 'tensor', z_perm(step))  32.5 us
    all_to_all x2, blocking collectives, dispatch(): lax.all_to_all(out.reshape(seq_count, slots, share), 'seq', 0, 0, tiled=T...  29.1 us
    pallas_call x2, Pallas kernels, ffn(): pl.pallas_call(ffn_kernel, out_shape=(jax.ShapeDtypeStruct((NZ, rows, sha...  24.9 us
    unnamed x62, local copies, waits for them, and re-layouts  14.1 us
    all_to_all x1, waiting for transfers between devices, local(): lax.all_to_all(jnp.broadcast_to(kv_own[None], (seq_count,) + kv_own.shape...  13.7 us
    ppermute x1, waiting for transfers between devices, local(): lax.ppermute(stats, 'tensor', [(t, t ^ 2) for t in range(ten_count)])  9.69 us
    all_to_all x2, starting transfers between devices, give_back(): lax.all_to_all(parts.reshape(seq_count, slots, share), 'seq', 0, 0, tiled...  8.81 us
  transfers between devices with their start and end apart: 38, of which 18 were waited for; matrix products, arithmetic and copies ran while one was open for 9% of the time, Pallas kernels for 3%

profile of v2, /device:TPU:0, one launch (start us, length us, event | category | flops | bytes accessed | tf_op | source)
XLA Modules:
  0.0 244.0 jit_solution(8940022451463133189)
XLA Ops:
  1.9 1.5 fusion.3
  3.4 1.7 fusion.15
  6.6 7.1 %all-to-all-start = ((bf16[16,128,256]{2,1,0:T(8,128)(2,1)}), bf16[16,128,256]{2,1,0:T(8,128)(2,1)S(1)}, u32[]{:S(2)}, u32[]{:S(2)}) async-start(bf16[16,128,256]{2,1,0:T(8,128)(2,1)} %broadcast_in_dim.110), calls=%async_computation | async-start | bytes 2097152 | tf_op jit(solution)/shard_map/all_to_all | solution.py:315
  14.0 3.3 %fusion.17 = f32[128,512]{1,0:T(8,128)S(1)} fusion(bf16[4096,512]{1,0:T(8,128)(2,1)} %param.20, bf16[128,4096]{1,0:T(8,128)(2,1)} %param.15, f32[4096]{0:T(1024)S(1)} %copy-done.29, f32[128]{0:T(128)S(1)} %add_rsqrt_fusion), kind=kOutput, calls=%fused_computation.37 | convolution fusion | flops 538968064 | bytes 5521920 | tf_op jit(solution)/shard_map/dot_general | solution.py:306
  17.8 13.7 %all-to-all-done = bf16[16,128,256]{2,1,0:T(8,128)(2,1)S(1)} async-done(((bf16[16,128,256]{2,1,0:T(8,128)(2,1)}), bf16[16,128,256]{2,1,0:T(8,128)(2,1)S(1)}, u32[]{:S(2)}, u32[]{:S(2)}) %all-to-all-start) | async-done | bytes 1048608 | tf_op jit(solution)/shard_map/all_to_all | solution.py:315
  31.5 7.1 %shard_map.158 = (f32[4,128,512]{2,1,0:T(8,128)S(1)}, bf16[4,128,512]{2,1,0:T(8,128)(2,1)}) custom-call(s32[8]{0:T(128)S(1)} %pad_add_fusion.ids, s32[1]{0:T(128)} %bitcast.first_ref, bf16[512,128]{1,0:T(8,128)(2,1)S(1)} %maximum_maximum_fusion.q_ref, s32[128,1]{1,0:T(8,128)S(1)} %copy.20.start_ref, bf16[2048,256]{1,0:T(8,128)(2,1)S(1)} %bitcast.80, ...), custom_call_target="tpu_custom_call" | custom-call | tf_op jit(solution)/shard_map/pallas_call | solution.py:92
  40.2 1.6 collective-permute-done
  41.8 1.4 fusion.29
  43.2 2.0 collective-permute-start.1
  45.2 2.2 collective-permute-start.2
  47.4 1.8 collective-permute-start.3
  51.1 2.2 collective-permute-done.2
  53.3 1.8 collective-permute-done.3
  55.1 1.7 fusion.22
  57.1 13.9 %all_to_all.25 = bf16[16,32,512]{2,1,0:T(8,128)(2,1)S(1)} all-to-all(bf16[16,32,512]{2,1,0:T(8,128)(2,1)S(1)} %bitcast.91), channel_id=1, replica_groups=mesh['seq'=16,'tensor'=8] {'seq'}, dimensions={0} | all-to-all | bytes 1048576 | tf_op jit(solution)/shard_map/all_to_all | solution.py:353
  71.9 2.4 collective-permute-start.8
  74.8 9.7 %collective-permute-done.7.refs_1_ = bf16[512,512]{1,0:T(8,128)(2,1)S(1)} collective-permute-done((bf16[512,512]{1,0:T(8,128)(2,1)S(1)}, bf16[512,512]{1,0:T(8,128)(2,1)S(1)}, u32[]{:S(2)}, u32[]{:S(2)}) %collective-permute-start.7) | collective-permute-done | bytes 524320 | tf_op jit(solution)/shard_map/ppermute | solution.py:37
  86.3 3.1 %collective-permute-start.10 = (bf16[256,512]{1,0:T(8,128)(2,1)}, bf16[256,512]{1,0:T(8,128)(2,1)}, u32[]{:S(2)}, u32[]{:S(2)}) collective-permute-start(bf16[256,512]{1,0:T(8,128)(2,1)} %slice.142), channel_id=1, source_target_pairs={{0,6},{1,7},{2,0},{3,1},{4,2},{5,3},{6,4},{7,5},{8,14},{9,15},{10,... | collective-permute-start | bytes 786440 | tf_op jit(solution)/shard_map/ppermute | solution.py:37
  91.9 1.2 collective-permute-done.9.refs_3_
  98.5 12.7 %shard_map.159 = (bf16[4,512,512]{2,1,0:T(8,128)(2,1)S(1)}, bf16[4,512,512]{2,1,0:T(8,128)(2,1)S(1)}) custom-call(s32[24]{0:T(128)S(1)} %pad_add_fusion.1.ids, f32[8,512]{1,0:T(8,128)S(1)} %reshape.167.gain_ref, bf16[4096,512]{1,0:T(8,128)(2,1)} %wg_hbm.3, bf16[4096,512]{1,0:T(8,128)(2,1)} %wu_hbm.3, bf16[512,4096]{1,0:T(8,128)(2,1)} %wd_hbm.3, ...), custom_call_target="tpu_custom_call" | custom-call | tf_op jit(solution)/shard_map/pallas_call | solution.py:169
  111.7 15.2 %all_to_all.26 = bf16[16,32,512]{2,1,0:T(8,128)(2,1)S(1)} all-to-all(bf16[16,32,512]{2,1,0:T(8,128)(2,1)S(1)} %bitcast.92), channel_id=1, replica_groups=mesh['seq'=16,'tensor'=8] {'seq'}, dimensions={0} | all-to-all | bytes 1048576 | tf_op jit(solution)/shard_map/all_to_all | solution.py:353
  127.0 3.7 %collective-permute-start.22 = (bf16[512,512]{1,0:T(8,128)(2,1)S(1)}, bf16[512,512]{1,0:T(8,128)(2,1)S(1)}, u32[]{:S(2)}, u32[]{:S(2)}) collective-permute-start(bf16[512,512]{1,0:T(8,128)(2,1)S(1)} %bitcast.87), channel_id=1, source_target_pairs={{0,6},{1,7},{2,0},{3,1},{4,2},{5,3},{6,4},{7,5},{8,14},{9,15},{10,... | collective-permute-start | bytes 1572872 | tf_op jit(solution)/shard_map/ppermute | solution.py:37
  130.7 11.0 %collective-permute-done.21.refs_1_ = bf16[512,512]{1,0:T(8,128)(2,1)S(1)} collective-permute-done((bf16[512,512]{1,0:T(8,128)(2,1)S(1)}, bf16[512,512]{1,0:T(8,128)(2,1)S(1)}, u32[]{:S(2)}, u32[]{:S(2)}) %collective-permute-start.21) | collective-permute-done | bytes 524320 | tf_op jit(solution)/shard_map/ppermute | solution.py:37
  141.8 3.3 %collective-permute-start.24 = (bf16[256,512]{1,0:T(8,128)(2,1)S(1)}, bf16[256,512]{1,0:T(8,128)(2,1)S(1)}, u32[]{:S(2)}, u32[]{:S(2)}) collective-permute-start(bf16[256,512]{1,0:T(8,128)(2,1)S(1)} %slice.144), channel_id=1, source_target_pairs={{0,6},{1,7},{2,0},{3,1},{4,2},{5,3},{6,4},{7,5},{8,14},{9,15},{10,... | collective-permute-start | bytes 786440 | tf_op jit(solution)/shard_map/ppermute | solution.py:37
  145.6 3.9 %collective-permute-done.23.refs_3_ = bf16[256,512]{1,0:T(8,128)(2,1)S(1)} collective-permute-done((bf16[256,512]{1,0:T(8,128)(2,1)S(1)}, bf16[256,512]{1,0:T(8,128)(2,1)S(1)}, u32[]{:S(2)}, u32[]{:S(2)}) %collective-permute-start.23) | collective-permute-done | bytes 262176 | tf_op jit(solution)/shard_map/ppermute | solution.py:37
  150.4 1.4 collective-permute-done.28.refs_8_
  152.2 12.2 %shard_map.163 = (bf16[4,512,512]{2,1,0:T(8,128)(2,1)S(1)}, bf16[4,512,512]{2,1,0:T(8,128)(2,1)S(1)}) custom-call(s32[24]{0:T(128)S(1)} %pad_add_fusion.1.ids, f32[8,512]{1,0:T(8,128)S(1)} %reshape.167.gain_ref, bf16[4096,512]{1,0:T(8,128)(2,1)} %wg_hbm.3, bf16[4096,512]{1,0:T(8,128)(2,1)} %wu_hbm.3, bf16[512,4096]{1,0:T(8,128)(2,1)} %wd_hbm.3, ...), custom_call_target="tpu_custom_call" | custom-call | tf_op jit(solution)/shard_map/pallas_call | solution.py:169
  166.9 3.3 %collective-permute-start.18 = (bf16[512,512]{1,0:T(8,128)(2,1)S(1)}, bf16[512,512]{1,0:T(8,128)(2,1)S(1)}, u32[]{:S(2)}, u32[]{:S(2)}) collective-permute-start(bf16[512,512]{1,0:T(8,128)(2,1)S(1)} %get-tuple-element.21.refs_11_), channel_id=1, source_target_pairs={{0,6},{1,7},{2,0},{3,1},{4,2},{5,3},{6,4},{7,5},{8,14},{9,15},{10,... | collective-permute-start | bytes 1572872 | tf_op jit(solution)/shard_map/ppermute | solution.py:37
  171.6 9.7 %collective-permute-done.5 = f32[128,16]{0,1:T(8,128)S(1)} collective-permute-done((f32[128,16]{0,1:T(8,128)S(1)}, f32[128,16]{0,1:T(8,128)S(1)}, u32[]{:S(2)}, u32[]{:S(2)}) %collective-permute-start.5) | collective-permute-done | bytes 8224 | tf_op jit(solution)/shard_map/ppermute | solution.py:365
  181.3 3.5 %collective-permute-start.6 = (f32[128,16]{0,1:T(8,128)S(1)}, f32[128,16]{0,1:T(8,128)S(1)}, u32[]{:S(2)}, u32[]{:S(2)}) collective-permute-start(f32[128,16]{0,1:T(8,128)S(1)} %add.190), channel_id=1, source_target_pairs={{0,4},{1,5},{2,6},{3,7},{4,0},{5,1},{6,2},{7,3},{8,12},{9,13},{10,... | collective-permute-start | bytes 24584 | tf_op jit(solution)/shard_map/ppermute | solution.py:366
  185.2 3.2 %collective-permute-start.20 = (bf16[256,512]{1,0:T(8,128)(2,1)S(1)}, bf16[256,512]{1,0:T(8,128)(2,1)S(1)}, u32[]{:S(2)}, u32[]{:S(2)}) collective-permute-start(bf16[256,512]{1,0:T(8,128)(2,1)S(1)} %get-tuple-element.23), channel_id=1, source_target_pairs={{0,6},{1,7},{2,0},{3,1},{4,2},{5,3},{6,4},{7,5},{8,14},{9,15},{10,... | collective-permute-start | bytes 786440 | tf_op jit(solution)/shard_map/ppermute | solution.py:37
  188.4 1.3 shard_map.164
  190.0 3.2 %collective-permute-start.32 = (bf16[512,512]{1,0:T(8,128)(2,1)}, bf16[512,512]{1,0:T(8,128)(2,1)}, u32[]{:S(2)}, u32[]{:S(2)}) collective-permute-start(bf16[512,512]{1,0:T(8,128)(2,1)} %get-tuple-element.27), channel_id=1, source_target_pairs={{0,6},{1,7},{2,0},{3,1},{4,2},{5,3},{6,4},{7,5},{8,14},{9,15},{10,... | collective-permute-start | bytes 1572872 | tf_op jit(solution)/shard_map/ppermute | solution.py:37
  193.3 4.2 %fusion.2 = bf16[2048,256]{1,0:T(8,128)(2,1)} fusion(bf16[2048,256]{1,0:T(8,128)(2,1)S(1)} %bitcast.81, s32[2048]{0:T(1024)S(1)} %fusion.13), kind=kOutput, calls=%fused_computation.5 | convolution fusion | flops 2152202240 | bytes 2105344 | tf_op jit(solution)/shard_map/dot_general | solution.py:423
  198.5 4.2 %all-to-all-start.2 = ((bf16[16,32,512]{2,1,0:T(8,128)(2,1)}), bf16[16,32,512]{2,1,0:T(8,128)(2,1)}, u32[]{:S(2)}, u32[]{:S(2)}) async-start(bf16[16,32,512]{2,1,0:T(8,128)(2,1)} %bitcast.17), calls=%async_computation.2 | async-start | bytes 1048576 | tf_op jit(solution)/shard_map/all_to_all | solution.py:388
  202.8 2.1 collective-permute-done.31.below_ref
  204.9 1.6 copy-done.2
  206.5 1.6 copy-done.5
  208.1 2.1 shard_map.165
  210.2 3.2 %collective-permute-start.34 = (bf16[256,512]{1,0:T(8,128)(2,1)}, bf16[256,512]{1,0:T(8,128)(2,1)S(1)}, u32[]{:S(2)}, u32[]{:S(2)}) collective-permute-start(bf16[256,512]{1,0:T(8,128)(2,1)} %get-tuple-element.29), channel_id=1, source_target_pairs={{0,6},{1,7},{2,0},{3,1},{4,2},{5,3},{6,4},{7,5},{8,14},{9,15},{10,... | collective-permute-start | bytes 786440 | tf_op jit(solution)/shard_map/ppermute | solution.py:37
  213.9 4.5 %collective-permute-done.33.low_ref = bf16[256,512]{1,0:T(8,128)(2,1)S(1)} collective-permute-done((bf16[256,512]{1,0:T(8,128)(2,1)}, bf16[256,512]{1,0:T(8,128)(2,1)S(1)}, u32[]{:S(2)}, u32[]{:S(2)}) %collective-permute-start.33) | collective-permute-done | bytes 262176 | tf_op jit(solution)/shard_map/ppermute | solution.py:37
  219.1 1.6 copy-done.3
  220.7 1.6 copy-done.6
  223.3 1.5 shard_map.166
  225.5 4.6 %all-to-all-start.4 = ((bf16[16,32,512]{2,1,0:T(8,128)(2,1)}), bf16[16,32,512]{2,1,0:T(8,128)(2,1)S(1)}, u32[]{:S(2)}, u32[]{:S(2)}) async-start(bf16[16,32,512]{2,1,0:T(8,128)(2,1)} %bitcast.90), calls=%async_computation.4 | async-start | bytes 1048576 | tf_op jit(solution)/shard_map/all_to_all | solution.py:388
  231.5 1.3 convolution_bitcast_fusion.2
  232.8 7.5 %all-to-all-done.4 = bf16[16,32,512]{2,1,0:T(8,128)(2,1)S(1)} async-done(((bf16[16,32,512]{2,1,0:T(8,128)(2,1)}), bf16[16,32,512]{2,1,0:T(8,128)(2,1)S(1)}, u32[]{:S(2)}, u32[]{:S(2)}) %all-to-all-start.4) | async-done | bytes 524320 | tf_op jit(solution)/shard_map/all_to_all | solution.py:388
  242.1 2.0 fusion.10
  (168 shorter events, 32.6 us)
Async XLA Ops:
  5.1 8.9 %copy-start.29 = (f32[4096]{0:T(1024)S(1)}, f32[4096]{0:T(1024)}, u32[]{:S(2)}) copy-start(f32[4096]{0:T(1024)} %param.19) | copy-start | bytes 49156
  6.6 24.8 %all-to-all-start = ((bf16[16,128,256]{2,1,0:T(8,128)(2,1)}), bf16[16,128,256]{2,1,0:T(8,128)(2,1)S(1)}, u32[]{:S(2)}, u32[]{:S(2)}) async-start(bf16[16,128,256]{2,1,0:T(8,128)(2,1)} %broadcast_in_dim.110), calls=%async_computation | async-start | bytes 2097152 | tf_op jit(solution)/shard_map/all_to_all | solution.py:315
  39.6 2.3 collective-permute-start
  41.8 32.4 %copy-start.28 = (s32[4]{0:T(128)S(1)}, s32[4]{0:T(128)}, u32[]{:S(2)}) copy-start(s32[4]{0:T(128)} %constant.76.clone) | copy-start | bytes 52
  43.2 46.2 %copy-start.27 = (s32[8]{0:T(128)S(1)}, s32[8]{0:T(128)}, u32[]{:S(2)}) copy-start(s32[8]{0:T(128)} %constant.77.clone) | copy-start | bytes 100
  43.2 7.9 %collective-permute-start.1 = (bf16[128,512]{1,0:T(8,128)(2,1)S(1)}, bf16[128,512]{1,0:T(8,128)(2,1)S(1)}, u32[]{:S(2)}, u32[]{:S(2)}) collective-permute-start(bf16[128,512]{1,0:T(8,128)(2,1)S(1)} %get-tuple-element.38), channel_id=1, source_target_pairs={{0,2},{1,3},{2,4},{3,5},{4,6},{5,7},{6,0},{7,1},{8,10},{9,11},{10,... | collective-permute-start | bytes 393224 | tf_op jit(solution)/shard_map/ppermute | solution.py:37
  45.2 8.1 %collective-permute-start.2 = (bf16[128,512]{1,0:T(8,128)(2,1)S(1)}, bf16[128,512]{1,0:T(8,128)(2,1)S(1)}, u32[]{:S(2)}, u32[]{:S(2)}) collective-permute-start(bf16[128,512]{1,0:T(8,128)(2,1)S(1)} %get-tuple-element.40), channel_id=1, source_target_pairs={{0,6},{1,7},{2,0},{3,1},{4,2},{5,3},{6,4},{7,5},{8,14},{9,15},{10,... | collective-permute-start | bytes 393224 | tf_op jit(solution)/shard_map/ppermute | solution.py:37
  47.4 7.7 %collective-permute-start.3 = (bf16[128,512]{1,0:T(8,128)(2,1)S(1)}, bf16[128,512]{1,0:T(8,128)(2,1)S(1)}, u32[]{:S(2)}, u32[]{:S(2)}) collective-permute-start(bf16[128,512]{1,0:T(8,128)(2,1)S(1)} %get-tuple-element.39), channel_id=1, source_target_pairs={{0,4},{1,5},{2,6},{3,7},{4,0},{5,1},{6,2},{7,3},{8,12},{9,13},{10,... | collective-permute-start | bytes 393224 | tf_op jit(solution)/shard_map/ppermute | solution.py:37
  71.0 13.5 %collective-permute-start.7 = (bf16[512,512]{1,0:T(8,128)(2,1)S(1)}, bf16[512,512]{1,0:T(8,128)(2,1)S(1)}, u32[]{:S(2)}, u32[]{:S(2)}) collective-permute-start(bf16[512,512]{1,0:T(8,128)(2,1)S(1)} %bitcast.82), channel_id=1, source_target_pairs={{0,2},{1,3},{2,4},{3,5},{4,6},{5,7},{6,0},{7,1},{8,10},{9,11},{10,... | collective-permute-start | bytes 1572872 | tf_op jit(solution)/shard_map/ppermute | solution.py:37
  71.9 13.4 %collective-permute-start.8 = (bf16[512,512]{1,0:T(8,128)(2,1)S(1)}, bf16[512,512]{1,0:T(8,128)(2,1)S(1)}, u32[]{:S(2)}, u32[]{:S(2)}) collective-permute-start(bf16[512,512]{1,0:T(8,128)(2,1)S(1)} %bitcast.83), channel_id=1, source_target_pairs={{0,6},{1,7},{2,0},{3,1},{4,2},{5,3},{6,4},{7,5},{8,14},{9,15},{10,... | collective-permute-start | bytes 1572872 | tf_op jit(solution)/shard_map/ppermute | solution.py:37
  85.3 7.8 %collective-permute-start.9 = (bf16[256,512]{1,0:T(8,128)(2,1)}, bf16[256,512]{1,0:T(8,128)(2,1)S(1)}, u32[]{:S(2)}, u32[]{:S(2)}) collective-permute-start(bf16[256,512]{1,0:T(8,128)(2,1)} %slice.141), channel_id=1, source_target_pairs={{0,2},{1,3},{2,4},{3,5},{4,6},{5,7},{6,0},{7,1},{8,10},{9,11},{10,... | collective-permute-start | bytes 786440 | tf_op jit(solution)/shard_map/ppermute | solution.py:37
  86.3 7.3 %collective-permute-start.10 = (bf16[256,512]{1,0:T(8,128)(2,1)}, bf16[256,512]{1,0:T(8,128)(2,1)}, u32[]{:S(2)}, u32[]{:S(2)}) collective-permute-start(bf16[256,512]{1,0:T(8,128)(2,1)} %slice.142), channel_id=1, source_target_pairs={{0,6},{1,7},{2,0},{3,1},{4,2},{5,3},{6,4},{7,5},{8,14},{9,15},{10,... | collective-permute-start | bytes 786440 | tf_op jit(solution)/shard_map/ppermute | solution.py:37
  90.8 4.3 %collective-permute-start.11 = (bf16[512,512]{1,0:T(8,128)(2,1)}, bf16[512,512]{1,0:T(8,128)(2,1)S(1)}, u32[]{:S(2)}, u32[]{:S(2)}) collective-permute-start(bf16[512,512]{1,0:T(8,128)(2,1)} %bitcast.84), channel_id=1, source_target_pairs={{0,1},{1,0},{2,3},{3,2},{4,5},{5,4},{6,7},{7,6},{8,9},{9,8},{10,11... | collective-permute-start | bytes 1572872 | tf_op jit(solution)/shard_map/ppermute | solution.py:41
  90.8 4.7 %collective-permute-start.12 = (bf16[512,512]{1,0:T(8,128)(2,1)}, bf16[512,512]{1,0:T(8,128)(2,1)S(1)}, u32[]{:S(2)}, u32[]{:S(2)}) collective-permute-start(bf16[512,512]{1,0:T(8,128)(2,1)} %copy-done.10), channel_id=1, source_target_pairs={{0,1},{1,0},{2,3},{3,2},{4,5},{5,4},{6,7},{7,6},{8,9},{9,8},{10,11... | collective-permute-start | bytes 1572872 | tf_op jit(solution)/shard_map/ppermute | solution.py:41
  91.3 4.1 %collective-permute-start.13 = (bf16[512,512]{1,0:T(8,128)(2,1)}, bf16[512,512]{1,0:T(8,128)(2,1)S(1)}, u32[]{:S(2)}, u32[]{:S(2)}) collective-permute-start(bf16[512,512]{1,0:T(8,128)(2,1)} %copy-done.12), channel_id=1, source_target_pairs={{0,1},{1,0},{2,3},{3,2},{4,5},{5,4},{6,7},{7,6},{8,9},{9,8},{10,11... | collective-permute-start | bytes 1572872 | tf_op jit(solution)/shard_map/ppermute | solution.py:41
  93.1 1.9 collective-permute-start.14
  93.7 1.7 collective-permute-start.15
  98.5 12.9 %copy-start.19 = (pred[512,128]{1,0:T(32,128)(4,1)S(1)}, pred[512,128]{1,0:T(32,128)(4,1)}, u32[]{:S(2)}) copy-start(pred[512,128]{1,0:T(32,128)(4,1)} %get-tuple-element.52) | copy-start | bytes 196612
  111.2 38.8 %collective-permute-start.16 = (bf16[4,512,512]{2,1,0:T(8,128)(2,1)S(1)}, bf16[4,512,512]{2,1,0:T(8,128)(2,1)S(1)}, u32[]{:S(2)}, u32[]{:S(2)}) collective-permute-start(bf16[4,512,512]{2,1,0:T(8,128)(2,1)S(1)} %get-tuple-element.19), channel_id=1, source_target_pairs={{0,1},{1,0},{2,3},{3,2},{4,5},{5,4},{6,7},{7,6},{8,9},{9,8},{10,11... | collective-permute-start | bytes 6291464 | tf_op jit(solution)/shard_map/ppermute | solution.py:41
  127.0 14.7 %collective-permute-start.21 = (bf16[512,512]{1,0:T(8,128)(2,1)S(1)}, bf16[512,512]{1,0:T(8,128)(2,1)S(1)}, u32[]{:S(2)}, u32[]{:S(2)}) collective-permute-start(bf16[512,512]{1,0:T(8,128)(2,1)S(1)} %bitcast.86), channel_id=1, source_target_pairs={{0,2},{1,3},{2,4},{3,5},{4,6},{5,7},{6,0},{7,1},{8,10},{9,11},{10,... | collective-permute-start | bytes 1572872 | tf_op jit(solution)/shard_map/ppermute | solution.py:37
  127.0 14.8 %collective-permute-start.22 = (bf16[512,512]{1,0:T(8,128)(2,1)S(1)}, bf16[512,512]{1,0:T(8,128)(2,1)S(1)}, u32[]{:S(2)}, u32[]{:S(2)}) collective-permute-start(bf16[512,512]{1,0:T(8,128)(2,1)S(1)} %bitcast.87), channel_id=1, source_target_pairs={{0,6},{1,7},{2,0},{3,1},{4,2},{5,3},{6,4},{7,5},{8,14},{9,15},{10,... | collective-permute-start | bytes 1572872 | tf_op jit(solution)/shard_map/ppermute | solution.py:37
  141.7 7.8 %collective-permute-start.23 = (bf16[256,512]{1,0:T(8,128)(2,1)S(1)}, bf16[256,512]{1,0:T(8,128)(2,1)S(1)}, u32[]{:S(2)}, u32[]{:S(2)}) collective-permute-start(bf16[256,512]{1,0:T(8,128)(2,1)S(1)} %slice.143), channel_id=1, source_target_pairs={{0,2},{1,3},{2,4},{3,5},{4,6},{5,7},{6,0},{7,1},{8,10},{9,11},{10,... | collective-permute-start | bytes 786440 | tf_op jit(solution)/shard_map/ppermute | solution.py:37
  141.8 7.7 %collective-permute-start.24 = (bf16[256,512]{1,0:T(8,128)(2,1)S(1)}, bf16[256,512]{1,0:T(8,128)(2,1)S(1)}, u32[]{:S(2)}, u32[]{:S(2)}) collective-permute-start(bf16[256,512]{1,0:T(8,128)(2,1)S(1)} %slice.144), channel_id=1, source_target_pairs={{0,6},{1,7},{2,0},{3,1},{4,2},{5,3},{6,4},{7,5},{8,14},{9,15},{10,... | collective-permute-start | bytes 786440 | tf_op jit(solution)/shard_map/ppermute | solution.py:37
  145.1 5.3 %collective-permute-start.25 = (bf16[512,512]{1,0:T(8,128)(2,1)S(1)}, bf16[512,512]{1,0:T(8,128)(2,1)S(1)}, u32[]{:S(2)}, u32[]{:S(2)}) collective-permute-start(bf16[512,512]{1,0:T(8,128)(2,1)S(1)} %bitcast.88), channel_id=1, source_target_pairs={{0,1},{1,0},{2,3},{3,2},{4,5},{5,4},{6,7},{7,6},{8,9},{9,8},{10,11... | collective-permute-start | bytes 1572872 | tf_op jit(solution)/shard_map/ppermute | solution.py:41
  145.1 7.1 %collective-permute-start.26 = (bf16[512,512]{1,0:T(8,128)(2,1)S(1)}, bf16[512,512]{1,0:T(8,128)(2,1)S(1)}, u32[]{:S(2)}, u32[]{:S(2)}) collective-permute-start(bf16[512,512]{1,0:T(8,128)(2,1)S(1)} %collective-permute-done.21.refs_1_), channel_id=1, source_target_pairs={{0,1},{1,0},{2,3},{3,2},{4,5},{5,4},{6,7},{7,6},{8,9},{9,8},{10,11... | collective-permute-start | bytes 1572872 | tf_op jit(solution)/shard_map/ppermute | solution.py:41
  149.5 2.7 %collective-permute-start.27 = (bf16[512,512]{1,0:T(8,128)(2,1)S(1)}, bf16[512,512]{1,0:T(8,128)(2,1)S(1)}, u32[]{:S(2)}, u32[]{:S(2)}) collective-permute-start(bf16[512,512]{1,0:T(8,128)(2,1)S(1)} %collective-permute-done.22.refs_2_), channel_id=1, source_target_pairs={{0,1},{1,0},{2,3},{3,2},{4,5},{5,4},{6,7},{7,6},{8,9},{9,8},{10,11... | collective-permute-start | bytes 1572872 | tf_op jit(solution)/shard_map/ppermute | solution.py:41
  149.5 2.3 collective-permute-start.28
  150.1 2.1 collective-permute-start.29
  152.2 13.4 %copy-start.30 = (s32[15]{0:T(128)S(1)}, s32[15]{0:T(128)}, u32[]{:S(2)}) copy-start(s32[15]{0:T(128)} %param.18) | copy-start | bytes 184
  152.2 13.4 %copy-start.21 = (s32[2048]{0:T(1024)S(1)}, s32[2048]{0:T(1024)}, u32[]{:S(2)}) copy-start(s32[2048]{0:T(1024)} %copy-done.20) | copy-start | bytes 24580
  152.2 17.9 %copy-start.25 = (f32[128]{0:T(128)S(1)}, f32[128]{0:T(128)}, u32[]{:S(2)}) copy-start(f32[128]{0:T(128)} %get-tuple-element.32) | copy-start | bytes 1540
  164.5 23.9 %copy-start.1 = (bf16[4,512,512]{2,1,0:T(8,128)(2,1)}, bf16[4,512,512]{2,1,0:T(8,128)(2,1)S(1)}, u32[]{:S(2)}) copy-start(bf16[4,512,512]{2,1,0:T(8,128)(2,1)S(1)} %get-tuple-element.24.mine_ref) | copy-start | bytes 6291460
  164.5 23.9 %collective-permute-start.30 = (bf16[4,512,512]{2,1,0:T(8,128)(2,1)S(1)}, bf16[4,512,512]{2,1,0:T(8,128)(2,1)S(1)}, u32[]{:S(2)}, u32[]{:S(2)}) collective-permute-start(bf16[4,512,512]{2,1,0:T(8,128)(2,1)S(1)} %get-tuple-element.25), channel_id=1, source_target_pairs={{0,1},{1,0},{2,3},{3,2},{4,5},{5,4},{6,7},{7,6},{8,9},{9,8},{10,11... | collective-permute-start | bytes 6291464 | tf_op jit(solution)/shard_map/ppermute | solution.py:41
  166.9 18.0 %collective-permute-start.17 = (bf16[512,512]{1,0:T(8,128)(2,1)S(1)}, bf16[512,512]{1,0:T(8,128)(2,1)S(1)}, u32[]{:S(2)}, u32[]{:S(2)}) collective-permute-start(bf16[512,512]{1,0:T(8,128)(2,1)S(1)} %get-tuple-element.20.refs_10_), channel_id=1, source_target_pairs={{0,2},{1,3},{2,4},{3,5},{4,6},{5,7},{6,0},{7,1},{8,10},{9,11},{10,... | collective-permute-start | bytes 1572872 | tf_op jit(solution)/shard_map/ppermute | solution.py:37
  166.9 18.0 %collective-permute-start.18 = (bf16[512,512]{1,0:T(8,128)(2,1)S(1)}, bf16[512,512]{1,0:T(8,128)(2,1)S(1)}, u32[]{:S(2)}, u32[]{:S(2)}) collective-permute-start(bf16[512,512]{1,0:T(8,128)(2,1)S(1)} %get-tuple-element.21.refs_11_), channel_id=1, source_target_pairs={{0,6},{1,7},{2,0},{3,1},{4,2},{5,3},{6,4},{7,5},{8,14},{9,15},{10,... | collective-permute-start | bytes 1572872 | tf_op jit(solution)/shard_map/ppermute | solution.py:37
  170.2 1.2 collective-permute-start.4
  171.5 9.8 %collective-permute-start.5 = (f32[128,16]{0,1:T(8,128)S(1)}, f32[128,16]{0,1:T(8,128)S(1)}, u32[]{:S(2)}, u32[]{:S(2)}) collective-permute-start(f32[128,16]{0,1:T(8,128)S(1)} %fusion.111), channel_id=1, source_target_pairs={{0,2},{1,3},{2,0},{3,1},{4,6},{5,7},{6,4},{7,5},{8,10},{9,11},{10,... | collective-permute-start | bytes 24584 | tf_op jit(solution)/shard_map/ppermute | solution.py:365
  181.3 16.1 %collective-permute-start.6 = (f32[128,16]{0,1:T(8,128)S(1)}, f32[128,16]{0,1:T(8,128)S(1)}, u32[]{:S(2)}, u32[]{:S(2)}) collective-permute-start(f32[128,16]{0,1:T(8,128)S(1)} %add.190), channel_id=1, source_target_pairs={{0,4},{1,5},{2,6},{3,7},{4,0},{5,1},{6,2},{7,3},{8,12},{9,13},{10,... | collective-permute-start | bytes 24584 | tf_op jit(solution)/shard_map/ppermute | solution.py:366
  185.1 12.4 %collective-permute-start.19 = (bf16[256,512]{1,0:T(8,128)(2,1)S(1)}, bf16[256,512]{1,0:T(8,128)(2,1)S(1)}, u32[]{:S(2)}, u32[]{:S(2)}) collective-permute-start(bf16[256,512]{1,0:T(8,128)(2,1)S(1)} %get-tuple-element.22), channel_id=1, source_target_pairs={{0,2},{1,3},{2,4},{3,5},{4,6},{5,7},{6,0},{7,1},{8,10},{9,11},{10,... | collective-permute-start | bytes 786440 | tf_op jit(solution)/shard_map/ppermute | solution.py:37
  185.2 12.3 %collective-permute-start.20 = (bf16[256,512]{1,0:T(8,128)(2,1)S(1)}, bf16[256,512]{1,0:T(8,128)(2,1)S(1)}, u32[]{:S(2)}, u32[]{:S(2)}) collective-permute-start(bf16[256,512]{1,0:T(8,128)(2,1)S(1)} %get-tuple-element.23), channel_id=1, source_target_pairs={{0,6},{1,7},{2,0},{3,1},{4,2},{5,3},{6,4},{7,5},{8,14},{9,15},{10,... | collective-permute-start | bytes 786440 | tf_op jit(solution)/shard_map/ppermute | solution.py:37
  190.0 14.8 %collective-permute-start.31 = (bf16[512,512]{1,0:T(8,128)(2,1)}, bf16[512,512]{1,0:T(8,128)(2,1)}, u32[]{:S(2)}, u32[]{:S(2)}) collective-permute-start(bf16[512,512]{1,0:T(8,128)(2,1)} %get-tuple-element.26), channel_id=1, source_target_pairs={{0,2},{1,3},{2,4},{3,5},{4,6},{5,7},{6,0},{7,1},{8,10},{9,11},{10,... | collective-permute-start | bytes 1572872 | tf_op jit(solution)/shard_map/ppermute | solution.py:37
  190.0 14.8 %collective-permute-start.32 = (bf16[512,512]{1,0:T(8,128)(2,1)}, bf16[512,512]{1,0:T(8,128)(2,1)}, u32[]{:S(2)}, u32[]{:S(2)}) collective-permute-start(bf16[512,512]{1,0:T(8,128)(2,1)} %get-tuple-element.27), channel_id=1, source_target_pairs={{0,6},{1,7},{2,0},{3,1},{4,2},{5,3},{6,4},{7,5},{8,14},{9,15},{10,... | collective-permute-start | bytes 1572872 | tf_op jit(solution)/shard_map/ppermute | solution.py:37
  198.5 27.0 %all-to-all-start.2 = ((bf16[16,32,512]{2,1,0:T(8,128)(2,1)}), bf16[16,32,512]{2,1,0:T(8,128)(2,1)}, u32[]{:S(2)}, u32[]{:S(2)}) async-start(bf16[16,32,512]{2,1,0:T(8,128)(2,1)} %bitcast.17), calls=%async_computation.2 | async-start | bytes 1048576 | tf_op jit(solution)/shard_map/all_to_all | solution.py:388
  202.8 10.6 %copy-start.23 = (s32[128,2]{0,1:T(2,128)S(1)}, s32[128,2]{0,1:T(2,128)}, u32[]{:S(2)}) copy-start(s32[128,2]{0,1:T(2,128)} %param.17) | copy-start | bytes 3076
  210.2 8.2 %collective-permute-start.33 = (bf16[256,512]{1,0:T(8,128)(2,1)}, bf16[256,512]{1,0:T(8,128)(2,1)S(1)}, u32[]{:S(2)}, u32[]{:S(2)}) collective-permute-start(bf16[256,512]{1,0:T(8,128)(2,1)} %get-tuple-element.28), channel_id=1, source_target_pairs={{0,2},{1,3},{2,4},{3,5},{4,6},{5,7},{6,0},{7,1},{8,10},{9,11},{10,... | collective-permute-start | bytes 786440 | tf_op jit(solution)/shard_map/ppermute | solution.py:37
  210.2 8.2 %collective-permute-start.34 = (bf16[256,512]{1,0:T(8,128)(2,1)}, bf16[256,512]{1,0:T(8,128)(2,1)S(1)}, u32[]{:S(2)}, u32[]{:S(2)}) collective-permute-start(bf16[256,512]{1,0:T(8,128)(2,1)} %get-tuple-element.29), channel_id=1, source_target_pairs={{0,6},{1,7},{2,0},{3,1},{4,2},{5,3},{6,4},{7,5},{8,14},{9,15},{10,... | collective-permute-start | bytes 786440 | tf_op jit(solution)/shard_map/ppermute | solution.py:37
  213.4 18.0 %copy-start.24 = (s32[128,2]{0,1:T(2,128)S(1)}, s32[128,2]{0,1:T(2,128)}, u32[]{:S(2)}) copy-start(s32[128,2]{0,1:T(2,128)} %param.17) | copy-start | bytes 3076
  225.5 14.7 %all-to-all-start.4 = ((bf16[16,32,512]{2,1,0:T(8,128)(2,1)}), bf16[16,32,512]{2,1,0:T(8,128)(2,1)S(1)}, u32[]{:S(2)}, u32[]{:S(2)}) async-start(bf16[16,32,512]{2,1,0:T(8,128)(2,1)} %bitcast.90), calls=%async_computation.4 | async-start | bytes 1048576 | tf_op jit(solution)/shard_map/all_to_all | solution.py:388
  (21 other events, 43.2 us)

commit v3 on v2

--- a/solution.py
+++ b/solution.py
@@ -102,24 +102,27 @@
     )(ids, first, q, start, kv, w_out)
 
 
-def ffn_kernel(ids, gain_ref, wg_hbm, wu_hbm, wd_hbm, *refs):
-    pieces = refs[:10]
-    mine_ref, sib_ref = refs[-8:-6]
-    xs_ref, act_ref, wg_ref, wu_ref, wd_ref, sems = refs[-6:]
+def ffn_kernel(ids, gain_ref, *refs):
+    weights = refs[:6]
+    pieces = refs[6:11]
+    outs = refs[-10:-6]
+    xs_ref, act_ref, gate_ref, up_ref, down_ref, sems = refs[-6:]
+    held = [gate_ref.at[0], up_ref.at[0], gate_ref.at[1], up_ref.at[1]]
+    held += [down_ref.at[0], down_ref.at[1]]
     copies = [
         pltpu.make_async_copy(hbm, ref, sems.at[i])
-        for i, (hbm, ref) in enumerate(((wg_hbm, wg_ref), (wu_hbm, wu_ref), (wd_hbm, wd_ref)))
+        for i, (hbm, ref) in enumerate(zip(weights, held, strict=True))
     ]
     for copy in copies:
         copy.start()
     rows, share = pieces[0].shape
     half = rows // 2
-    width = wg_ref.shape[0]
+    width = gate_ref.shape[1]
     tile = 32
 
     for side in range(2):
-        chosen = [(pieces[5 * s + k], 0, 4 * s + k) for s in range(2) for k in range(3)]
-        chosen += [(pieces[5 * s + 3 + side], side * half, 4 * s + 3) for s in range(2)]
+        chosen = [(pieces[k], 0, k) for k in range(3)]
+        chosen += [(pieces[3 + side], side * half, 3)]
 
         def norm(i, carry):
             at_row = pl.multiple_of(side * half + i * tile, tile)
@@ -138,55 +141,47 @@
             return carry
 
         lax.fori_loop(0, half // tile, norm, 0)
-    copies[0].wait()
-    copies[1].wait()
-
-    def hidden(i, carry):
-        at_row = pl.ds(pl.multiple_of(i * half, half), half)
-        v = xs_ref[at_row, :]
-        gate = jnp.dot(v, wg_ref[...], preferred_element_type=F32)
-        up = jnp.dot(v, wu_ref[...], preferred_element_type=F32)
-        act_ref[at_row, :] = (gate / (1.0 + jnp.exp(-gate)) * up).astype(BF16)
-        return carry
-
-    lax.fori_loop(0, 2, hidden, 0)
-    copies[2].wait()
-
-    def body(i, carry):
-        block = i // 2
-        at_row = pl.ds(pl.multiple_of((i - block * 2) * half, half), half)
-        for ref, base in ((sib_ref, 16), (mine_ref, 8)):
-            w = wd_ref[:, pl.ds(pl.multiple_of(ids[base + i] * share, share), share)]
-            out = jnp.dot(act_ref[at_row, :], w, preferred_element_type=F32)
-            ref[block, at_row, :] = out.astype(BF16)
-        return carry
-
-    lax.fori_loop(0, 8, body, 0)
-
-
-def ffn(ids, gain, w_gate, w_up, w_down, pieces, after):
+    for k in range(2):
+        copies[2 * k].wait()
+        gate = jnp.dot(xs_ref[...], gate_ref[k], preferred_element_type=F32)
+        copies[2 * k + 1].wait()
+        up = jnp.dot(xs_ref[...], up_ref[k], preferred_element_type=F32)
+        act_ref[k] = (gate / (1.0 + jnp.exp(-gate)) * up).astype(BF16)
+    copies[4].wait()
+    copies[5].wait()
+    for k, ref in enumerate(outs):
+
+        def body(i, carry):
+            at_row = pl.ds(pl.multiple_of(i * half, half), half)
+            column = pl.ds(pl.multiple_of(ids[4 + 2 * k + i] * share, share), share)
+            total = jnp.dot(act_ref[0, at_row, :], down_ref[0, :, column], preferred_element_type=F32)
+            total = total + jnp.dot(
+                act_ref[1, at_row, :], down_ref[1, :, column], preferred_element_type=F32
+            )
+            ref[at_row, :] = total.astype(BF16)
+            return carry
+
+        lax.fori_loop(0, 2, body, 0)
+
+
+def ffn(ids, gain, weights, pieces):
     rows, share = pieces[0].shape
+    depth, width = weights[0].shape
     return pl.pallas_call(
         ffn_kernel,
-        out_shape=(
-            jax.ShapeDtypeStruct((NZ, rows, share), BF16),
-            jax.ShapeDtypeStruct((NZ, rows, share), BF16),
-        ),
-        in_specs=[SMEM_SPEC, VMEM_SPEC]
-        + [HBM_SPEC] * 3
-        + [VMEM_SPEC] * len(pieces)
-        + [ANY_SPEC] * len(after),
-        out_specs=(VMEM_SPEC,) * 2,
+        out_shape=(jax.ShapeDtypeStruct((rows, share), BF16),) * 4,
+        in_specs=[SMEM_SPEC, VMEM_SPEC] + [HBM_SPEC] * 6 + [VMEM_SPEC] * len(pieces),
+        out_specs=(VMEM_SPEC,) * 4,
         scratch_shapes=[
-            pltpu.VMEM((rows, w_gate.shape[0]), BF16),
-            pltpu.VMEM((rows, w_gate.shape[1]), BF16),
-            pltpu.VMEM(w_gate.shape, BF16),
-            pltpu.VMEM(w_up.shape, BF16),
-            pltpu.VMEM(w_down.shape, BF16),
-            pltpu.SemaphoreType.DMA((3,)),
+            pltpu.VMEM((rows, depth), BF16),
+            pltpu.VMEM((2, rows, width), BF16),
+            pltpu.VMEM((2, depth, width), BF16),
+            pltpu.VMEM((2, depth, width), BF16),
+            pltpu.VMEM((2, width, depth), BF16),
+            pltpu.SemaphoreType.DMA((6,)),
         ],
-        compiler_params=pltpu.CompilerParams(vmem_limit_bytes=36 * MIB),
-    )(ids, gain, w_gate, w_up, w_down, *pieces, *after)
+        compiler_params=pltpu.CompilerParams(vmem_limit_bytes=40 * MIB),
+    )(ids, gain, *weights, *pieces)
 
 
 def gather_ring(own):
@@ -195,65 +190,46 @@
     above = send_z(own, -1)
     far_a = send_z(below[:half], 1)
     far_b = send_z(above[half:], -1)
-    own_s = send_core(own)
-    near_s = [send_core(below), send_core(above)]
-    far_s = [send_core(far_a), send_core(far_b)]
-    return [own, below, above, far_a, far_b, own_s] + near_s + far_s
-
-
-def mix_kernel(mine_ref, got_ref, up_ref, down_ref):
-    for k, ref in enumerate((up_ref, down_ref)):
-        ref[...] = (mine_ref[k].astype(F32) + got_ref[k].astype(F32)).astype(BF16)
-
-
-def relay_kernel(mine_ref, got_ref, below_ref, above_ref, low_ref, high_ref):
-    total = mine_ref[0].astype(F32) + got_ref[0].astype(F32)
+    return [own, below, above, far_a, far_b]
+
+
+def relay_kernel(relay_ref, below_ref, above_ref, low_ref, high_ref):
     half = low_ref.shape[0]
-    low_ref[...] = (total[:half] + below_ref[:half, :].astype(F32)).astype(BF16)
-    high_ref[...] = (total[half:] + above_ref[half:, :].astype(F32)).astype(BF16)
-
-
-def end_kernel(mine_ref, got_ref, below_ref, above_ref, low_ref, high_ref, out_ref):
-    total = mine_ref[0].astype(F32) + got_ref[0].astype(F32)
+    low = relay_ref[:half, :].astype(F32) + below_ref[:half, :].astype(F32)
+    high = relay_ref[half:, :].astype(F32) + above_ref[half:, :].astype(F32)
+    low_ref[...] = low.astype(BF16)
+    high_ref[...] = high.astype(BF16)
+
+
+def end_kernel(rest_ref, below_ref, above_ref, low_ref, high_ref, out_ref):
     half = low_ref.shape[0]
+    total = rest_ref[...].astype(F32)
     first = total[:half] + above_ref[:half, :].astype(F32) + low_ref[...].astype(F32)
     second = total[half:] + below_ref[half:, :].astype(F32) + high_ref[...].astype(F32)
     out_ref[:half, :] = first.astype(BF16)
     out_ref[half:, :] = second.astype(BF16)
 
 
-def combine_blocks(kernel, pair, count, index, more, outs):
-    _, rows, share = pair[0].shape
-    block = pl.BlockSpec((count, rows, share), lambda i: (index, 0, 0))
-
-    def whole(height):
-        return pl.BlockSpec((height, share), lambda i: (0, 0))
-
+def local_call(kernel, args, heights):
+    share = args[0].shape[1]
     return pl.pallas_call(
         kernel,
-        grid=(1,),
-        out_shape=tuple(jax.ShapeDtypeStruct((height, share), BF16) for height in outs),
-        in_specs=[block, block] + [whole(v.shape[0]) for v in more],
-        out_specs=tuple(whole(height) for height in outs),
+        out_shape=tuple(jax.ShapeDtypeStruct((height, share), BF16) for height in heights),
+        in_specs=[VMEM_SPEC] * len(args),
+        out_specs=(VMEM_SPEC,) * len(heights),
         compiler_params=pltpu.CompilerParams(vmem_limit_bytes=16 * MIB),
-    )(*pair, *more)
-
-
-def scatter_start(mine, sib):
-    rows = mine.shape[1]
-    got = send_core(sib)
-    return *combine_blocks(mix_kernel, (mine, got), 2, 0, (), (rows, rows)), mine, got
-
-
-def scatter_end(up, down, mine, got):
+    )(*args)
+
+
+def scatter_ring(up, down, relay, rest):
     rows = up.shape[0]
     half = rows // 2
     from_below = send_z(up, 1)
     from_above = send_z(down, -1)
-    moved = (from_below, from_above)
-    low, high = combine_blocks(relay_kernel, (mine, got), 1, 2, moved, (half, half))
-    last = (send_z(low, 1), send_z(high, -1))
-    return combine_blocks(end_kernel, (mine, got), 1, 3, moved + last, (rows,))[0]
+    low, high = local_call(relay_kernel, (relay, from_below, from_above), (half, half))
+    low = send_z(low, 1)
+    high = send_z(high, -1)
+    return local_call(end_kernel, (rest, from_below, from_above, low, high), (rows,))[0]
 
 
 def local(
@@ -316,6 +292,12 @@
         jnp.broadcast_to(kv_own[None], (seq_count,) + kv_own.shape), "seq", 0, 0, tiled=True
     ).reshape(total, kv_own.shape[1])
 
+    g_sib, u_sib, d_sib = (send_core(w) for w in (w_gate, w_up, w_down))
+    g_sib, u_sib, d_sib = (
+        pltpu.with_memory_space_constraint(w, pltpu.HBM) for w in (g_sib, u_sib, d_sib)
+    )
+    weights = [w_gate, w_up, g_sib, u_sib, w_down, d_sib]
+
     ring = lax.rem(z + jnp.arange(NZ, dtype=jnp.int32), NZ) * 2
     other_c = 1 - c
     out_ids = jnp.concatenate([ring + c, ring + other_c])
@@ -330,8 +312,14 @@
     own_tokens = lax.dynamic_slice_in_dim(tokens, ten_rank * share, share, 1)
     residual = (own_tokens.astype(F32) + attn_sum).astype(BF16)
 
-    capacity = rows // 2
-    slots = capacity // 2
+    sibling = send_core(residual)
+    wide = jnp.where(
+        c == 0,
+        jnp.concatenate([residual, sibling], axis=1),
+        jnp.concatenate([sibling, residual], axis=1),
+    )
+
+    slots = rows // 8
     holders = seq_count // EXPERTS
     expert_ids = jnp.arange(EXPERTS, dtype=jnp.int32)
     hit = (routes[:, 0:1] == expert_ids[None, :]) | (routes[:, 1:2] == expert_ids[None, :])
@@ -341,27 +329,30 @@
     slot_of = jnp.where(hit, rank, -1)
     slot_dup = jnp.repeat(slot_of.T, holders, axis=0)
 
-    def pack(low):
-        want = low + jnp.arange(slots, dtype=jnp.int32)
+    def pack(chunk):
+        want = (2 * c + chunk) * slots + jnp.arange(slots, dtype=jnp.int32)
         return slot_dup[:, None, :] == want[None, :, None]
 
-    picks = [pack(0), pack(slots)]
+    picks = [pack(0), pack(1)]
+
+    def exchange(flat):
+        got = lax.all_to_all(
+            flat.reshape(seq_count, slots, 2 * share), "seq", 0, 0, tiled=True
+        )
+        return got.reshape(seq_count * slots, 2 * share)
 
     def dispatch(pick):
         flat = pick.reshape(seq_count * slots, rows).astype(BF16)
-        out = jnp.dot(flat, residual, preferred_element_type=F32).astype(BF16)
-        got = lax.all_to_all(out.reshape(seq_count, slots, share), "seq", 0, 0, tiled=True)
-        return got.reshape(seq_count * slots, share)
-
-    gain_share = lax.dynamic_slice_in_dim(gain_moe, ten_rank * share, share)
-    router = lax.dynamic_slice_in_dim(w_router, ten_rank * share, share)
-    res32 = residual.astype(F32)
+        return exchange(jnp.dot(flat, wide, preferred_element_type=F32).astype(BF16))
+
+    gain_wide = lax.dynamic_slice_in_dim(gain_moe, z * 2 * share, 2 * share)
+    router = lax.dynamic_slice_in_dim(w_router, z * 2 * share, 2 * share)
+    wide32 = wide.astype(F32)
     part = jnp.dot(
-        res32 * gain_share, router, preferred_element_type=F32, precision=lax.Precision.HIGHEST
-    )
-    square = jnp.sum(res32 * res32, axis=1, keepdims=True)
+        wide32 * gain_wide, router, preferred_element_type=F32, precision=lax.Precision.HIGHEST
+    )
+    square = jnp.sum(wide32 * wide32, axis=1, keepdims=True)
     stats = jnp.concatenate([part, square, jnp.zeros((rows, 7), F32)], axis=1)
-    stats = stats + send_core(stats)
     stats = stats + lax.ppermute(stats, "tensor", [(t, t ^ 2) for t in range(ten_count)])
     stats = stats + lax.ppermute(stats, "tensor", [(t, t ^ 4) for t in range(ten_count)])
     logits = stats[:, :EXPERTS] * lax.rsqrt(stats[:, EXPERTS : EXPERTS + 1] / width + EPS)
@@ -371,27 +362,19 @@
     gate_of = jnp.sum(jnp.where(picked, gates[:, :, None], 0.0), axis=1)
     gate_dup = jnp.repeat(gate_of, holders, axis=1)
 
-    gain_rows = gain_moe.reshape(ten_count, share)
-    source = lax.rem(z + jnp.array([0, 3, 1, 2], jnp.int32), NZ) * 2
-    target = lax.rem(z + jnp.array([2, 1, 3, 2, 1, 3, 0, 0], jnp.int32), NZ) * 2
-    ids = jnp.concatenate([source + c, source + other_c, target + c, target + other_c])
+    gain_rows = gain_moe.reshape(NZ, 2 * share)
+    hops = jnp.array([0, 3, 1, 2, 2, 1, 3, 2, 1, 3, 0, 0], jnp.int32)
+    ids = lax.rem(z + hops, NZ)
     a_own = dispatch(picks[0])
     a_pieces = gather_ring(a_own)
     b_own = dispatch(picks[1])
     b_pieces = gather_ring(b_own)
-    a_out = ffn(ids, gain_rows, w_gate, w_up, w_down, a_pieces, [])
-    a_start = scatter_start(*a_out)
-    b_out = ffn(ids, gain_rows, w_gate, w_up, w_down, b_pieces, a_start[:2])
-    b_start = scatter_start(*b_out)
-
-    def give_back(parts):
-        got = lax.all_to_all(parts.reshape(seq_count, slots, share), "seq", 0, 0, tiled=True)
-        return got.reshape(seq_count * slots, share)
-
-    a_final = scatter_end(*a_start)
-    b_final = scatter_end(*b_start)
-    a_back = give_back(a_final)
-    b_back = give_back(b_final)
+    a_out = ffn(ids, gain_rows, weights, a_pieces)
+    b_out = ffn(ids, gain_rows, weights, b_pieces)
+    a_final = scatter_ring(*a_out)
+    b_final = scatter_ring(*b_out)
+    a_back = exchange(a_final)
+    b_back = exchange(b_final)
 
     def combine(pick, back):
         weight = jnp.where(pick.transpose(2, 0, 1), gate_dup[:, :, None], 0.0)
@@ -403,7 +386,10 @@
         )
 
     mixture = combine(picks[0], a_back) + combine(picks[1], b_back)
-    layer_out = (res32 + mixture).astype(BF16)
+    left, right = mixture[:, :share], mixture[:, share:]
+    theirs = send_core(jnp.where(c == 0, right, left).astype(BF16))
+    mine = jnp.where(c == 0, left, right)
+    layer_out = (residual.astype(F32) + mine + theirs.astype(F32)).astype(BF16)
 
     owner_ext = jnp.concatenate([owners, jnp.full((1,), -1, jnp.int32)])
     label_ids = jnp.arange(short_count + 2, dtype=jnp.int32)

time: 245 us -> 207 us (0.84)
  the two profiles are of different devices: /device:TPU:0 before, /device:TPU:33 now
where the time goes in v3:
time: 207 us; the launch traced here: 204 us
  starting transfers between devices  66.2 us (32%)
  waiting for transfers between devices  43.7 us (21%)
  Pallas kernels  36.9 us (18%)
  matrix products  19.1 us (9%)
  blocking collectives  14.3 us (7%)
  local copies, waits for them, and re-layouts  12.5 us (6%)
  other arithmetic  10.1 us (5%)
    pallas_call x2, Pallas kernels, ffn(): pl.pallas_call(ffn_kernel, out_shape=(jax.ShapeDtypeStruct((rows, share),...  26.8 us
    ppermute x19, starting transfers between devices, send_z(): return lax.ppermute(value, 'tensor', z_perm(step))  22.5 us
    ppermute x19, waiting for transfers between devices, send_z(): return lax.ppermute(value, 'tensor', z_perm(step))  19.1 us
    ppermute x6, starting transfers between devices, send_core(): return lax.ppermute(value, 'tensor', core_perm())  18.7 us
    all_to_all x3, starting transfers between devices, exchange(): lax.all_to_all(flat.reshape(seq_count, slots, 2 * share), 'seq', 0, 0, ti...  14.9 us
    all_to_all x1, blocking collectives, exchange(): lax.all_to_all(flat.reshape(seq_count, slots, 2 * share), 'seq', 0, 0, ti...  14.3 us
    all_to_all x1, waiting for transfers between devices, local(): lax.all_to_all(jnp.broadcast_to(kv_own[None], (seq_count,) + kv_own.shape...  10.5 us
    pallas_call x1, Pallas kernels, attend(): pl.pallas_call(attention_kernel, out_shape=(jax.ShapeDtypeStruct((NZ, row...  7.09 us
  transfers between devices with their start and end apart: 31, of which 13 were waited for; matrix products, arithmetic and copies ran while one was open for 13% of the time, Pallas kernels for 18%

profile of v3, /device:TPU:33, one launch (start us, length us, event | category | flops | bytes accessed | tf_op | source)
XLA Modules:
  0.0 204.0 jit_solution(12618037305134652061)
XLA Ops:
  0.7 1.7 fusion.3
  3.4 1.7 fusion.15
  6.6 6.8 %all-to-all-start = ((bf16[16,128,256]{2,1,0:T(8,128)(2,1)}), bf16[16,128,256]{2,1,0:T(8,128)(2,1)S(1)}, u32[]{:S(2)}, u32[]{:S(2)}) async-start(bf16[16,128,256]{2,1,0:T(8,128)(2,1)} %broadcast_in_dim.110), calls=%async_computation | async-start | bytes 2097152 | tf_op jit(solution)/shard_map/all_to_all | solution.py:291
  15.2 3.3 %fusion.17 = f32[128,512]{1,0:T(8,128)S(1)} fusion(bf16[4096,512]{1,0:T(8,128)(2,1)} %param.19, bf16[128,4096]{1,0:T(8,128)(2,1)} %param.14, f32[4096]{0:T(1024)S(1)} %copy-done.16, f32[128]{0:T(128)S(1)} %add_rsqrt_fusion), kind=kOutput, calls=%fused_computation.31 | convolution fusion | flops 538968064 | bytes 5521920 | tf_op jit(solution)/shard_map/dot_general | solution.py:282
  18.9 10.5 %all-to-all-done = bf16[16,128,256]{2,1,0:T(8,128)(2,1)S(1)} async-done(((bf16[16,128,256]{2,1,0:T(8,128)(2,1)}), bf16[16,128,256]{2,1,0:T(8,128)(2,1)S(1)}, u32[]{:S(2)}, u32[]{:S(2)}) %all-to-all-start) | async-done | bytes 1048608 | tf_op jit(solution)/shard_map/all_to_all | solution.py:291
  29.4 7.1 %shard_map.149 = (f32[4,128,512]{2,1,0:T(8,128)S(1)}, bf16[4,128,512]{2,1,0:T(8,128)(2,1)}) custom-call(s32[8]{0:T(128)S(1)} %pad_add_fusion.ids, s32[1]{0:T(128)} %bitcast.first_ref, bf16[512,128]{1,0:T(8,128)(2,1)S(1)} %maximum_maximum_fusion.q_ref, s32[128,1]{1,0:T(8,128)S(1)} %copy.19.start_ref, bf16[2048,256]{1,0:T(8,128)(2,1)S(1)} %bitcast.73, ...), custom_call_target="tpu_custom_call" | custom-call | tf_op jit(solution)/shard_map/pallas_call | solution.py:92
  37.5 2.6 %collective-permute-start = (bf16[4,128,512]{2,1,0:T(8,128)(2,1)}, bf16[4,128,512]{2,1,0:T(8,128)(2,1)}, u32[]{:S(2)}, u32[]{:S(2)}) collective-permute-start(bf16[4,128,512]{2,1,0:T(8,128)(2,1)} %get-tuple-element.17), channel_id=1, source_target_pairs={{0,1},{1,0},{2,3},{3,2},{4,5},{5,4},{6,7},{7,6},{8,9},{9,8},{10,11... | collective-permute-start | bytes 1572872 | tf_op jit(solution)/shard_map/ppermute | solution.py:41
  40.1 1.9 collective-permute-done
  42.0 1.4 fusion.26
  43.3 2.8 %collective-permute-start.3 = (bf16[128,512]{1,0:T(8,128)(2,1)S(1)}, bf16[128,512]{1,0:T(8,128)(2,1)}, u32[]{:S(2)}, u32[]{:S(2)}) collective-permute-start(bf16[128,512]{1,0:T(8,128)(2,1)S(1)} %get-tuple-element.33), channel_id=1, source_target_pairs={{0,4},{1,5},{2,6},{3,7},{4,0},{5,1},{6,2},{7,3},{8,12},{9,13},{10,... | collective-permute-start | bytes 393224 | tf_op jit(solution)/shard_map/ppermute | solution.py:37
  49.7 1.6 collective-permute-start.1
  52.1 1.3 collective-permute-done.2
  55.1 2.2 %collective-permute-start.4 = (bf16[128,512]{1,0:T(8,128)(2,1)S(1)}, bf16[128,512]{1,0:T(8,128)(2,1)S(1)}, u32[]{:S(2)}, u32[]{:S(2)}) collective-permute-start(bf16[128,512]{1,0:T(8,128)(2,1)S(1)} %fusion.22), channel_id=1, source_target_pairs={{0,1},{1,0},{2,3},{3,2},{4,5},{5,4},{6,7},{7,6},{8,9},{9,8},{10,11... | collective-permute-start | bytes 393224 | tf_op jit(solution)/shard_map/ppermute | solution.py:41
  58.6 14.3 %all_to_all.25 = bf16[16,16,1024]{2,1,0:T(8,128)(2,1)} all-to-all(bf16[16,16,1024]{2,1,0:T(8,128)(2,1)S(1)} %bitcast.78), channel_id=1, replica_groups=mesh['seq'=16,'tensor'=8] {'seq'}, dimensions={0} | all-to-all | bytes 1048576 | tf_op jit(solution)/shard_map/all_to_all | solution.py:339
  72.9 1.7 collective-permute-start.18
  75.9 4.2 %all-to-all-start.1 = ((bf16[16,16,1024]{2,1,0:T(8,128)(2,1)}), bf16[16,16,1024]{2,1,0:T(8,128)(2,1)}, u32[]{:S(2)}, u32[]{:S(2)}) async-start(bf16[16,16,1024]{2,1,0:T(8,128)(2,1)} %bitcast.77), calls=%async_computation.1 | async-start | bytes 1048576 | tf_op jit(solution)/shard_map/all_to_all | solution.py:339
  80.3 5.6 %collective-permute-done.18.refs_7_ = bf16[256,1024]{1,0:T(8,128)(2,1)} collective-permute-done((bf16[256,1024]{1,0:T(8,128)(2,1)}, bf16[256,1024]{1,0:T(8,128)(2,1)}, u32[]{:S(2)}, u32[]{:S(2)}) %collective-permute-start.18) | collective-permute-done | bytes 524320 | tf_op jit(solution)/shard_map/ppermute | solution.py:37
  86.0 1.7 slice.151
  88.6 1.7 slice.152
  90.3 1.4 collective-permute-start.21
  92.0 1.3 fusion.14
  93.2 1.4 collective-permute-done.20.refs_9_
  94.6 1.4 collective-permute-done.21.refs_10_
  96.0 2.0 collective-permute-start.11
  98.0 1.6 fusion.13
  99.7 13.3 %shard_map.153 = (bf16[256,1024]{1,0:T(8,128)(2,1)S(1)}, bf16[256,1024]{1,0:T(8,128)(2,1)S(1)}, bf16[256,1024]{1,0:T(8,128)(2,1)S(1)}, bf16[256,1024]{1,0:T(8,128)(2,1)S(1)}) custom-call(s32[12]{0:T(128)S(1)} %compare_select_fusion.1.ids, f32[4,1024]{1,0:T(4,128)S(1)} %reshape.171.gain_ref, bf16[4096,512]{1,0:T(8,128)(2,1)} %refs_0_.3, ...), custom_call_target="tpu_custom_call" | custom-call | tf_op jit(solution)/shard_map/pallas_call | solution.py:170
  113.3 3.0 %collective-permute-start.23 = (bf16[256,1024]{1,0:T(8,128)(2,1)S(1)}, bf16[256,1024]{1,0:T(8,128)(2,1)S(1)}, u32[]{:S(2)}, u32[]{:S(2)}) collective-permute-start(bf16[256,1024]{1,0:T(8,128)(2,1)S(1)} %get-tuple-element.26), channel_id=1, source_target_pairs={{0,6},{1,7},{2,0},{3,1},{4,2},{5,3},{6,4},{7,5},{8,14},{9,15},{10,... | collective-permute-start | bytes 1572872 | tf_op jit(solution)/shard_map/ppermute | solution.py:37
  116.4 2.6 %collective-permute-start.5 = (f32[128,16]{0,1:T(8,128)S(1)}, f32[128,16]{0,1:T(8,128)S(1)}, u32[]{:S(2)}, u32[]{:S(2)}) collective-permute-start(f32[128,16]{0,1:T(8,128)S(1)} %maximum_maximum_fusion.1), channel_id=1, source_target_pairs={{0,2},{1,3},{2,0},{3,1},{4,6},{5,7},{6,4},{7,5},{8,10},{9,11},{10,... | collective-permute-start | bytes 24584 | tf_op jit(solution)/shard_map/ppermute | solution.py:356
  119.2 1.5 collective-permute-start.13
  120.8 3.9 %collective-permute-done.5 = f32[128,16]{0,1:T(8,128)S(1)} collective-permute-done((f32[128,16]{0,1:T(8,128)S(1)}, f32[128,16]{0,1:T(8,128)S(1)}, u32[]{:S(2)}, u32[]{:S(2)}) %collective-permute-start.5) | collective-permute-done | bytes 8224 | tf_op jit(solution)/shard_map/ppermute | solution.py:356
  125.7 1.8 collective-permute-start.24
  127.4 1.4 collective-permute-start.25
  129.0 2.7 %collective-permute-done.6 = f32[128,16]{0,1:T(8,128)S(1)} collective-permute-done((f32[128,16]{0,1:T(8,128)S(1)}, f32[128,16]{0,1:T(8,128)S(1)}, u32[]{:S(2)}, u32[]{:S(2)}) %collective-permute-start.6) | collective-permute-done | bytes 8224 | tf_op jit(solution)/shard_map/ppermute | solution.py:357
  131.7 13.5 %shard_map.150 = (bf16[256,1024]{1,0:T(8,128)(2,1)}, bf16[256,1024]{1,0:T(8,128)(2,1)}, bf16[256,1024]{1,0:T(8,128)(2,1)S(1)}, bf16[256,1024]{1,0:T(8,128)(2,1)S(1)}) custom-call(s32[12]{0:T(128)S(1)} %compare_select_fusion.1.ids, f32[4,1024]{1,0:T(4,128)S(1)} %reshape.171.gain_ref, bf16[4096,512]{1,0:T(8,128)(2,1)} %refs_0_.3, bf16[4096,512]{1,0:T(8,128)(2,1)} %refs_1_.3, ...), custom_call_target="tpu_custom_call" | custom-call | tf_op jit(solution)/shard_map/pallas_call | solution.py:170
  147.8 6.2 %all-to-all-start.4 = ((bf16[16,16,1024]{2,1,0:T(8,128)(2,1)}), bf16[16,16,1024]{2,1,0:T(8,128)(2,1)}, u32[]{:S(2)}, u32[]{:S(2)}) async-start(bf16[16,16,1024]{2,1,0:T(8,128)(2,1)} %bitcast.75), calls=%async_computation.4 | async-start | bytes 1048576 | tf_op jit(solution)/shard_map/all_to_all | solution.py:339
  155.9 1.3 shard_map.151
  157.3 1.5 collective-permute-start.16
  158.8 6.5 %collective-permute-done.16.low_ref = bf16[128,1024]{1,0:T(8,128)(2,1)S(1)} collective-permute-done((bf16[128,1024]{1,0:T(8,128)(2,1)S(1)}, bf16[128,1024]{1,0:T(8,128)(2,1)S(1)}, u32[]{:S(2)}, u32[]{:S(2)}) %collective-permute-start.16) | collective-permute-done | bytes 262176 | tf_op jit(solution)/shard_map/ppermute | solution.py:37
  165.4 1.6 collective-permute-done.17.high_ref
  168.0 1.4 shard_map.152
  170.2 4.4 %all-to-all-start.2 = ((bf16[16,16,1024]{2,1,0:T(8,128)(2,1)}), bf16[16,16,1024]{2,1,0:T(8,128)(2,1)}, u32[]{:S(2)}, u32[]{:S(2)}) async-start(bf16[16,16,1024]{2,1,0:T(8,128)(2,1)} %bitcast.76), calls=%async_computation.2 | async-start | bytes 1048576 | tf_op jit(solution)/shard_map/all_to_all | solution.py:339
  174.7 1.4 convolution_bitcast_fusion
  176.1 2.2 %fusion.8 = f32[128,1024]{1,0:T(8,128)} fusion(f32[128,1024]{1,0:T(8,128)S(1)} %convolution_bitcast_fusion, bf16[16,16,1024]{2,1,0:T(8,128)(2,1)} %all-to-all-done.4, f32[128,16]{0,1:T(8,128)S(1)} %bitcast.85, s32[128,16]{0,1:T(8,128)S(1)} %bitcast.81, s32[16]{0:T(128)S(1)} %copy-done.15), kind=kOutput, calls=%fused_computation.17 | convolution fusion | flops 67305472 | bytes 1589312 | tf_op jit(solution)/shard_map/dot_general | solution.py:384
  178.2 5.5 %all-to-all-done.2 = bf16[16,16,1024]{2,1,0:T(8,128)(2,1)} async-done(((bf16[16,16,1024]{2,1,0:T(8,128)(2,1)}), bf16[16,16,1024]{2,1,0:T(8,128)(2,1)}, u32[]{:S(2)}, u32[]{:S(2)}) %all-to-all-start.2) | async-done | bytes 524320 | tf_op jit(solution)/shard_map/all_to_all | solution.py:339
  183.7 1.4 convolution_bitcast_fusion.2
  185.1 1.5 fusion.7
  186.7 12.4 %collective-permute-start.26 = (bf16[128,512]{1,0:T(8,128)(2,1)S(1)}, bf16[128,512]{1,0:T(8,128)(2,1)S(1)}, u32[]{:S(2)}, u32[]{:S(2)}) collective-permute-start(bf16[128,512]{1,0:T(8,128)(2,1)S(1)} %select_convert_fusion), channel_id=1, source_target_pairs={{0,1},{1,0},{2,3},{3,2},{4,5},{5,4},{6,7},{7,6},{8,9},{9,8},{10,11... | collective-permute-start | bytes 393224 | tf_op jit(solution)/shard_map/ppermute | solution.py:41
  199.1 4.2 %fusion.2 = bf16[2048,256]{1,0:T(8,128)(2,1)} fusion(bf16[2048,256]{1,0:T(8,128)(2,1)S(1)} %bitcast.74, s32[2048]{0:T(1024)S(1)} %fusion.11), kind=kOutput, calls=%fused_computation.5 | convolution fusion | flops 2152202240 | bytes 2105344 | tf_op jit(solution)/shard_map/dot_general | solution.py:409
  (126 shorter events, 24.6 us)
Async XLA Ops:
  0.6 2.8 %copy-start = (bf16[4096,256]{1,0:T(8,128)(2,1)S(1)}, bf16[4096,256]{1,0:T(8,128)(2,1)}, u32[]{:S(2)}) copy-start(bf16[4096,256]{1,0:T(8,128)(2,1)} %param.20) | copy-start | bytes 6291460
  5.1 10.0 %copy-start.16 = (f32[4096]{0:T(1024)S(1)}, f32[4096]{0:T(1024)}, u32[]{:S(2)}) copy-start(f32[4096]{0:T(1024)} %param.18) | copy-start | bytes 49156
  6.6 22.8 %all-to-all-start = ((bf16[16,128,256]{2,1,0:T(8,128)(2,1)}), bf16[16,128,256]{2,1,0:T(8,128)(2,1)S(1)}, u32[]{:S(2)}, u32[]{:S(2)}) async-start(bf16[16,128,256]{2,1,0:T(8,128)(2,1)} %broadcast_in_dim.110), calls=%async_computation | async-start | bytes 2097152 | tf_op jit(solution)/shard_map/all_to_all | solution.py:291
  13.4 86.3 %collective-permute-start.7 = (bf16[4096,512]{1,0:T(8,128)(2,1)}, bf16[4096,512]{1,0:T(8,128)(2,1)}, u32[]{:S(2)}, u32[]{:S(2)}) collective-permute-start(bf16[4096,512]{1,0:T(8,128)(2,1)} %refs_0_.3), channel_id=1, source_target_pairs={{0,1},{1,0},{2,3},{3,2},{4,5},{5,4},{6,7},{7,6},{8,9},{9,8},{10,11... | collective-permute-start | bytes 12582920 | tf_op jit(solution)/shard_map/ppermute | solution.py:41
  14.4 85.3 %collective-permute-start.8 = (bf16[4096,512]{1,0:T(8,128)(2,1)}, bf16[4096,512]{1,0:T(8,128)(2,1)}, u32[]{:S(2)}, u32[]{:S(2)}) collective-permute-start(bf16[4096,512]{1,0:T(8,128)(2,1)} %refs_1_.3), channel_id=1, source_target_pairs={{0,1},{1,0},{2,3},{3,2},{4,5},{5,4},{6,7},{7,6},{8,9},{9,8},{10,11... | collective-permute-start | bytes 12582920 | tf_op jit(solution)/shard_map/ppermute | solution.py:41
  14.5 85.2 %collective-permute-start.9 = (bf16[512,4096]{1,0:T(8,128)(2,1)}, bf16[512,4096]{1,0:T(8,128)(2,1)}, u32[]{:S(2)}, u32[]{:S(2)}) collective-permute-start(bf16[512,4096]{1,0:T(8,128)(2,1)} %refs_4_.3), channel_id=1, source_target_pairs={{0,1},{1,0},{2,3},{3,2},{4,5},{5,4},{6,7},{7,6},{8,9},{9,8},{10,11... | collective-permute-start | bytes 12582920 | tf_op jit(solution)/shard_map/ppermute | solution.py:41
  36.5 1.0 copy-start.3
  37.5 4.5 %collective-permute-start = (bf16[4,128,512]{2,1,0:T(8,128)(2,1)}, bf16[4,128,512]{2,1,0:T(8,128)(2,1)}, u32[]{:S(2)}, u32[]{:S(2)}) collective-permute-start(bf16[4,128,512]{2,1,0:T(8,128)(2,1)} %get-tuple-element.17), channel_id=1, source_target_pairs={{0,1},{1,0},{2,3},{3,2},{4,5},{5,4},{6,7},{7,6},{8,9},{9,8},{10,11... | collective-permute-start | bytes 1572872 | tf_op jit(solution)/shard_map/ppermute | solution.py:41
  43.3 6.4 %collective-permute-start.3 = (bf16[128,512]{1,0:T(8,128)(2,1)S(1)}, bf16[128,512]{1,0:T(8,128)(2,1)}, u32[]{:S(2)}, u32[]{:S(2)}) collective-permute-start(bf16[128,512]{1,0:T(8,128)(2,1)S(1)} %get-tuple-element.33), channel_id=1, source_target_pairs={{0,4},{1,5},{2,6},{3,7},{4,0},{5,1},{6,2},{7,3},{8,12},{9,13},{10,... | collective-permute-start | bytes 393224 | tf_op jit(solution)/shard_map/ppermute | solution.py:37
  49.0 4.4 %collective-permute-start.2 = (bf16[128,512]{1,0:T(8,128)(2,1)S(1)}, bf16[128,512]{1,0:T(8,128)(2,1)S(1)}, u32[]{:S(2)}, u32[]{:S(2)}) collective-permute-start(bf16[128,512]{1,0:T(8,128)(2,1)S(1)} %get-tuple-element.34), channel_id=1, source_target_pairs={{0,6},{1,7},{2,0},{3,1},{4,2},{5,3},{6,4},{7,5},{8,14},{9,15},{10,... | collective-permute-start | bytes 393224 | tf_op jit(solution)/shard_map/ppermute | solution.py:37
  49.7 4.1 %collective-permute-start.1 = (bf16[128,512]{1,0:T(8,128)(2,1)S(1)}, bf16[128,512]{1,0:T(8,128)(2,1)S(1)}, u32[]{:S(2)}, u32[]{:S(2)}) collective-permute-start(bf16[128,512]{1,0:T(8,128)(2,1)S(1)} %get-tuple-element.32), channel_id=1, source_target_pairs={{0,2},{1,3},{2,4},{3,5},{4,6},{5,7},{6,0},{7,1},{8,10},{9,11},{10,... | collective-permute-start | bytes 393224 | tf_op jit(solution)/shard_map/ppermute | solution.py:37
  55.1 19.8 %copy-start.8 = (bf16[128,512]{1,0:T(8,128)(2,1)}, bf16[128,512]{1,0:T(8,128)(2,1)S(1)}, u32[]{:S(2)}) copy-start(bf16[128,512]{1,0:T(8,128)(2,1)S(1)} %fusion.22) | copy-start | bytes 393220
  55.1 3.2 %collective-permute-start.4 = (bf16[128,512]{1,0:T(8,128)(2,1)S(1)}, bf16[128,512]{1,0:T(8,128)(2,1)S(1)}, u32[]{:S(2)}, u32[]{:S(2)}) collective-permute-start(bf16[128,512]{1,0:T(8,128)(2,1)S(1)} %fusion.22), channel_id=1, source_target_pairs={{0,1},{1,0},{2,3},{3,2},{4,5},{5,4},{6,7},{7,6},{8,9},{9,8},{10,11... | collective-permute-start | bytes 393224 | tf_op jit(solution)/shard_map/ppermute | solution.py:41
  58.3 17.6 %copy-start.10 = (bf16[128,512]{1,0:T(8,128)(2,1)}, bf16[128,512]{1,0:T(8,128)(2,1)S(1)}, u32[]{:S(2)}) copy-start(bf16[128,512]{1,0:T(8,128)(2,1)S(1)} %collective-permute-done.4) | copy-start | bytes 393220
  58.3 21.9 %copy-start.17 = (s32[15]{0:T(128)S(1)}, s32[15]{0:T(128)}, u32[]{:S(2)}) copy-start(s32[15]{0:T(128)} %param.17) | copy-start | bytes 184
  58.6 33.2 %copy-start.11 = (f32[4096]{0:T(1024)S(1)}, f32[4096]{0:T(1024)}, u32[]{:S(2)}) copy-start(f32[4096]{0:T(1024)} %param.22) | copy-start | bytes 49156
  58.6 33.4 %copy-start.18 = (s32[12]{0:T(128)S(1)}, s32[12]{0:T(128)}, u32[]{:S(2)}) copy-start(s32[12]{0:T(128)} %constant.75.clone) | copy-start | bytes 148
  72.9 13.0 %collective-permute-start.18 = (bf16[256,1024]{1,0:T(8,128)(2,1)}, bf16[256,1024]{1,0:T(8,128)(2,1)}, u32[]{:S(2)}, u32[]{:S(2)}) collective-permute-start(bf16[256,1024]{1,0:T(8,128)(2,1)} %bitcast.21.refs_6_), channel_id=1, source_target_pairs={{0,2},{1,3},{2,4},{3,5},{4,6},{5,7},{6,0},{7,1},{8,10},{9,11},{10,... | collective-permute-start | bytes 1572872 | tf_op jit(solution)/shard_map/ppermute | solution.py:37
  74.6 14.0 %collective-permute-start.19 = (bf16[256,1024]{1,0:T(8,128)(2,1)}, bf16[256,1024]{1,0:T(8,128)(2,1)}, u32[]{:S(2)}, u32[]{:S(2)}) collective-permute-start(bf16[256,1024]{1,0:T(8,128)(2,1)} %bitcast.21.refs_6_), channel_id=1, source_target_pairs={{0,6},{1,7},{2,0},{3,1},{4,2},{5,3},{6,4},{7,5},{8,14},{9,15},{10,... | collective-permute-start | bytes 1572872 | tf_op jit(solution)/shard_map/ppermute | solution.py:37
  75.9 17.3 %all-to-all-start.1 = ((bf16[16,16,1024]{2,1,0:T(8,128)(2,1)}), bf16[16,16,1024]{2,1,0:T(8,128)(2,1)}, u32[]{:S(2)}, u32[]{:S(2)}) async-start(bf16[16,16,1024]{2,1,0:T(8,128)(2,1)} %bitcast.77), calls=%async_computation.1 | async-start | bytes 1048576 | tf_op jit(solution)/shard_map/all_to_all | solution.py:339
  87.7 7.0 %collective-permute-start.20 = (bf16[128,1024]{1,0:T(8,128)(2,1)}, bf16[128,1024]{1,0:T(8,128)(2,1)S(1)}, u32[]{:S(2)}, u32[]{:S(2)}) collective-permute-start(bf16[128,1024]{1,0:T(8,128)(2,1)} %slice.151), channel_id=1, source_target_pairs={{0,2},{1,3},{2,4},{3,5},{4,6},{5,7},{6,0},{7,1},{8,10},{9,11},{10,... | collective-permute-start | bytes 786440 | tf_op jit(solution)/shard_map/ppermute | solution.py:37
  90.3 5.7 %collective-permute-start.21 = (bf16[128,1024]{1,0:T(8,128)(2,1)}, bf16[128,1024]{1,0:T(8,128)(2,1)}, u32[]{:S(2)}, u32[]{:S(2)}) collective-permute-start(bf16[128,1024]{1,0:T(8,128)(2,1)} %slice.152), channel_id=1, source_target_pairs={{0,6},{1,7},{2,0},{3,1},{4,2},{5,3},{6,4},{7,5},{8,14},{9,15},{10,... | collective-permute-start | bytes 786440 | tf_op jit(solution)/shard_map/ppermute | solution.py:37
  94.6 24.5 %collective-permute-start.10 = (bf16[256,1024]{1,0:T(8,128)(2,1)}, bf16[256,1024]{1,0:T(8,128)(2,1)S(1)}, u32[]{:S(2)}, u32[]{:S(2)}) collective-permute-start(bf16[256,1024]{1,0:T(8,128)(2,1)} %bitcast.16.refs_6_), channel_id=1, source_target_pairs={{0,2},{1,3},{2,4},{3,5},{4,6},{5,7},{6,0},{7,1},{8,10},{9,11},{10,... | collective-permute-start | bytes 1572872 | tf_op jit(solution)/shard_map/ppermute | solution.py:37
  96.0 23.2 %collective-permute-start.11 = (bf16[256,1024]{1,0:T(8,128)(2,1)}, bf16[256,1024]{1,0:T(8,128)(2,1)S(1)}, u32[]{:S(2)}, u32[]{:S(2)}) collective-permute-start(bf16[256,1024]{1,0:T(8,128)(2,1)} %bitcast.16.refs_6_), channel_id=1, source_target_pairs={{0,6},{1,7},{2,0},{3,1},{4,2},{5,3},{6,4},{7,5},{8,14},{9,15},{10,... | collective-permute-start | bytes 1572872 | tf_op jit(solution)/shard_map/ppermute | solution.py:37
  113.0 12.5 %collective-permute-start.22 = (bf16[256,1024]{1,0:T(8,128)(2,1)S(1)}, bf16[256,1024]{1,0:T(8,128)(2,1)S(1)}, u32[]{:S(2)}, u32[]{:S(2)}) collective-permute-start(bf16[256,1024]{1,0:T(8,128)(2,1)S(1)} %get-tuple-element.25), channel_id=1, source_target_pairs={{0,2},{1,3},{2,4},{3,5},{4,6},{5,7},{6,0},{7,1},{8,10},{9,11},{10,... | collective-permute-start | bytes 1572872 | tf_op jit(solution)/shard_map/ppermute | solution.py:37
  113.3 12.3 %collective-permute-start.23 = (bf16[256,1024]{1,0:T(8,128)(2,1)S(1)}, bf16[256,1024]{1,0:T(8,128)(2,1)S(1)}, u32[]{:S(2)}, u32[]{:S(2)}) collective-permute-start(bf16[256,1024]{1,0:T(8,128)(2,1)S(1)} %get-tuple-element.26), channel_id=1, source_target_pairs={{0,6},{1,7},{2,0},{3,1},{4,2},{5,3},{6,4},{7,5},{8,14},{9,15},{10,... | collective-permute-start | bytes 1572872 | tf_op jit(solution)/shard_map/ppermute | solution.py:37
  116.4 8.3 %collective-permute-start.5 = (f32[128,16]{0,1:T(8,128)S(1)}, f32[128,16]{0,1:T(8,128)S(1)}, u32[]{:S(2)}, u32[]{:S(2)}) collective-permute-start(f32[128,16]{0,1:T(8,128)S(1)} %maximum_maximum_fusion.1), channel_id=1, source_target_pairs={{0,2},{1,3},{2,0},{3,1},{4,6},{5,7},{6,4},{7,5},{8,10},{9,11},{10,... | collective-permute-start | bytes 24584 | tf_op jit(solution)/shard_map/ppermute | solution.py:356
  119.1 12.6 %collective-permute-start.12 = (bf16[128,1024]{1,0:T(8,128)(2,1)S(1)}, bf16[128,1024]{1,0:T(8,128)(2,1)S(1)}, u32[]{:S(2)}, u32[]{:S(2)}) collective-permute-start(bf16[128,1024]{1,0:T(8,128)(2,1)S(1)} %slice.149), channel_id=1, source_target_pairs={{0,2},{1,3},{2,4},{3,5},{4,6},{5,7},{6,0},{7,1},{8,10},{9,11},{10,... | collective-permute-start | bytes 786440 | tf_op jit(solution)/shard_map/ppermute | solution.py:37
  119.2 12.5 %collective-permute-start.13 = (bf16[128,1024]{1,0:T(8,128)(2,1)S(1)}, bf16[128,1024]{1,0:T(8,128)(2,1)S(1)}, u32[]{:S(2)}, u32[]{:S(2)}) collective-permute-start(bf16[128,1024]{1,0:T(8,128)(2,1)S(1)} %slice.150), channel_id=1, source_target_pairs={{0,6},{1,7},{2,0},{3,1},{4,2},{5,3},{6,4},{7,5},{8,14},{9,15},{10,... | collective-permute-start | bytes 786440 | tf_op jit(solution)/shard_map/ppermute | solution.py:37
  124.8 6.9 %collective-permute-start.6 = (f32[128,16]{0,1:T(8,128)S(1)}, f32[128,16]{0,1:T(8,128)S(1)}, u32[]{:S(2)}, u32[]{:S(2)}) collective-permute-start(f32[128,16]{0,1:T(8,128)S(1)} %fusion.108), channel_id=1, source_target_pairs={{0,4},{1,5},{2,6},{3,7},{4,0},{5,1},{6,2},{7,3},{8,12},{9,13},{10,... | collective-permute-start | bytes 24584 | tf_op jit(solution)/shard_map/ppermute | solution.py:357
  125.7 21.1 %collective-permute-start.24 = (bf16[128,1024]{1,0:T(8,128)(2,1)S(1)}, bf16[128,1024]{1,0:T(8,128)(2,1)S(1)}, u32[]{:S(2)}, u32[]{:S(2)}) collective-permute-start(bf16[128,1024]{1,0:T(8,128)(2,1)S(1)} %get-tuple-element.28), channel_id=1, source_target_pairs={{0,2},{1,3},{2,4},{3,5},{4,6},{5,7},{6,0},{7,1},{8,10},{9,11},{10,... | collective-permute-start | bytes 786440 | tf_op jit(solution)/shard_map/ppermute | solution.py:37
  127.4 19.4 %collective-permute-start.25 = (bf16[128,1024]{1,0:T(8,128)(2,1)S(1)}, bf16[128,1024]{1,0:T(8,128)(2,1)S(1)}, u32[]{:S(2)}, u32[]{:S(2)}) collective-permute-start(bf16[128,1024]{1,0:T(8,128)(2,1)S(1)} %get-tuple-element.29), channel_id=1, source_target_pairs={{0,6},{1,7},{2,0},{3,1},{4,2},{5,3},{6,4},{7,5},{8,14},{9,15},{10,... | collective-permute-start | bytes 786440 | tf_op jit(solution)/shard_map/ppermute | solution.py:37
  145.2 1.8 copy-start.4
  145.2 1.8 copy-start.6
  145.2 8.8 %copy-start.12 = (s32[128,2]{0,1:T(2,128)S(1)}, s32[128,2]{0,1:T(2,128)}, u32[]{:S(2)}) copy-start(s32[128,2]{0,1:T(2,128)} %param.16) | copy-start | bytes 3076
  145.3 8.8 %collective-permute-start.14 = (bf16[256,1024]{1,0:T(8,128)(2,1)}, bf16[256,1024]{1,0:T(8,128)(2,1)}, u32[]{:S(2)}, u32[]{:S(2)}) collective-permute-start(bf16[256,1024]{1,0:T(8,128)(2,1)} %get-tuple-element.19), channel_id=1, source_target_pairs={{0,2},{1,3},{2,4},{3,5},{4,6},{5,7},{6,0},{7,1},{8,10},{9,11},{10,... | collective-permute-start | bytes 1572872 | tf_op jit(solution)/shard_map/ppermute | solution.py:37
  145.7 9.2 %collective-permute-start.15 = (bf16[256,1024]{1,0:T(8,128)(2,1)}, bf16[256,1024]{1,0:T(8,128)(2,1)}, u32[]{:S(2)}, u32[]{:S(2)}) collective-permute-start(bf16[256,1024]{1,0:T(8,128)(2,1)} %get-tuple-element.20), channel_id=1, source_target_pairs={{0,6},{1,7},{2,0},{3,1},{4,2},{5,3},{6,4},{7,5},{8,14},{9,15},{10,... | collective-permute-start | bytes 1572872 | tf_op jit(solution)/shard_map/ppermute | solution.py:37
  147.8 22.4 %all-to-all-start.4 = ((bf16[16,16,1024]{2,1,0:T(8,128)(2,1)}), bf16[16,16,1024]{2,1,0:T(8,128)(2,1)}, u32[]{:S(2)}, u32[]{:S(2)}) async-start(bf16[16,16,1024]{2,1,0:T(8,128)(2,1)} %bitcast.75), calls=%async_computation.4 | async-start | bytes 1048576 | tf_op jit(solution)/shard_map/all_to_all | solution.py:339
  154.9 1.0 copy-start.7
  157.3 17.4 %copy-start.15 = (s32[16]{0:T(128)S(1)}, s32[16]{0:T(128)}, u32[]{:S(2)}) copy-start(s32[16]{0:T(128)} %copy-done.14) | copy-start | bytes 196
  157.3 8.1 %collective-permute-start.16 = (bf16[128,1024]{1,0:T(8,128)(2,1)S(1)}, bf16[128,1024]{1,0:T(8,128)(2,1)S(1)}, u32[]{:S(2)}, u32[]{:S(2)}) collective-permute-start(bf16[128,1024]{1,0:T(8,128)(2,1)S(1)} %get-tuple-element.22), channel_id=1, source_target_pairs={{0,2},{1,3},{2,4},{3,5},{4,6},{5,7},{6,0},{7,1},{8,10},{9,11},{10,... | collective-permute-start | bytes 786440 | tf_op jit(solution)/shard_map/ppermute | solution.py:37
  158.8 8.2 %collective-permute-start.17 = (bf16[128,1024]{1,0:T(8,128)(2,1)S(1)}, bf16[128,1024]{1,0:T(8,128)(2,1)S(1)}, u32[]{:S(2)}, u32[]{:S(2)}) collective-permute-start(bf16[128,1024]{1,0:T(8,128)(2,1)S(1)} %get-tuple-element.23), channel_id=1, source_target_pairs={{0,6},{1,7},{2,0},{3,1},{4,2},{5,3},{6,4},{7,5},{8,14},{9,15},{10,... | collective-permute-start | bytes 786440 | tf_op jit(solution)/shard_map/ppermute | solution.py:37
  167.0 1.0 copy-start.5
  169.4 0.8 copy-start.2
  170.2 13.5 %copy-start.13 = (s32[16]{0:T(128)S(1)}, s32[16]{0:T(128)}, u32[]{:S(2)}) copy-start(s32[16]{0:T(128)} %iota_add_fusion.1) | copy-start | bytes 196
  170.2 13.5 %all-to-all-start.2 = ((bf16[16,16,1024]{2,1,0:T(8,128)(2,1)}), bf16[16,16,1024]{2,1,0:T(8,128)(2,1)}, u32[]{:S(2)}, u32[]{:S(2)}) async-start(bf16[16,16,1024]{2,1,0:T(8,128)(2,1)} %bitcast.76), calls=%async_computation.2 | async-start | bytes 1048576 | tf_op jit(solution)/shard_map/all_to_all | solution.py:339
  186.7 16.6 %copy-start.9 = (bf16[128,512]{1,0:T(8,128)(2,1)S(1)}, bf16[128,512]{1,0:T(8,128)(2,1)}, u32[]{:S(2)}) copy-start(bf16[128,512]{1,0:T(8,128)(2,1)} %copy-done.8) | copy-start | bytes 393220
  186.7 16.6 %collective-permute-start.26 = (bf16[128,512]{1,0:T(8,128)(2,1)S(1)}, bf16[128,512]{1,0:T(8,128)(2,1)S(1)}, u32[]{:S(2)}, u32[]{:S(2)}) collective-permute-start(bf16[128,512]{1,0:T(8,128)(2,1)S(1)} %select_convert_fusion), channel_id=1, source_target_pairs={{0,1},{1,0},{2,3},{3,2},{4,5},{5,4},{6,7},{7,6},{8,9},{9,8},{10,11... | collective-permute-start | bytes 393224 | tf_op jit(solution)/shard_map/ppermute | solution.py:41
  (2 other events, 1.3 us)

commit v4 on v3

--- a/solution.py
+++ b/solution.py
@@ -104,7 +104,7 @@
 
 def ffn_kernel(ids, gain_ref, *refs):
     weights = refs[:6]
-    pieces = refs[6:11]
+    pieces = refs[6:-10]
     outs = refs[-10:-6]
     xs_ref, act_ref, gate_ref, up_ref, down_ref, sems = refs[-6:]
     held = [gate_ref.at[0], up_ref.at[0], gate_ref.at[1], up_ref.at[1]]
@@ -122,7 +122,7 @@
 
     for side in range(2):
         chosen = [(pieces[k], 0, k) for k in range(3)]
-        chosen += [(pieces[3 + side], side * half, 3)]
+        chosen += [(pieces[3 + side], side * half, 3) if len(pieces) > 4 else (pieces[3], 0, 3)]
 
         def norm(i, carry):
             at_row = pl.multiple_of(side * half + i * tile, tile)
@@ -184,12 +184,34 @@
     )(ids, gain, *weights, *pieces)
 
 
+def in_vmem(value):
+    return pltpu.with_memory_space_constraint(value, pltpu.VMEM)
+
+
+def in_hbm(value):
+    return pltpu.with_memory_space_constraint(value, pltpu.HBM)
+
+
+def gather_direct(own):
+    below = in_vmem(send_z(own, 1))
+    above = in_vmem(send_z(own, -1))
+    far = in_vmem(send_z(own, 2))
+    return [own, below, above, far]
+
+
+def split_kernel(below_ref, above_ref, low_ref, high_ref):
+    half = low_ref.shape[0]
+    low_ref[...] = below_ref[:half, :]
+    high_ref[...] = above_ref[half:, :]
+
+
 def gather_ring(own):
     half = own.shape[0] // 2
-    below = send_z(own, 1)
-    above = send_z(own, -1)
-    far_a = send_z(below[:half], 1)
-    far_b = send_z(above[half:], -1)
+    below = in_vmem(send_z(own, 1))
+    above = in_vmem(send_z(own, -1))
+    low, high = local_call(split_kernel, (below, above), (half, half))
+    far_a = in_vmem(send_z(low, 1))
+    far_b = in_vmem(send_z(high, -1))
     return [own, below, above, far_a, far_b]
 
 
@@ -221,15 +243,53 @@
     )(*args)
 
 
+def sum_kernel(*refs):
+    total = refs[0][...].astype(F32)
+    for ref in refs[1:-1]:
+        total = total + ref[...].astype(F32)
+    refs[-1][...] = total.astype(BF16)
+
+
+def scatter_direct(near, above, far, rest):
+    moved = [in_vmem(send_z(v, d)) for v, d in ((near, 1), (above, -1), (far, 2))]
+    return local_call(sum_kernel, (in_hbm(rest), *moved), (rest.shape[0],))[0]
+
+
 def scatter_ring(up, down, relay, rest):
     rows = up.shape[0]
     half = rows // 2
-    from_below = send_z(up, 1)
-    from_above = send_z(down, -1)
-    low, high = local_call(relay_kernel, (relay, from_below, from_above), (half, half))
-    low = send_z(low, 1)
-    high = send_z(high, -1)
-    return local_call(end_kernel, (rest, from_below, from_above, low, high), (rows,))[0]
+    from_below = in_vmem(send_z(up, 1))
+    from_above = in_vmem(send_z(down, -1))
+    low, high = local_call(
+        relay_kernel, (in_hbm(relay), from_below, from_above), (half, half)
+    )
+    low = in_hbm(send_z(in_hbm(low), 1))
+    high = in_hbm(send_z(in_hbm(high), -1))
+    moved = (from_below, from_above, low, high)
+    return local_call(end_kernel, (in_hbm(rest), *moved), (rows,))[0]
+
+
+def cache_kernel(slot_ref, kv_ref, out_ref):
+    rows, total = out_ref.shape[0], kv_ref.shape[0]
+    place = pl.program_id(0) * rows + lax.broadcasted_iota(jnp.int32, (rows, total), 0)
+    take = jnp.where(place == slot_ref[...], 1.0, 0.0).astype(BF16)
+    out_ref[...] = jnp.dot(take, kv_ref[...], preferred_element_type=F32).astype(BF16)
+
+
+def fill_cache(slot, kv):
+    total, width = kv.shape
+    rows = 256
+    return pl.pallas_call(
+        cache_kernel,
+        grid=(total // rows,),
+        out_shape=jax.ShapeDtypeStruct((total, width), BF16),
+        in_specs=[
+            pl.BlockSpec((1, total), lambda i: (0, 0)),
+            pl.BlockSpec((total, width), lambda i: (0, 0)),
+        ],
+        out_specs=pl.BlockSpec((rows, width), lambda i: (i, 0)),
+        compiler_params=pltpu.CompilerParams(vmem_limit_bytes=12 * MIB),
+    )(slot, kv)
 
 
 def local(
@@ -363,15 +423,16 @@
     gate_dup = jnp.repeat(gate_of, holders, axis=1)
 
     gain_rows = gain_moe.reshape(NZ, 2 * share)
-    hops = jnp.array([0, 3, 1, 2, 2, 1, 3, 2, 1, 3, 0, 0], jnp.int32)
-    ids = lax.rem(z + hops, NZ)
+    from_z = [0, 3, 1, 2]
+    direct_ids = lax.rem(z + jnp.array(from_z + [1, 1, 3, 3, 2, 2, 0, 0], jnp.int32), NZ)
+    ring_ids = lax.rem(z + jnp.array(from_z + [2, 1, 3, 2, 1, 3, 0, 0], jnp.int32), NZ)
     a_own = dispatch(picks[0])
     a_pieces = gather_ring(a_own)
     b_own = dispatch(picks[1])
-    b_pieces = gather_ring(b_own)
-    a_out = ffn(ids, gain_rows, weights, a_pieces)
-    b_out = ffn(ids, gain_rows, weights, b_pieces)
-    a_final = scatter_ring(*a_out)
+    b_pieces = gather_direct(b_own)
+    a_out = ffn(direct_ids, gain_rows, weights, a_pieces)
+    b_out = ffn(ring_ids, gain_rows, weights, b_pieces)
+    a_final = scatter_direct(*a_out)
     b_final = scatter_ring(*b_out)
     a_back = exchange(a_final)
     b_back = exchange(b_final)
@@ -404,10 +465,8 @@
     sizes = jnp.sum(held.astype(F32), axis=1).astype(BF16)
     ahead = jnp.dot(earlier, sizes[:, None], preferred_element_type=F32)
     slot = jnp.where(held, (inside + ahead).astype(jnp.int32), -1).reshape(1, total)
-    places = jnp.arange(total, dtype=jnp.int32)
-    take = (places[:, None] == slot).astype(BF16)
-    cache = jnp.dot(take, kv_all, preferred_element_type=F32)
-    return layer_out, cache.astype(BF16)
+    cache = fill_cache(slot, kv_all)
+    return layer_out, cache
 
 
 def solution(mesh):

time: 207 us -> 203 us (0.981)
  Pallas kernels: 36.9 us -> 46.4 us
  starting transfers between devices: 66.2 us -> 57.3 us
  matrix products: 19.1 us -> 14.8 us
  local copies, waits for them, and re-layouts: 12.5 us -> 9.45 us
    pallas_call x0 -> x1, Pallas kernels: none -> 4.87 us  [fill_cache(): pl.pallas_call(cache_kernel, grid=(total // rows,), out_shape=jax.ShapeDt...]
    ppermute x6, starting transfers between devices: 18.7 us -> 14.2 us  [send_core(): return lax.ppermute(value, 'tensor', core_perm())]
    dot_general x1 -> x0, matrix products: 4.16 us -> none  [local(): cache = jnp.dot(take, kv_all, preferred_element_type=F32)]
    pallas_call x4, Pallas kernels: 3.02 us -> 7.15 us  [local_call(): pl.pallas_call(kernel, out_shape=tuple((jax.ShapeDtypeStruct((height, sha...]
    ppermute x1, waiting for transfers between devices: 3.94 us -> 0.01 us  [local(): lax.ppermute(stats, 'tensor', [(t, t ^ 2) for t in range(ten_count)])]
    ppermute x19 -> x17, starting transfers between devices: 22.5 us -> 19 us  [send_z(): return lax.ppermute(value, 'tensor', z_perm(step))]
    slice x4 -> x0, local copies, waits for them, and re-layouts: 3.38 us -> none  [the longest x2 1.69 us: gather_ring(): far_b = send_z(above[half:], -1)]
    ppermute x1, waiting for transfers between devices: 2.72 us -> 5.41 us  [local(): lax.ppermute(stats, 'tensor', [(t, t ^ 4) for t in range(ten_count)])]
  transfers between devices with their start and end apart: 31 -> 29, of which waited for: 13 -> 13; matrix products, arithmetic and copies ran while one was open for 13% -> 10% of each run, Pallas kernels for 18% -> 23%
where the time goes in v4:
time: 203 us; the launch traced here: 200 us
  starting transfers between devices  57.3 us (28%)
  Pallas kernels  46.4 us (23%)
  waiting for transfers between devices  44.8 us (22%)
  matrix products  14.8 us (7%)
  blocking collectives  14.4 us (7%)
  other arithmetic  11.4 us (6%)
  local copies, waits for them, and re-layouts  9.45 us (5%)
    pallas_call x2, Pallas kernels, ffn(): pl.pallas_call(ffn_kernel, out_shape=(jax.ShapeDtypeStruct((rows, share),...  27.3 us
    ppermute x17, waiting for transfers between devices, send_z(): return lax.ppermute(value, 'tensor', z_perm(step))  20.2 us
    ppermute x17, starting transfers between devices, send_z(): return lax.ppermute(value, 'tensor', z_perm(step))  19 us
    all_to_all x3, starting transfers between devices, exchange(): lax.all_to_all(flat.reshape(seq_count, slots, 2 * share), 'seq', 0, 0, ti...  14.6 us
    all_to_all x1, blocking collectives, exchange(): lax.all_to_all(flat.reshape(seq_count, slots, 2 * share), 'seq', 0, 0, ti...  14.4 us
    ppermute x6, starting transfers between devices, send_core(): return lax.ppermute(value, 'tensor', core_perm())  14.2 us
    all_to_all x1, waiting for transfers between devices, local(): lax.all_to_all(jnp.broadcast_to(kv_own[None], (seq_count,) + kv_own.shape...  10.5 us
    pallas_call x4, Pallas kernels, local_call(): pl.pallas_call(kernel, out_shape=tuple((jax.ShapeDtypeStruct((height, sha...  7.15 us
  transfers between devices with their start and end apart: 29, of which 13 were waited for; matrix products, arithmetic and copies ran while one was open for 10% of the time, Pallas kernels for 23%

profile of v4, /device:TPU:33, one launch (start us, length us, event | category | flops | bytes accessed | tf_op | source)
XLA Modules:
  0.0 199.6 jit_solution(1030509656743609691)
XLA Ops:
  0.7 1.7 fusion
  3.6 1.7 fusion.11
  5.8 1.1 broadcast_in_dim.109
  6.9 6.8 %all-to-all-start = ((bf16[16,128,256]{2,1,0:T(8,128)(2,1)}), bf16[16,128,256]{2,1,0:T(8,128)(2,1)S(1)}, u32[]{:S(2)}, u32[]{:S(2)}) async-start(bf16[16,128,256]{2,1,0:T(8,128)(2,1)} %broadcast_in_dim.109), calls=%async_computation | async-start | bytes 2097152 | tf_op jit(solution)/shard_map/all_to_all | solution.py:351
  15.2 3.3 %fusion.13 = f32[128,512]{1,0:T(8,128)S(1)} fusion(bf16[4096,512]{1,0:T(8,128)(2,1)} %param.20, bf16[128,4096]{1,0:T(8,128)(2,1)} %param.15, f32[4096]{0:T(1024)S(1)} %copy-done.22, f32[128]{0:T(128)S(1)} %add_rsqrt_fusion), kind=kOutput, calls=%fused_computation.26 | convolution fusion | flops 538968064 | bytes 5521920 | tf_op jit(solution)/shard_map/dot_general | solution.py:342
  19.2 10.5 %all-to-all-done = bf16[16,128,256]{2,1,0:T(8,128)(2,1)S(1)} async-done(((bf16[16,128,256]{2,1,0:T(8,128)(2,1)}), bf16[16,128,256]{2,1,0:T(8,128)(2,1)S(1)}, u32[]{:S(2)}, u32[]{:S(2)}) %all-to-all-start) | async-done | bytes 1048608 | tf_op jit(solution)/shard_map/all_to_all | solution.py:351
  29.7 7.1 %shard_map.158 = (f32[4,128,512]{2,1,0:T(8,128)S(1)}, bf16[4,128,512]{2,1,0:T(8,128)(2,1)}) custom-call(s32[8]{0:T(128)S(1)} %pad_add_fusion.ids, s32[1]{0:T(128)} %bitcast.first_ref, bf16[512,128]{1,0:T(8,128)(2,1)S(1)} %maximum_maximum_fusion.q_ref, s32[128,1]{1,0:T(8,128)S(1)} %copy.20.start_ref, bf16[2048,256]{1,0:T(8,128)(2,1)S(1)} %bitcast.71, ...), custom_call_target="tpu_custom_call" | custom-call | tf_op jit(solution)/shard_map/pallas_call | solution.py:92
  37.8 2.6 %collective-permute-start = (bf16[4,128,512]{2,1,0:T(8,128)(2,1)}, bf16[4,128,512]{2,1,0:T(8,128)(2,1)}, u32[]{:S(2)}, u32[]{:S(2)}) collective-permute-start(bf16[4,128,512]{2,1,0:T(8,128)(2,1)} %get-tuple-element.17), channel_id=1, source_target_pairs={{0,1},{1,0},{2,3},{3,2},{4,5},{5,4},{6,7},{7,6},{8,9},{9,8},{10,11... | collective-permute-start | bytes 1572872 | tf_op jit(solution)/shard_map/ppermute | solution.py:41
  40.4 1.9 collective-permute-done
  42.3 1.4 fusion.22
  43.6 2.8 %collective-permute-start.3 = (bf16[128,512]{1,0:T(8,128)(2,1)S(1)}, bf16[128,512]{1,0:T(8,128)(2,1)}, u32[]{:S(2)}, u32[]{:S(2)}) collective-permute-start(bf16[128,512]{1,0:T(8,128)(2,1)S(1)} %get-tuple-element.33), channel_id=1, source_target_pairs={{0,4},{1,5},{2,6},{3,7},{4,0},{5,1},{6,2},{7,3},{8,12},{9,13},{10,... | collective-permute-start | bytes 393224 | tf_op jit(solution)/shard_map/ppermute | solution.py:37
  50.0 1.6 collective-permute-start.1
  51.6 1.6 collective-permute-done.2
  54.1 1.2 fusion.18
  55.3 3.0 %collective-permute-start.4 = (bf16[128,512]{1,0:T(8,128)(2,1)S(1)}, bf16[128,512]{1,0:T(8,128)(2,1)S(1)}, u32[]{:S(2)}, u32[]{:S(2)}) collective-permute-start(bf16[128,512]{1,0:T(8,128)(2,1)S(1)} %fusion.18), channel_id=1, source_target_pairs={{0,1},{1,0},{2,3},{3,2},{4,5},{5,4},{6,7},{7,6},{8,9},{9,8},{10,11... | collective-permute-start | bytes 393224 | tf_op jit(solution)/shard_map/ppermute | solution.py:41
  59.8 14.4 %all_to_all.25 = bf16[16,16,1024]{2,1,0:T(8,128)(2,1)} all-to-all(bf16[16,16,1024]{2,1,0:T(8,128)(2,1)S(1)} %bitcast.77), channel_id=1, replica_groups=mesh['seq'=16,'tensor'=8] {'seq'}, dimensions={0} | all-to-all | bytes 1048576 | tf_op jit(solution)/shard_map/all_to_all | solution.py:399
  75.6 1.1 convolution_convert_fusion
  76.7 4.2 %all-to-all-start.3 = ((bf16[16,16,1024]{2,1,0:T(8,128)(2,1)}), bf16[16,16,1024]{2,1,0:T(8,128)(2,1)}, u32[]{:S(2)}, u32[]{:S(2)}) async-start(bf16[16,16,1024]{2,1,0:T(8,128)(2,1)} %bitcast.76), calls=%async_computation.3 | async-start | bytes 1048576 | tf_op jit(solution)/shard_map/all_to_all | solution.py:399
  81.0 5.6 %collective-permute-done.10.below_ref.refs_7_ = bf16[256,1024]{1,0:T(8,128)(2,1)} collective-permute-done((bf16[256,1024]{1,0:T(8,128)(2,1)}, bf16[256,1024]{1,0:T(8,128)(2,1)}, u32[]{:S(2)}, u32[]{:S(2)}) %collective-permute-start.10) | collective-permute-done | bytes 524320 | tf_op jit(solution)/shard_map/ppermute | solution.py:37
  87.3 2.0 %shard_map.159 = (bf16[128,1024]{1,0:T(8,128)(2,1)}, bf16[128,1024]{1,0:T(8,128)(2,1)}) custom-call(bf16[256,1024]{1,0:T(8,128)(2,1)} %collective-permute-done.10.below_ref.refs_7_, bf16[256,1024]{1,0:T(8,128)(2,1)} %collective-permute-done.11.above_ref.refs_8_), custom_call_target="tpu_custom_call" | custom-call | tf_op jit(solution)/shard_map/pallas_call | solution.py:237
  89.3 1.3 collective-permute-start.12
  91.7 1.3 dynamic_slice.14
  93.5 1.9 collective-permute-done.12.refs_9_
  96.4 1.5 fusion.9
  98.0 1.2 fusion.10
  99.1 1.9 collective-permute-start.18
  101.7 2.7 %collective-permute-start.5 = (f32[128,16]{0,1:T(8,128)S(1)}, f32[128,16]{0,1:T(8,128)S(1)}, u32[]{:S(2)}, u32[]{:S(2)}) collective-permute-start(f32[128,16]{0,1:T(8,128)S(1)} %maximum_maximum_fusion.1), channel_id=1, source_target_pairs={{0,2},{1,3},{2,0},{3,1},{4,6},{5,7},{6,4},{7,5},{8,10},{9,11},{10,... | collective-permute-start | bytes 24584 | tf_op jit(solution)/shard_map/ppermute | solution.py:416
  105.8 13.3 %shard_map.160 = (bf16[256,1024]{1,0:T(8,128)(2,1)S(1)}, bf16[256,1024]{1,0:T(8,128)(2,1)S(1)}, bf16[256,1024]{1,0:T(8,128)(2,1)S(1)}, bf16[256,1024]{1,0:T(8,128)(2,1)S(1)}) custom-call(s32[12]{0:T(128)S(1)} %compare_select_fusion.3.ids, f32[4,1024]{1,0:T(4,128)S(1)} %reshape.172.gain_ref, bf16[4096,512]{1,0:T(8,128)(2,1)} %refs_0_.3, ...), custom_call_target="tpu_custom_call" | custom-call | tf_op jit(solution)/shard_map/pallas_call | solution.py:170
  119.9 1.3 collective-permute-start.14
  121.4 3.0 %collective-permute-start.16 = (bf16[256,1024]{1,0:T(8,128)(2,1)S(1)}, bf16[256,1024]{1,0:T(8,128)(2,1)S(1)}, u32[]{:S(2)}, u32[]{:S(2)}) collective-permute-start(bf16[256,1024]{1,0:T(8,128)(2,1)S(1)} %get-tuple-element.23), channel_id=1, source_target_pairs={{0,4},{1,5},{2,6},{3,7},{4,0},{5,1},{6,2},{7,3},{8,12},{9,13},{10,... | collective-permute-start | bytes 1572872 | tf_op jit(solution)/shard_map/ppermute | solution.py:37
  124.6 14.0 %shard_map.162 = (bf16[256,1024]{1,0:T(8,128)(2,1)}, bf16[256,1024]{1,0:T(8,128)(2,1)}, bf16[256,1024]{1,0:T(8,128)(2,1)S(1)}, bf16[256,1024]{1,0:T(8,128)(2,1)S(1)}) custom-call(s32[12]{0:T(128)S(1)} %compare_select_fusion.1.ids, f32[4,1024]{1,0:T(4,128)S(1)} %reshape.172.gain_ref, bf16[4096,512]{1,0:T(8,128)(2,1)} %refs_0_.3, bf16[4096,512]{1,0:T(8,128)(2,1)} %refs_1_.3, ...), custom_call_target="tpu_custom_call" | custom-call | tf_op jit(solution)/shard_map/pallas_call | solution.py:170
  138.6 1.9 collective-permute-start.20
  140.5 5.4 %collective-permute-done.6 = f32[128,16]{0,1:T(8,128)S(1)} collective-permute-done((f32[128,16]{0,1:T(8,128)S(1)}, f32[128,16]{0,1:T(8,128)S(1)}, u32[]{:S(2)}, u32[]{:S(2)}) %collective-permute-start.6) | collective-permute-done | bytes 8224 | tf_op jit(solution)/shard_map/ppermute | solution.py:417
  146.3 1.3 shard_map.161
  148.4 5.7 %all-to-all-start.2 = ((bf16[16,16,1024]{2,1,0:T(8,128)(2,1)}), bf16[16,16,1024]{2,1,0:T(8,128)(2,1)}, u32[]{:S(2)}, u32[]{:S(2)}) async-start(bf16[16,16,1024]{2,1,0:T(8,128)(2,1)} %bitcast.73), calls=%async_computation.2 | async-start | bytes 1048576 | tf_op jit(solution)/shard_map/all_to_all | solution.py:399
  154.1 2.9 %collective-permute-done.21.above_ref = bf16[256,1024]{1,0:T(8,128)(2,1)} collective-permute-done((bf16[256,1024]{1,0:T(8,128)(2,1)}, bf16[256,1024]{1,0:T(8,128)(2,1)}, u32[]{:S(2)}, u32[]{:S(2)}) %collective-permute-start.21) | collective-permute-done | bytes 524320 | tf_op jit(solution)/shard_map/ppermute | solution.py:37
  157.0 2.1 %shard_map.163 = (bf16[128,1024]{1,0:T(8,128)(2,1)}, bf16[128,1024]{1,0:T(8,128)(2,1)S(1)}) custom-call(bf16[256,1024]{1,0:T(8,128)(2,1)} %copy-done.6, bf16[256,1024]{1,0:T(8,128)(2,1)} %collective-permute-done.20.below_ref, bf16[256,1024]{1,0:T(8,128)(2,1)} %collective-permute-done.21.above_ref), custom_call_target="tpu_custom_call" | custom-call | tf_op jit(solution)/shard_map/pallas_call | solution.py:237
  160.7 4.1 %collective-permute-done.22.low_ref = bf16[128,1024]{1,0:T(8,128)(2,1)} collective-permute-done((bf16[128,1024]{1,0:T(8,128)(2,1)}, bf16[128,1024]{1,0:T(8,128)(2,1)}, u32[]{:S(2)}, u32[]{:S(2)}) %collective-permute-start.22) | collective-permute-done | bytes 262176 | tf_op jit(solution)/shard_map/ppermute | solution.py:37
  164.8 1.5 collective-permute-done.23.high_ref
  166.3 1.7 shard_map.164
  168.8 4.7 %all-to-all-start.4 = ((bf16[16,16,1024]{2,1,0:T(8,128)(2,1)}), bf16[16,16,1024]{2,1,0:T(8,128)(2,1)}, u32[]{:S(2)}, u32[]{:S(2)}) async-start(bf16[16,16,1024]{2,1,0:T(8,128)(2,1)} %bitcast.74), calls=%async_computation.4 | async-start | bytes 1048576 | tf_op jit(solution)/shard_map/all_to_all | solution.py:399
  173.6 2.2 %convolution_bitcast_fusion.2 = f32[128,1024]{1,0:T(8,128)} fusion(bf16[16,16,1024]{2,1,0:T(8,128)(2,1)} %all-to-all-done.2, f32[128,16]{0,1:T(8,128)S(1)} %bitcast.83, s32[128,16]{0,1:T(8,128)S(1)} %bitcast.79, s32[16]{0:T(128)S(1)} %copy-done.16), kind=kOutput, calls=%fused_computation.9 | convolution fusion | flops 67305472 | bytes 1065024 | tf_op jit(solution)/shard_map/dot_general | solution.py:445
  175.8 6.8 %all-to-all-done.4 = bf16[16,16,1024]{2,1,0:T(8,128)(2,1)} async-done(((bf16[16,16,1024]{2,1,0:T(8,128)(2,1)}), bf16[16,16,1024]{2,1,0:T(8,128)(2,1)}, u32[]{:S(2)}, u32[]{:S(2)}) %all-to-all-start.4) | async-done | bytes 524320 | tf_op jit(solution)/shard_map/all_to_all | solution.py:399
  182.6 1.4 convolution_bitcast_fusion
  184.0 1.4 fusion.5
  185.4 1.4 fusion.4
  186.9 7.0 %collective-permute-start.24 = (bf16[128,512]{1,0:T(8,128)(2,1)S(1)}, bf16[128,512]{1,0:T(8,128)(2,1)S(1)}, u32[]{:S(2)}, u32[]{:S(2)}) collective-permute-start(bf16[128,512]{1,0:T(8,128)(2,1)S(1)} %select_convert_fusion), channel_id=1, source_target_pairs={{0,1},{1,0},{2,3},{3,2},{4,5},{5,4},{6,7},{7,6},{8,9},{9,8},{10,11... | collective-permute-start | bytes 393224 | tf_op jit(solution)/shard_map/ppermute | solution.py:41
  194.0 4.9 %shard_map.165 = bf16[2048,256]{1,0:T(8,128)(2,1)} custom-call(s32[1,2048]{1,0:T(1,128)S(1)} %bitcast.75, bf16[2048,256]{1,0:T(8,128)(2,1)S(1)} %bitcast.72), custom_call_target="tpu_custom_call" | custom-call | tf_op jit(solution)/shard_map/pallas_call | solution.py:282
  (129 shorter events, 23.3 us)
Async XLA Ops:
  0.6 3.0 %copy-start = (bf16[4096,256]{1,0:T(8,128)(2,1)S(1)}, bf16[4096,256]{1,0:T(8,128)(2,1)}, u32[]{:S(2)}) copy-start(bf16[4096,256]{1,0:T(8,128)(2,1)} %param.21) | copy-start | bytes 6291460
  5.4 9.8 %copy-start.22 = (f32[4096]{0:T(1024)S(1)}, f32[4096]{0:T(1024)}, u32[]{:S(2)}) copy-start(f32[4096]{0:T(1024)} %param.19) | copy-start | bytes 49156
  6.9 22.8 %all-to-all-start = ((bf16[16,128,256]{2,1,0:T(8,128)(2,1)}), bf16[16,128,256]{2,1,0:T(8,128)(2,1)S(1)}, u32[]{:S(2)}, u32[]{:S(2)}) async-start(bf16[16,128,256]{2,1,0:T(8,128)(2,1)} %broadcast_in_dim.109), calls=%async_computation | async-start | bytes 2097152 | tf_op jit(solution)/shard_map/all_to_all | solution.py:351
  13.7 88.0 %collective-permute-start.7 = (bf16[4096,512]{1,0:T(8,128)(2,1)}, bf16[4096,512]{1,0:T(8,128)(2,1)}, u32[]{:S(2)}, u32[]{:S(2)}) collective-permute-start(bf16[4096,512]{1,0:T(8,128)(2,1)} %refs_0_.3), channel_id=1, source_target_pairs={{0,1},{1,0},{2,3},{3,2},{4,5},{5,4},{6,7},{7,6},{8,9},{9,8},{10,11... | collective-permute-start | bytes 12582920 | tf_op jit(solution)/shard_map/ppermute | solution.py:41
  14.7 89.7 %collective-permute-start.8 = (bf16[4096,512]{1,0:T(8,128)(2,1)}, bf16[4096,512]{1,0:T(8,128)(2,1)}, u32[]{:S(2)}, u32[]{:S(2)}) collective-permute-start(bf16[4096,512]{1,0:T(8,128)(2,1)} %refs_1_.3), channel_id=1, source_target_pairs={{0,1},{1,0},{2,3},{3,2},{4,5},{5,4},{6,7},{7,6},{8,9},{9,8},{10,11... | collective-permute-start | bytes 12582920 | tf_op jit(solution)/shard_map/ppermute | solution.py:41
  14.8 91.0 %collective-permute-start.9 = (bf16[512,4096]{1,0:T(8,128)(2,1)}, bf16[512,4096]{1,0:T(8,128)(2,1)}, u32[]{:S(2)}, u32[]{:S(2)}) collective-permute-start(bf16[512,4096]{1,0:T(8,128)(2,1)} %refs_4_.3), channel_id=1, source_target_pairs={{0,1},{1,0},{2,3},{3,2},{4,5},{5,4},{6,7},{7,6},{8,9},{9,8},{10,11... | collective-permute-start | bytes 12582920 | tf_op jit(solution)/shard_map/ppermute | solution.py:41
  29.7 21.9 %copy-start.13 = (s32[128,2]{0,1:T(2,128)S(1)}, s32[128,2]{0,1:T(2,128)}, u32[]{:S(2)}) copy-start(s32[128,2]{0,1:T(2,128)} %param.17) | copy-start | bytes 3076
  36.8 1.0 copy-start.3
  37.8 4.5 %collective-permute-start = (bf16[4,128,512]{2,1,0:T(8,128)(2,1)}, bf16[4,128,512]{2,1,0:T(8,128)(2,1)}, u32[]{:S(2)}, u32[]{:S(2)}) collective-permute-start(bf16[4,128,512]{2,1,0:T(8,128)(2,1)} %get-tuple-element.17), channel_id=1, source_target_pairs={{0,1},{1,0},{2,3},{3,2},{4,5},{5,4},{6,7},{7,6},{8,9},{9,8},{10,11... | collective-permute-start | bytes 1572872 | tf_op jit(solution)/shard_map/ppermute | solution.py:41
  43.6 6.4 %collective-permute-start.3 = (bf16[128,512]{1,0:T(8,128)(2,1)S(1)}, bf16[128,512]{1,0:T(8,128)(2,1)}, u32[]{:S(2)}, u32[]{:S(2)}) collective-permute-start(bf16[128,512]{1,0:T(8,128)(2,1)S(1)} %get-tuple-element.33), channel_id=1, source_target_pairs={{0,4},{1,5},{2,6},{3,7},{4,0},{5,1},{6,2},{7,3},{8,12},{9,13},{10,... | collective-permute-start | bytes 393224 | tf_op jit(solution)/shard_map/ppermute | solution.py:37
  46.4 30.3 %copy-start.15 = (s32[16]{0:T(128)}, s32[16]{0:T(128)S(1)}, u32[]{:S(2)}) copy-start(s32[16]{0:T(128)S(1)} %iota_add_fusion.1) | copy-start | bytes 196
  48.3 4.9 %collective-permute-start.2 = (bf16[128,512]{1,0:T(8,128)(2,1)S(1)}, bf16[128,512]{1,0:T(8,128)(2,1)S(1)}, u32[]{:S(2)}, u32[]{:S(2)}) collective-permute-start(bf16[128,512]{1,0:T(8,128)(2,1)S(1)} %get-tuple-element.34), channel_id=1, source_target_pairs={{0,6},{1,7},{2,0},{3,1},{4,2},{5,3},{6,4},{7,5},{8,14},{9,15},{10,... | collective-permute-start | bytes 393224 | tf_op jit(solution)/shard_map/ppermute | solution.py:37
  50.0 4.1 %collective-permute-start.1 = (bf16[128,512]{1,0:T(8,128)(2,1)S(1)}, bf16[128,512]{1,0:T(8,128)(2,1)S(1)}, u32[]{:S(2)}, u32[]{:S(2)}) collective-permute-start(bf16[128,512]{1,0:T(8,128)(2,1)S(1)} %get-tuple-element.32), channel_id=1, source_target_pairs={{0,2},{1,3},{2,4},{3,5},{4,6},{5,7},{6,0},{7,1},{8,10},{9,11},{10,... | collective-permute-start | bytes 393224 | tf_op jit(solution)/shard_map/ppermute | solution.py:37
  55.3 42.6 %copy-start.8 = (bf16[128,512]{1,0:T(8,128)(2,1)}, bf16[128,512]{1,0:T(8,128)(2,1)S(1)}, u32[]{:S(2)}) copy-start(bf16[128,512]{1,0:T(8,128)(2,1)S(1)} %fusion.18) | copy-start | bytes 393220
  55.3 4.1 %collective-permute-start.4 = (bf16[128,512]{1,0:T(8,128)(2,1)S(1)}, bf16[128,512]{1,0:T(8,128)(2,1)S(1)}, u32[]{:S(2)}, u32[]{:S(2)}) collective-permute-start(bf16[128,512]{1,0:T(8,128)(2,1)S(1)} %fusion.18), channel_id=1, source_target_pairs={{0,1},{1,0},{2,3},{3,2},{4,5},{5,4},{6,7},{7,6},{8,9},{9,8},{10,11... | collective-permute-start | bytes 393224 | tf_op jit(solution)/shard_map/ppermute | solution.py:41
  59.4 16.2 %copy-start.10 = (bf16[128,512]{1,0:T(8,128)(2,1)}, bf16[128,512]{1,0:T(8,128)(2,1)S(1)}, u32[]{:S(2)}) copy-start(bf16[128,512]{1,0:T(8,128)(2,1)S(1)} %collective-permute-done.4) | copy-start | bytes 393220
  74.2 12.4 %collective-permute-start.10 = (bf16[256,1024]{1,0:T(8,128)(2,1)}, bf16[256,1024]{1,0:T(8,128)(2,1)}, u32[]{:S(2)}, u32[]{:S(2)}) collective-permute-start(bf16[256,1024]{1,0:T(8,128)(2,1)} %bitcast.16.refs_6_), channel_id=1, source_target_pairs={{0,2},{1,3},{2,4},{3,5},{4,6},{5,7},{6,0},{7,1},{8,10},{9,11},{10,... | collective-permute-start | bytes 1572872 | tf_op jit(solution)/shard_map/ppermute | solution.py:37
  75.0 12.3 %collective-permute-start.11 = (bf16[256,1024]{1,0:T(8,128)(2,1)}, bf16[256,1024]{1,0:T(8,128)(2,1)}, u32[]{:S(2)}, u32[]{:S(2)}) collective-permute-start(bf16[256,1024]{1,0:T(8,128)(2,1)} %bitcast.16.refs_6_), channel_id=1, source_target_pairs={{0,6},{1,7},{2,0},{3,1},{4,2},{5,3},{6,4},{7,5},{8,14},{9,15},{10,... | collective-permute-start | bytes 1572872 | tf_op jit(solution)/shard_map/ppermute | solution.py:37
  76.7 16.8 %all-to-all-start.3 = ((bf16[16,16,1024]{2,1,0:T(8,128)(2,1)}), bf16[16,16,1024]{2,1,0:T(8,128)(2,1)}, u32[]{:S(2)}, u32[]{:S(2)}) async-start(bf16[16,16,1024]{2,1,0:T(8,128)(2,1)} %bitcast.76), calls=%async_computation.3 | async-start | bytes 1048576 | tf_op jit(solution)/shard_map/all_to_all | solution.py:399
  89.3 6.1 %collective-permute-start.12 = (bf16[128,1024]{1,0:T(8,128)(2,1)}, bf16[128,1024]{1,0:T(8,128)(2,1)S(1)}, u32[]{:S(2)}, u32[]{:S(2)}) collective-permute-start(bf16[128,1024]{1,0:T(8,128)(2,1)} %get-tuple-element.18), channel_id=1, source_target_pairs={{0,2},{1,3},{2,4},{3,5},{4,6},{5,7},{6,0},{7,1},{8,10},{9,11},{10,... | collective-permute-start | bytes 786440 | tf_op jit(solution)/shard_map/ppermute | solution.py:37
  90.6 8.5 %collective-permute-start.13 = (bf16[128,1024]{1,0:T(8,128)(2,1)}, bf16[128,1024]{1,0:T(8,128)(2,1)}, u32[]{:S(2)}, u32[]{:S(2)}) collective-permute-start(bf16[128,1024]{1,0:T(8,128)(2,1)} %get-tuple-element.19), channel_id=1, source_target_pairs={{0,6},{1,7},{2,0},{3,1},{4,2},{5,3},{6,4},{7,5},{8,14},{9,15},{10,... | collective-permute-start | bytes 786440 | tf_op jit(solution)/shard_map/ppermute | solution.py:37
  95.4 26.0 %collective-permute-start.17 = (bf16[256,1024]{1,0:T(8,128)(2,1)}, bf16[256,1024]{1,0:T(8,128)(2,1)}, u32[]{:S(2)}, u32[]{:S(2)}) collective-permute-start(bf16[256,1024]{1,0:T(8,128)(2,1)} %bitcast.21.refs_6_), channel_id=1, source_target_pairs={{0,2},{1,3},{2,4},{3,5},{4,6},{5,7},{6,0},{7,1},{8,10},{9,11},{10,... | collective-permute-start | bytes 1572872 | tf_op jit(solution)/shard_map/ppermute | solution.py:37
  99.1 5.3 %copy-start.19 = (f32[128]{0:T(128)}, f32[128]{0:T(128)S(1)}, u32[]{:S(2)}) copy-start(f32[128]{0:T(128)S(1)} %fusion.10) | copy-start | bytes 1540
  99.1 25.3 %collective-permute-start.18 = (bf16[256,1024]{1,0:T(8,128)(2,1)}, bf16[256,1024]{1,0:T(8,128)(2,1)}, u32[]{:S(2)}, u32[]{:S(2)}) collective-permute-start(bf16[256,1024]{1,0:T(8,128)(2,1)} %bitcast.21.refs_6_), channel_id=1, source_target_pairs={{0,6},{1,7},{2,0},{3,1},{4,2},{5,3},{6,4},{7,5},{8,14},{9,15},{10,... | collective-permute-start | bytes 1572872 | tf_op jit(solution)/shard_map/ppermute | solution.py:37
  101.7 19.5 %collective-permute-start.5 = (f32[128,16]{0,1:T(8,128)S(1)}, f32[128,16]{0,1:T(8,128)S(1)}, u32[]{:S(2)}, u32[]{:S(2)}) collective-permute-start(f32[128,16]{0,1:T(8,128)S(1)} %maximum_maximum_fusion.1), channel_id=1, source_target_pairs={{0,2},{1,3},{2,0},{3,1},{4,6},{5,7},{6,4},{7,5},{8,10},{9,11},{10,... | collective-permute-start | bytes 24584 | tf_op jit(solution)/shard_map/ppermute | solution.py:416
  104.4 20.2 %collective-permute-start.19 = (bf16[256,1024]{1,0:T(8,128)(2,1)}, bf16[256,1024]{1,0:T(8,128)(2,1)}, u32[]{:S(2)}, u32[]{:S(2)}) collective-permute-start(bf16[256,1024]{1,0:T(8,128)(2,1)} %bitcast.21.refs_6_), channel_id=1, source_target_pairs={{0,4},{1,5},{2,6},{3,7},{4,0},{5,1},{6,2},{7,3},{8,12},{9,13},{10,... | collective-permute-start | bytes 1572872 | tf_op jit(solution)/shard_map/ppermute | solution.py:37
  105.8 18.6 %copy-start.20 = (f32[128]{0:T(128)S(1)}, f32[128]{0:T(128)}, u32[]{:S(2)}) copy-start(f32[128]{0:T(128)} %copy-done.19) | copy-start | bytes 1540
  105.8 18.6 %copy-start.21 = (f32[16]{0:T(128)S(1)}, f32[16]{0:T(128)}, u32[]{:S(2)}) copy-start(f32[16]{0:T(128)} %pad.4.clone) | copy-start | bytes 196
  105.8 18.7 %copy-start.23 = (s32[15]{0:T(128)S(1)}, s32[15]{0:T(128)}, u32[]{:S(2)}) copy-start(s32[15]{0:T(128)} %param.18) | copy-start | bytes 184
  119.9 26.3 %collective-permute-start.14 = (bf16[256,1024]{1,0:T(8,128)(2,1)S(1)}, bf16[256,1024]{1,0:T(8,128)(2,1)S(1)}, u32[]{:S(2)}, u32[]{:S(2)}) collective-permute-start(bf16[256,1024]{1,0:T(8,128)(2,1)S(1)} %get-tuple-element.21), channel_id=1, source_target_pairs={{0,2},{1,3},{2,4},{3,5},{4,6},{5,7},{6,0},{7,1},{8,10},{9,11},{10,... | collective-permute-start | bytes 1572872 | tf_op jit(solution)/shard_map/ppermute | solution.py:37
  121.2 25.0 %collective-permute-start.15 = (bf16[256,1024]{1,0:T(8,128)(2,1)S(1)}, bf16[256,1024]{1,0:T(8,128)(2,1)S(1)}, u32[]{:S(2)}, u32[]{:S(2)}) collective-permute-start(bf16[256,1024]{1,0:T(8,128)(2,1)S(1)} %get-tuple-element.22), channel_id=1, source_target_pairs={{0,6},{1,7},{2,0},{3,1},{4,2},{5,3},{6,4},{7,5},{8,14},{9,15},{10,... | collective-permute-start | bytes 1572872 | tf_op jit(solution)/shard_map/ppermute | solution.py:37
  121.4 24.9 %collective-permute-start.16 = (bf16[256,1024]{1,0:T(8,128)(2,1)S(1)}, bf16[256,1024]{1,0:T(8,128)(2,1)S(1)}, u32[]{:S(2)}, u32[]{:S(2)}) collective-permute-start(bf16[256,1024]{1,0:T(8,128)(2,1)S(1)} %get-tuple-element.23), channel_id=1, source_target_pairs={{0,4},{1,5},{2,6},{3,7},{4,0},{5,1},{6,2},{7,3},{8,12},{9,13},{10,... | collective-permute-start | bytes 1572872 | tf_op jit(solution)/shard_map/ppermute | solution.py:37
  124.4 21.4 %collective-permute-start.6 = (f32[128,16]{0,1:T(8,128)S(1)}, f32[128,16]{0,1:T(8,128)S(1)}, u32[]{:S(2)}, u32[]{:S(2)}) collective-permute-start(f32[128,16]{0,1:T(8,128)S(1)} %fusion.105), channel_id=1, source_target_pairs={{0,4},{1,5},{2,6},{3,7},{4,0},{5,1},{6,2},{7,3},{8,12},{9,13},{10,... | collective-permute-start | bytes 24584 | tf_op jit(solution)/shard_map/ppermute | solution.py:417
  124.5 21.3 %copy-start.12 = (s32[2048]{0:T(1024)S(1)}, s32[2048]{0:T(1024)}, u32[]{:S(2)}) copy-start(s32[2048]{0:T(1024)} %copy-done.11) | copy-start | bytes 24580
  138.5 9.0 %copy-start.4 = (bf16[256,1024]{1,0:T(8,128)(2,1)}, bf16[256,1024]{1,0:T(8,128)(2,1)S(1)}, u32[]{:S(2)}) copy-start(bf16[256,1024]{1,0:T(8,128)(2,1)S(1)} %get-tuple-element.24.rest_ref) | copy-start | bytes 1572868
  138.5 9.0 %copy-start.6 = (bf16[256,1024]{1,0:T(8,128)(2,1)}, bf16[256,1024]{1,0:T(8,128)(2,1)S(1)}, u32[]{:S(2)}) copy-start(bf16[256,1024]{1,0:T(8,128)(2,1)S(1)} %get-tuple-element.27.relay_ref) | copy-start | bytes 1572868
  138.6 15.5 %collective-permute-start.20 = (bf16[256,1024]{1,0:T(8,128)(2,1)}, bf16[256,1024]{1,0:T(8,128)(2,1)}, u32[]{:S(2)}, u32[]{:S(2)}) collective-permute-start(bf16[256,1024]{1,0:T(8,128)(2,1)} %get-tuple-element.25), channel_id=1, source_target_pairs={{0,2},{1,3},{2,4},{3,5},{4,6},{5,7},{6,0},{7,1},{8,10},{9,11},{10,... | collective-permute-start | bytes 1572872 | tf_op jit(solution)/shard_map/ppermute | solution.py:37
  145.9 11.2 %collective-permute-start.21 = (bf16[256,1024]{1,0:T(8,128)(2,1)}, bf16[256,1024]{1,0:T(8,128)(2,1)}, u32[]{:S(2)}, u32[]{:S(2)}) collective-permute-start(bf16[256,1024]{1,0:T(8,128)(2,1)} %get-tuple-element.26), channel_id=1, source_target_pairs={{0,6},{1,7},{2,0},{3,1},{4,2},{5,3},{6,4},{7,5},{8,14},{9,15},{10,... | collective-permute-start | bytes 1572872 | tf_op jit(solution)/shard_map/ppermute | solution.py:37
  146.2 14.4 %copy-start.14 = (s32[128,2]{0,1:T(2,128)S(1)}, s32[128,2]{0,1:T(2,128)}, u32[]{:S(2)}) copy-start(s32[128,2]{0,1:T(2,128)} %param.17) | copy-start | bytes 3076
  148.4 20.4 %all-to-all-start.2 = ((bf16[16,16,1024]{2,1,0:T(8,128)(2,1)}), bf16[16,16,1024]{2,1,0:T(8,128)(2,1)}, u32[]{:S(2)}, u32[]{:S(2)}) async-start(bf16[16,16,1024]{2,1,0:T(8,128)(2,1)} %bitcast.73), calls=%async_computation.2 | async-start | bytes 1048576 | tf_op jit(solution)/shard_map/all_to_all | solution.py:399
  159.1 14.5 %copy-start.16 = (s32[16]{0:T(128)S(1)}, s32[16]{0:T(128)}, u32[]{:S(2)}) copy-start(s32[16]{0:T(128)} %copy-done.15) | copy-start | bytes 196
  159.1 5.7 %collective-permute-start.22 = (bf16[128,1024]{1,0:T(8,128)(2,1)}, bf16[128,1024]{1,0:T(8,128)(2,1)}, u32[]{:S(2)}, u32[]{:S(2)}) collective-permute-start(bf16[128,1024]{1,0:T(8,128)(2,1)} %get-tuple-element.28), channel_id=1, source_target_pairs={{0,2},{1,3},{2,4},{3,5},{4,6},{5,7},{6,0},{7,1},{8,10},{9,11},{10,... | collective-permute-start | bytes 786440 | tf_op jit(solution)/shard_map/ppermute | solution.py:37
  159.7 6.7 %collective-permute-start.23 = (bf16[128,1024]{1,0:T(8,128)(2,1)S(1)}, bf16[128,1024]{1,0:T(8,128)(2,1)}, u32[]{:S(2)}, u32[]{:S(2)}) collective-permute-start(bf16[128,1024]{1,0:T(8,128)(2,1)S(1)} %get-tuple-element.29), channel_id=1, source_target_pairs={{0,6},{1,7},{2,0},{3,1},{4,2},{5,3},{6,4},{7,5},{8,14},{9,15},{10,... | collective-permute-start | bytes 786440 | tf_op jit(solution)/shard_map/ppermute | solution.py:37
  166.3 16.3 %copy-start.18 = (s32[16]{0:T(128)S(1)}, s32[16]{0:T(128)}, u32[]{:S(2)}) copy-start(s32[16]{0:T(128)} %copy-done.17) | copy-start | bytes 196
  168.8 13.8 %all-to-all-start.4 = ((bf16[16,16,1024]{2,1,0:T(8,128)(2,1)}), bf16[16,16,1024]{2,1,0:T(8,128)(2,1)}, u32[]{:S(2)}, u32[]{:S(2)}) async-start(bf16[16,16,1024]{2,1,0:T(8,128)(2,1)} %bitcast.74), calls=%async_computation.4 | async-start | bytes 1048576 | tf_op jit(solution)/shard_map/all_to_all | solution.py:399
  182.6 2.8 %copy-start.7 = (f32[128,1024]{1,0:T(8,128)S(1)}, f32[128,1024]{1,0:T(8,128)}, u32[]{:S(2)}) copy-start(f32[128,1024]{1,0:T(8,128)} %convolution_bitcast_fusion.2) | copy-start | bytes 1572868
  185.4 13.5 %copy-start.9 = (bf16[128,512]{1,0:T(8,128)(2,1)S(1)}, bf16[128,512]{1,0:T(8,128)(2,1)}, u32[]{:S(2)}) copy-start(bf16[128,512]{1,0:T(8,128)(2,1)} %copy-done.8) | copy-start | bytes 393220
  186.9 12.0 %collective-permute-start.24 = (bf16[128,512]{1,0:T(8,128)(2,1)S(1)}, bf16[128,512]{1,0:T(8,128)(2,1)S(1)}, u32[]{:S(2)}, u32[]{:S(2)}) collective-permute-start(bf16[128,512]{1,0:T(8,128)(2,1)S(1)} %select_convert_fusion), channel_id=1, source_target_pairs={{0,1},{1,0},{2,3},{3,2},{4,5},{5,4},{6,7},{7,6},{8,9},{9,8},{10,11... | collective-permute-start | bytes 393224 | tf_op jit(solution)/shard_map/ppermute | solution.py:41
  (5 other events, 3.6 us)
